TPU v7x, 128 devices: a whole 4x4x4 slice. The times are simulated.
128 devices in a mesh: ctx: 16 (over y, z_lo, core), dp: 8 (over z_hi, x).
Axes of the slice: x: 4, y: 4, z: 4 (z_hi: 2, z_lo: 2; z = z_hi * 2 + z_lo), core: 2. Of those that a mesh axis runs over, the one named last changes fastest.
Arguments:
- query_rows: bfloat16 [8, 2048, 1024], P('dp', 'ctx'), may hold values from -6 to 6
- key_rows: bfloat16 [8, 2048, 1024], P('dp', 'ctx'), may hold values from -6 to 6
- value_rows: bfloat16 [8, 2048, 1024], P('dp', 'ctx'), may hold values from -6 to 6
- block_lists: int32 [8, 16, 4], P('dp'), may hold values from 0 to 15, as said below
- block_lengths: int32 [8, 16], P('dp'), may hold values from 2 to 128, as said below
- out_weight: bfloat16 [1024, 2048], replicated, may hold values from -0.125 to 0.125
- expert_input: bfloat16 [8, 2048, 2048], P('dp', 'ctx'), may hold values from -6 to 6
- layer_grad: bfloat16 [8, 2048, 2048], P('dp', 'ctx'), may hold values from -1.5 to 1.5
- route_experts: int32 [8, 2048, 6], P('dp', 'ctx'), may hold values from 0 to 15, all different within a row; in each aligned block of 128 rows (0 to 127, 128 to 255, ..., all dimensions but the last counted through in order) at most 64 rows name the same one
- route_weight: float32 [8, 2048, 6], P('dp', 'ctx'), may hold values from 0.02 to 0.4
- gate_weight: bfloat16 [16, 2048, 704], P('ctx'), may hold values from -0.125 to 0.125
- up_weight: bfloat16 [16, 2048, 704], P('ctx'), may hold values from -0.125 to 0.125
- down_weight: bfloat16 [16, 2048, 704], P('ctx'), may hold values from -0.21875 to 0.21875
Outputs:
- query_grad: bfloat16 [8, 2048, 1024], P('dp', 'ctx')
- key_grad: bfloat16 [8, 2048, 1024], P('dp', 'ctx')
- value_grad: bfloat16 [8, 2048, 1024], P('dp', 'ctx')
- gate_grad: float32 [16, 2048, 704], P('ctx', 'dp')
- up_grad: float32 [16, 2048, 704], P('ctx', 'dp')
- down_grad: float32 [16, 2048, 704], P('ctx', 'dp')
Inputs may be any that keep to these rules, and one draw needn't show every extreme that they name: `block_lists`: entry 0 of row i of a sequence's lists is i; every entry of row i lies in 0 to i. `block_lengths`: every sequence has a block of full length 128. `route_experts`: each token names 6 different experts. Among the 128 tokens of one device, no expert is named by more than 64 tokens.
All inputs are finite; a program needn't handle non-finite values.
Results may differ from a plain program's by a relative error of at most 0.012.
The roundings to bfloat16 on the way count: a program that leaves them out, or rounds other values in their place, can miss the bound.
Values may be sent and summed in bfloat16 or wider, within the bound.
No kernel may reach another device: no remote copies, remote signals or barrier semaphores. Data moves between devices by JAX's collectives and lax.ppermute only.
A program may use at most 192 MiB of HBM per device.

v0:
```python
import math

import jax
import jax.numpy as jnp
from jax import lax
from jax.experimental import pallas as pl
from jax.experimental.pallas import tpu as pltpu
from jax.sharding import PartitionSpec as P


HEADS = 8
HD = 128
TOPK = 6
BLK = 128
NSEL = 4
HALF = BLK // 2
TOGETHER = 2


def dot_nt(a, b):
    return lax.dot_general(a, b, (((1,), (1,)), ((), ())), preferred_element_type=jnp.float32)


def dot_nn(a, b):
    return lax.dot_general(a, b, (((1,), (0,)), ((), ())), preferred_element_type=jnp.float32)


def dot_tn(a, b):
    return lax.dot_general(a, b, (((0,), (0,)), ((), ())), preferred_element_type=jnp.float32)


def pack_kernel(q_ref, k_ref, v_ref, g_ref, w_ref, out_ref):
    out_grad = dot_nt(g_ref[...], w_ref[...]).astype(jnp.bfloat16)
    for head in range(2):
        cols = slice(head * HD, (head + 1) * HD)
        for half in range(2):
            rows, place = slice(half * HALF, (half + 1) * HALF), 2 * head + half
            out_ref[place, 0:BLK, :] = k_ref[:, cols]
            out_ref[place, BLK : 2 * BLK, :] = v_ref[:, cols]
            out_ref[place, 2 * BLK : 2 * BLK + HALF, :] = q_ref[rows, cols]
            out_ref[place, 2 * BLK + HALF :, :] = out_grad[rows, cols]


def pack_rows(queries, keys, values, grads, out_weight):
    width = out_weight.shape[1]
    col = pl.BlockSpec((BLK, 2 * HD), lambda h: (0, h))
    return pl.pallas_call(
        pack_kernel,
        grid=(HEADS // 2,),
        in_specs=[
            col,
            col,
            col,
            pl.BlockSpec((BLK, width), lambda h: (0, 0)),
            pl.BlockSpec((2 * HD, width), lambda h: (h, 0)),
        ],
        out_specs=pl.BlockSpec((4, 3 * BLK, HD), lambda h: (h, 0, 0)),
        out_shape=jax.ShapeDtypeStruct((2 * HEADS, 3 * BLK, HD), jnp.bfloat16),
        cost_estimate=pl.CostEstimate(
            flops=2 * BLK * HEADS * HD * width, bytes_accessed=7_000_000, transcendentals=0
        ),
        name="pack_rows",
    )(queries, keys, values, grads, out_weight)


def attention_kernel(lists_ref, lengths_ref, half_ref, rows_ref, out_ref, key_acc, value_acc):
    inv_root = 1.0 / math.sqrt(HD)
    blocks = rows_ref.shape[0]
    key_acc[...] = jnp.zeros_like(key_acc)
    value_acc[...] = jnp.zeros_like(value_acc)
    query_at = lax.broadcasted_iota(jnp.int32, (HALF, BLK), 0) + half_ref[0] * HALF
    key_at = lax.broadcasted_iota(jnp.int32, (HALF, BLK), 1)

    def score(i):
        query = rows_ref[i, 2 * BLK : 2 * BLK + HALF, :]
        listed = [lists_ref[i * NSEL + n] for n in range(NSEL)]
        scores = []
        for n, block in enumerate(listed):
            limit = lengths_ref[block]
            for earlier in listed[:n]:
                limit = jnp.where(earlier == block, 0, limit)
            reach = jnp.where(block < i, BLK, 0)
            allowed = (key_at < limit) & (key_at <= query_at + reach)
            raw = dot_nt(query, rows_ref[block, 0:BLK, :]) * inv_root
            scores.append(jnp.where(allowed, raw, -jnp.inf))
        return listed, scores

    def normalize(scores):
        top = scores[0]
        for part in scores[1:]:
            top = jnp.maximum(top, part)
        row_max = jnp.max(top, axis=1, keepdims=True)
        total = jnp.exp(scores[0] - row_max)
        for part in scores[1:]:
            total = total + jnp.exp(part - row_max)
        log_total = row_max + jnp.log(jnp.sum(total, axis=1, keepdims=True))
        return [jnp.exp(part - log_total) for part in scores]

    def terms(i, listed, probs):
        query = rows_ref[i, 2 * BLK : 2 * BLK + HALF, :]
        grad = rows_ref[i, 2 * BLK + HALF :, :]
        lows = [prob.astype(jnp.bfloat16) for prob in probs]
        head = dot_nn(lows[0], rows_ref[listed[0], BLK : 2 * BLK, :])
        for n in range(1, NSEL):
            head = head + dot_nn(lows[n], rows_ref[listed[n], BLK : 2 * BLK, :])
        prob_grads = [dot_nt(grad, rows_ref[block, BLK : 2 * BLK, :]) for block in listed]
        row_delta = jnp.sum(head * grad.astype(jnp.float32), axis=1, keepdims=True)
        dscores = [
            (prob * (prob_grad - row_delta)).astype(jnp.bfloat16)
            for prob, prob_grad in zip(probs, prob_grads)
        ]
        query_sum = dot_nn(dscores[0], rows_ref[listed[0], 0:BLK, :])
        for n in range(1, NSEL):
            query_sum = query_sum + dot_nn(dscores[n], rows_ref[listed[n], 0:BLK, :])
        key_terms = [dot_tn(dscore, query) for dscore in dscores]
        value_terms = [dot_tn(low, grad) for low in lows]
        return query_sum, key_terms, value_terms

    def some_blocks(group, carry):
        rows = [group * TOGETHER + u for u in range(TOGETHER)]
        scored = [score(i) for i in rows]
        probs = [normalize(scores) for _, scores in scored]
        results = [terms(i, scored[u][0], probs[u]) for u, i in enumerate(rows)]
        for u, i in enumerate(rows):
            query_sum, key_terms, value_terms = results[u]
            out_ref[i, 2 * BLK :, :] = (query_sum * inv_root).astype(jnp.bfloat16)
            for n, block in enumerate(scored[u][0]):
                key_acc[block] += key_terms[n]
                value_acc[block] += value_terms[n]
        return carry

    lax.fori_loop(0, blocks // TOGETHER, some_blocks, 0)
    for i in range(blocks):
        out_ref[i, 0:BLK, :] = (key_acc[i] * inv_root).astype(jnp.bfloat16)
        out_ref[i, BLK : 2 * BLK, :] = value_acc[i].astype(jnp.bfloat16)


def attention_rows(lists, lengths, half, rows):
    blocks = rows.shape[0]
    smem = pl.BlockSpec(memory_space=pltpu.SMEM)
    vmem = pl.BlockSpec(memory_space=pltpu.VMEM)
    return pl.pallas_call(
        attention_kernel,
        in_specs=[smem, smem, smem, vmem],
        out_specs=vmem,
        out_shape=jax.ShapeDtypeStruct((blocks, 2 * BLK + HALF, HD), jnp.bfloat16),
        scratch_shapes=[
            pltpu.VMEM((blocks, BLK, HD), jnp.float32),
            pltpu.VMEM((blocks, BLK, HD), jnp.float32),
        ],
        cost_estimate=pl.CostEstimate(flops=0, bytes_accessed=3_000_000, transcendentals=0),
        name="attention_rows",
    )(lists, lengths, half, rows)


def unpack_kernel(rows_ref, query_ref, key_ref, value_ref):
    for h in range(HEADS):
        cols = slice(h * HD, (h + 1) * HD)

        def both(rows):
            first = rows_ref[2 * h, rows, :].astype(jnp.float32)
            return (first + rows_ref[2 * h + 1, rows, :].astype(jnp.float32)).astype(jnp.bfloat16)

        key_ref[:, cols] = both(slice(0, BLK))
        value_ref[:, cols] = both(slice(BLK, 2 * BLK))
        query_ref[0:HALF, cols] = rows_ref[2 * h, 2 * BLK :, :]
        query_ref[HALF:BLK, cols] = rows_ref[2 * h + 1, 2 * BLK :, :]


def unpack_rows(rows):
    vmem = pl.BlockSpec(memory_space=pltpu.VMEM)
    shape = jax.ShapeDtypeStruct((BLK, HEADS * HD), jnp.bfloat16)
    return pl.pallas_call(
        unpack_kernel,
        in_specs=[vmem],
        out_specs=(vmem, vmem, vmem),
        out_shape=(shape, shape, shape),
        cost_estimate=pl.CostEstimate(flops=0, bytes_accessed=2_000_000, transcendentals=0),
        name="unpack_rows",
    )(rows)


def chip_moves(move):
    def index(y, z, core):
        return (y % 4) * 4 + (z % 2) * 2 + core % 2

    return [
        (index(y, z, core), index(*move(y, z, core)))
        for y in range(4)
        for z in range(2)
        for core in range(2)
    ]


Y_UP = chip_moves(lambda y, z, core: (y + 1, z, core))
Y_DOWN = chip_moves(lambda y, z, core: (y - 1, z, core))
Z_SWAP = chip_moves(lambda y, z, core: (y, z + 1, core))
CORE_SWAP = chip_moves(lambda y, z, core: (y, z, core + 1))
PIECE_STEPS = ((0, 0), (0, 1), (-1, 0), (1, 0), (-1, 1), (1, 1), (-2, 0), (2, 1))
LATE = 2


def sequence_moves(move):
    def index(z, x):
        return (z % 2) * 4 + x % 4

    return [(index(z, x), index(*move(z, x))) for z in range(2) for x in range(4)]


X_UP = sequence_moves(lambda z, x: (z, x + 1))
X_DOWN = sequence_moves(lambda z, x: (z, x - 1))
FAR_SWAP = sequence_moves(lambda z, x: (z + 1, x))


def after(value, *others):
    return lax.optimization_barrier((value, *others))[0]


def pass_on(value, move):
    return lax.ppermute(value, "ctx", move)


def piece_sources(my_index):
    y, z, core = my_index // 4, (my_index // 2) % 2, my_index % 2
    places = []
    for step in range(2):
        for dy, dz in PIECE_STEPS:
            places.append(((y + dy + 4) % 4) * 4 + ((z + dz) % 2) * 2 + (core + step) % 2)
    return jnp.stack(places)


def pick_kernel(count, scaled, *refs):
    onehot_ref, coef_ref = refs[0], refs[1]
    pieces, out_ref = refs[2 : 2 + count], refs[-1]
    slots = onehot_ref.shape[1]
    for p, piece in enumerate(pieces):
        picked = dot_nn(onehot_ref[p], piece[...])
        if scaled:
            picked = picked * coef_ref[p]
        out_ref[p * slots : (p + 1) * slots, :] = picked.astype(jnp.bfloat16)


def pick_rows(onehot, coef, pieces, scaled, buffer, first):
    count, (rows, width), slots = len(pieces), pieces[0].shape, onehot.shape[1]
    tile = 1024 if len(pieces) <= 2 * LATE else 512
    total = 2 * len(PIECE_STEPS) * slots
    in_specs = [
        pl.BlockSpec((count, slots, rows), lambda j: (0, 0, 0)),
        pl.BlockSpec((count, slots, 1), lambda j: (0, 0, 0)),
    ] + [pl.BlockSpec((rows, tile), lambda j: (0, j))] * count
    operands = [onehot, coef, *pieces]
    aliases = {}
    if buffer is not None:
        aliases = {len(operands): 0}
        operands.append(buffer)
        in_specs.append(pl.BlockSpec(memory_space=pl.ANY))
    block = count * slots
    return pl.pallas_call(
        lambda *refs: pick_kernel(count, scaled, *refs),
        grid=(width // tile,),
        in_specs=in_specs,
        out_specs=pl.BlockSpec((block, tile), lambda j: (first // block, j)),
        out_shape=jax.ShapeDtypeStruct((total, width), jnp.bfloat16),
        input_output_aliases=aliases,
        cost_estimate=pl.CostEstimate(
            flops=2 * block * rows * width,
            bytes_accessed=2 * count * (rows + slots) * width,
            transcendentals=0,
        ),
        name="pick_rows",
    )(*operands)


def route_slots(coef_rows, capacity):
    present = coef_rows > 0.0
    rank = jnp.cumsum(present.astype(jnp.int32), axis=1) - 1
    slot_ids = jnp.arange(capacity, dtype=jnp.int32)
    chosen = present[:, None, :] & (rank[:, None, :] == slot_ids[None, :, None])
    slot_coef = jnp.sum(jnp.where(chosen, coef_rows[:, None, :], 0.0), axis=2, keepdims=True)
    return chosen.astype(jnp.bfloat16), slot_coef


def term_kernel(per_step, homes, order_ref, delta_ref, *refs):
    rows, out_refs = refs[:per_step], refs[per_step:]
    step = pl.program_id(0)
    values = [dot_nn(delta_ref[...], row[...]).astype(jnp.bfloat16) for row in rows]
    for t in range(len(homes) // per_step):

        @pl.when(step == t)
        def _(t=t):
            for u, value in enumerate(values):
                array, place = homes[t * per_step + u]
                out_refs[array][place] = value


def weight_terms(order, delta, rows, stacks):
    count, per_step = order.shape[0], 4
    hidden, slots = delta.shape
    tile = rows.shape[1] // count
    homes = [(a, p) for a, depth in enumerate(stacks) for p in range(depth)]
    return pl.pallas_call(
        lambda *refs: term_kernel(per_step, homes, *refs),
        grid_spec=pltpu.PrefetchScalarGridSpec(
            num_scalar_prefetch=1,
            grid=(count // per_step,),
            in_specs=[pl.BlockSpec((hidden, slots), lambda j, order_ref: (0, 0))]
            + [
                pl.BlockSpec(
                    (slots, tile), lambda j, order_ref, u=u: (0, order_ref[j * per_step + u])
                )
                for u in range(per_step)
            ],
            out_specs=[
                pl.BlockSpec((depth, hidden, tile), lambda j, order_ref: (0, 0, 0))
                for depth in stacks
            ],
        ),
        out_shape=[jax.ShapeDtypeStruct((depth, hidden, tile), jnp.bfloat16) for depth in stacks],
        cost_estimate=pl.CostEstimate(flops=0, bytes_accessed=1_000_000, transcendentals=0),
        name="weight_terms",
    )(order, delta, *([rows] * per_step))


def term_order(steps):
    place = lax.axis_index("dp")
    z, x = place // 4, place % 4
    return jnp.stack([((z + dz) % 2) * 4 + (x + dx) % 4 for dx, dz in steps]).astype(jnp.int32)


RING_FIRST = ((2, 0), (1, 1), (2, 1), (3, 0), (1, 0), (3, 1), (0, 1), (0, 0))
ACROSS_FIRST = ((2, 1), (1, 1), (3, 1), (0, 1), (2, 0), (1, 0), (3, 0), (0, 0))


def add_terms(*terms):
    total = terms[0].astype(jnp.float32)
    for term in terms[1:]:
        total = total + term.astype(jnp.float32)
    return total


def sum_ring_first(upward, downward, rest):
    from_below = lax.ppermute(upward, "dp", X_UP)
    from_above = lax.ppermute(downward, "dp", X_DOWN)
    send_up = add_terms(rest[0], from_below[0]).astype(jnp.bfloat16)
    send_down = add_terms(rest[1], from_above[0]).astype(jnp.bfloat16)
    up_same = lax.ppermute(send_up, "dp", X_UP)
    down_other = lax.ppermute(send_down, "dp", X_DOWN)
    across = add_terms(rest[2], from_below[1], down_other).astype(jnp.bfloat16)
    arrived = lax.ppermute(across, "dp", FAR_SWAP)
    return add_terms(rest[3], up_same, from_above[1], arrived).T[None]


def sum_across_first(other, same):
    arrived = lax.ppermute(other, "dp", FAR_SWAP)
    cut = same.shape[1] // 2

    def kept(place, rows):
        return add_terms(same[place, rows], arrived[place, rows])

    head, tail = slice(0, cut), slice(cut, None)
    up_far = lax.ppermute(kept(0, head).astype(jnp.bfloat16), "dp", X_UP)
    down_far = lax.ppermute(kept(0, tail).astype(jnp.bfloat16), "dp", X_DOWN)
    next_sum = jnp.concatenate([kept(1, head) + up_far.astype(jnp.float32), kept(1, tail)])
    back_sum = jnp.concatenate([kept(2, head), kept(2, tail) + down_far.astype(jnp.float32)])
    from_below = lax.ppermute(next_sum.astype(jnp.bfloat16), "dp", X_UP)
    from_above = lax.ppermute(back_sum.astype(jnp.bfloat16), "dp", X_DOWN)
    return add_terms(kept(3, slice(None)), from_below, from_above).T[None]


def per_device(
    query_rows,
    key_rows,
    value_rows,
    block_lists,
    block_lengths,
    out_weight,
    expert_input,
    layer_grad,
    route_experts,
    route_weight,
    gate_weight,
    up_weight,
    down_weight,
):
    ctx_count = lax.axis_size("ctx")
    my_index = lax.axis_index("ctx")
    tokens_here = expert_input[0]
    grads_here = layer_grad[0]
    capacity = min(BLK, BLK * TOPK * 4 // (3 * ctx_count))

    all_experts = jnp.arange(ctx_count, dtype=jnp.int32)
    matches = route_experts[0][None, :, :] == all_experts[:, None, None]
    coef_out = jnp.sum(jnp.where(matches, route_weight[0][None], 0.0), axis=2)
    coef_in = lax.all_to_all(coef_out, "ctx", split_axis=0, concat_axis=0, tiled=True)
    onehot, slot_coef = route_slots(coef_in[piece_sources(my_index)], capacity)
    keep = len(PIECE_STEPS) - LATE
    halves = (slice(0, keep), slice(keep + LATE, 2 * keep + LATE))
    tails = (slice(keep, keep + LATE), slice(2 * keep + LATE, None))
    onehot, slot_coef = (
        jnp.concatenate([v[part] for part in halves + tails]) for v in (onehot, slot_coef)
    )

    early = 2 * keep

    def early_pick(mine, others, scaled, *gates):
        slots = after(onehot[:early], *gates)
        return pick_rows(slots, slot_coef[:early], mine + others, scaled, None, 0)

    def late_pick(mine, others, scaled, buffer, *gates):
        slots = after(onehot[early:], *gates)
        first = early * capacity
        return pick_rows(slots, slot_coef[early:], mine + others, scaled, buffer, first)

    beside, below, above = (pass_on(tokens_here, move) for move in (Z_SWAP, Y_UP, Y_DOWN))
    below_beside, above_beside = pass_on(beside, Y_UP), pass_on(beside, Y_DOWN)
    far, far_beside = pass_on(below, Y_UP), pass_on(above_beside, Y_DOWN)
    near_rows = [tokens_here, beside, below, above, below_beside, above_beside]
    near_others = [pass_on(piece, CORE_SWAP) for piece in near_rows]
    far_rows = [far, far_beside]
    far_others = [pass_on(piece, CORE_SWAP) for piece in far_rows]

    packed = pack_rows(
        query_rows[0], key_rows[0], value_rows[0], after(grads_here, beside, below), out_weight
    )

    grads_out = after(grads_here, below_beside, above_beside)
    g_beside, g_below, g_above = (pass_on(grads_out, move) for move in (Z_SWAP, Y_UP, Y_DOWN))
    buffer = early_pick(near_rows, near_others, False, packed)
    beside_out, below_out = after(g_beside, buffer), after(g_below, buffer)
    g_below_beside, g_above_beside = pass_on(beside_out, Y_UP), pass_on(beside_out, Y_DOWN)
    g_far = pass_on(below_out, Y_UP)
    rows_in = late_pick(far_rows, far_others, False, buffer)
    gate_pre = dot_nn(rows_in, gate_weight[0])
    g_far_beside = pass_on(after(g_above_beside, gate_pre), Y_DOWN)
    up_pre = dot_nn(rows_in, up_weight[0])
    gate_sig = jax.nn.sigmoid(gate_pre)
    gate_act = gate_pre * gate_sig
    hidden = (gate_act * up_pre).astype(jnp.bfloat16)
    g_near = [grads_here, g_beside, g_below, g_above, g_below_beside, g_above_beside]
    g_near_others = [pass_on(piece, CORE_SWAP) for piece in g_near]
    g_buffer = early_pick(g_near, g_near_others, True)
    g_fars = [g_far, g_far_beside]
    g_far_others = [pass_on(piece, CORE_SWAP) for piece in g_fars]
    grads_in = late_pick(g_fars, g_far_others, True, g_buffer)

    ring_order, across_order = term_order(RING_FIRST), term_order(ACROSS_FIRST)
    down_terms = weight_terms(ring_order, hidden.T, grads_in, (2, 2, 4))
    down_grad = sum_ring_first(*down_terms)
    hidden_grad = dot_nn(after(grads_in, down_terms[0]), down_weight[0])
    gate_delta = (hidden_grad * up_pre * gate_sig * (1.0 + gate_pre * (1.0 - gate_sig))).astype(
        jnp.bfloat16
    )
    up_delta = (hidden_grad * gate_act).astype(jnp.bfloat16)
    packed = after(packed, gate_delta)
    head_rows = lax.all_to_all(packed, "ctx", split_axis=0, concat_axis=0, tiled=True)
    up_terms = weight_terms(across_order, up_delta.T, rows_in, (4, 4))
    up_grad = sum_across_first(*up_terms)
    gate_terms = weight_terms(ring_order, after(gate_delta, up_terms[0]).T, rows_in, (2, 2, 4))
    gate_grad = sum_ring_first(*gate_terms)

    half = (my_index % 2).astype(jnp.int32).reshape(1)
    head_rows = after(head_rows, gate_terms[0])
    grad_rows = attention_rows(
        block_lists.reshape(-1), block_lengths.reshape(-1), half, head_rows
    )
    returned = lax.all_to_all(grad_rows, "ctx", split_axis=0, concat_axis=0, tiled=True)
    query_grad, key_grad, value_grad = unpack_rows(returned)
    return (query_grad[None], key_grad[None], value_grad[None], gate_grad, up_grad, down_grad)


def solution(mesh):
    in_specs = (
        P("dp", "ctx", None),
        P("dp", "ctx", None),
        P("dp", "ctx", None),
        P("dp", None, None),
        P("dp", None),
        P(),
        P("dp", "ctx", None),
        P("dp", "ctx", None),
        P("dp", "ctx", None),
        P("dp", "ctx", None),
        P("ctx", None, None),
        P("ctx", None, None),
        P("ctx", None, None),
    )
    out_specs = (
        P("dp", "ctx", None),
        P("dp", "ctx", None),
        P("dp", "ctx", None),
        P("ctx", "dp", None),
        P("ctx", "dp", None),
        P("ctx", "dp", None),
    )
    return jax.shard_map(
        per_device, mesh=mesh, in_specs=in_specs, out_specs=out_specs, check_vma=False
    )
```

profile of v0, /device:TPU:2, one launch (start us, length us, event | category | flops | bytes accessed | tf_op | source)
XLA Modules:
  0.0 263.0 jit_solution(9832849652437211677)
XLA Ops:
  11.7 7.1 %all-to-all-done = f32[16,1,128]{2,1,0:T(1,128)S(1)} async-done(((f32[16,1,128]{2,1,0:T(1,128)}), f32[16,1,128]{2,1,0:T(1,128)S(1)}, u32[]{:S(2)}, u32[]{:S(2)}) %all-to-all-start) | async-done | bytes 8224 | tf_op jit(solution)/shard_map/all_to_all | solution.py:394
  25.2 8.7 %collective-permute-done.3.refs_7_ = bf16[128,2048]{1,0:T(8,128)(2,1)} collective-permute-done((bf16[128,2048]{1,0:T(8,128)(2,1)}, bf16[128,2048]{1,0:T(8,128)(2,1)}, u32[]{:S(2)}, u32[]{:S(2)}) %collective-permute-start.3) | collective-permute-done | bytes 524320 | tf_op jit(solution)/shard_map/ppermute | solution.py:220
  33.9 4.2 %collective-permute-done.2.refs_6_ = bf16[128,2048]{1,0:T(8,128)(2,1)} collective-permute-done((bf16[128,2048]{1,0:T(8,128)(2,1)}, bf16[128,2048]{1,0:T(8,128)(2,1)}, u32[]{:S(2)}, u32[]{:S(2)}) %collective-permute-start.2) | collective-permute-done | bytes 524320 | tf_op jit(solution)/shard_map/ppermute | solution.py:220
  41.5 6.7 %collective-permute-done.15.refs_2_ = bf16[128,2048]{1,0:T(8,128)(2,1)} collective-permute-done((bf16[128,2048]{1,0:T(8,128)(2,1)}, bf16[128,2048]{1,0:T(8,128)(2,1)}, u32[]{:S(2)}, u32[]{:S(2)}) %collective-permute-start.15) | collective-permute-done | bytes 524320 | tf_op jit(solution)/shard_map/ppermute | solution.py:220
  48.3 4.5 %collective-permute-done.16.refs_3_ = bf16[128,2048]{1,0:T(8,128)(2,1)} collective-permute-done((bf16[128,2048]{1,0:T(8,128)(2,1)}, bf16[128,2048]{1,0:T(8,128)(2,1)}, u32[]{:S(2)}, u32[]{:S(2)}) %collective-permute-start.16) | collective-permute-done | bytes 524320 | tf_op jit(solution)/shard_map/ppermute | solution.py:220
  54.3 5.4 %pack_rows.1 = bf16[16,384,128]{2,1,0:T(8,128)(2,1)} custom-call(bf16[128,1024]{1,0:T(8,128)(2,1)} %bitcast.173, bf16[128,1024]{1,0:T(8,128)(2,1)} %bitcast.174, bf16[128,1024]{1,0:T(8,128)(2,1)} %bitcast.175, bf16[128,2048]{1,0:T(8,128)(2,1)} %bitcast.162, bf16[1024,2048]{1,0:T(8,128)(2,1)} %w_ref.1), custom_call_target="tpu_custom_call" | custom-call | flops 536870912 | bytes 7000000 | tf_op jit(solution)/shard_map/pack_rows/pallas_call | solution.py:47
  60.4 6.1 %pick_rows.4.refs_6_ = bf16[1024,2048]{1,0:T(8,128)(2,1)} custom-call(bf16[12,64,128]{2,1,0:T(8,128)(2,1)} %pad_maximum_fusion.3.refs_0_, f32[12,64,1]{2,1,0:T(8,128)} %pad_maximum_fusion.refs_1_, bf16[128,2048]{1,0:T(8,128)(2,1)} %bitcast.172, bf16[128,2048]{1,0:T(8,128)(2,1)} %collective-permute-done.refs_3_, bf16[128,2048]{1,0:T(8,128)(2,1)} %copy-done.7, ...), custom_call_target="tpu_custom_call" | custom-call | flops 402653184 | bytes 9437184 | tf_op jit(solution)/shard_map/pick_rows/pallas_call | solution.py:258
  74.1 7.9 %fusion.9 = f32[1024,704]{0,1:T(8,128)} fusion(bf16[1024,2048]{1,0:T(8,128)(2,1)} %pick_rows.5.refs_2_.refs_3_.refs_4_.refs_5_, bf16[1,2048,704]{1,2,0:T(8,128)(2,1)} %param.23), kind=kOutput, calls=%fused_computation.14 | convolution fusion | flops 2952790016 | bytes 9961472 | tf_op jit(solution)/shard_map/dot_general | solution.py:25
  82.0 9.8 %collective-permute-done.14.refs_7_ = bf16[128,2048]{1,0:T(8,128)(2,1)} collective-permute-done((bf16[128,2048]{1,0:T(8,128)(2,1)}, bf16[128,2048]{1,0:T(8,128)(2,1)}, u32[]{:S(2)}, u32[]{:S(2)}) %collective-permute-start.14) | collective-permute-done | bytes 524320 | tf_op jit(solution)/shard_map/ppermute | solution.py:220
  96.9 10.8 %collective-permute-done.12.refs_2_ = bf16[128,2048]{1,0:T(8,128)(2,1)} collective-permute-done((bf16[128,2048]{1,0:T(8,128)(2,1)}, bf16[128,2048]{1,0:T(8,128)(2,1)}, u32[]{:S(2)}, u32[]{:S(2)}) %collective-permute-start.12) | collective-permute-done | bytes 524320 | tf_op jit(solution)/shard_map/ppermute | solution.py:220
  108.2 7.5 %fusion.3 = (bf16[704,1024]{1,0:T(8,128)(2,1)}, f32[1024,704]{0,1:T(8,128)}) fusion(f32[1024,704]{0,1:T(8,128)} %fusion.9, bf16[1024,2048]{1,0:T(8,128)(2,1)} %pick_rows.5.refs_2_.refs_3_.refs_4_.refs_5_, bf16[1,2048,704]{1,2,0:T(8,128)(2,1)S(1)} %copy-done), kind=kOutput, calls=%fused_computation.6 | convolution fusion | flops 2957115392 | bytes 14286848 | tf_op jit(solution)/shard_map/dot_general | solution.py:25
  117.3 6.1 %pick_rows.6.refs_6_ = bf16[1024,2048]{1,0:T(8,128)(2,1)} custom-call(bf16[12,64,128]{2,1,0:T(8,128)(2,1)} %pad_maximum_fusion.3.refs_0_, f32[12,64,1]{2,1,0:T(8,128)} %pad_maximum_fusion.refs_1_, bf16[128,2048]{1,0:T(8,128)(2,1)} %bitcast.163, bf16[128,2048]{1,0:T(8,128)(2,1)} %collective-permute-done.13.refs_3_, ...), custom_call_target="tpu_custom_call" | custom-call | flops 402653184 | bytes 9437184 | tf_op jit(solution)/shard_map/pick_rows/pallas_call | solution.py:258
  126.3 8.3 %weight_terms.3 = (bf16[2,704,256]{2,1,0:T(8,128)(2,1)}, bf16[2,704,256]{2,1,0:T(8,128)(2,1)}, bf16[4,704,256]{2,1,0:T(8,128)(2,1)}) custom-call(s32[8]{0:T(128)} %stack.114.refs_0_, bf16[704,1024]{1,0:T(8,128)(2,1)} %get-tuple-element.68.refs_1_, bf16[1024,2048]{1,0:T(8,128)(2,1)} %pick_rows.7.refs_2_.refs_3_.refs_4_.refs_5_, ...), custom_call_target="tpu_custom_call" | custom-call | bytes 1000000 | tf_op jit(solution)/shard_map/weight_terms/pallas_call | solution.py:301
  136.6 8.9 %multiply_convert_fusion = (bf16[1024,704]{0,1:T(8,128)(2,1)}, f32[1024,704]{0,1:T(8,128)S(1)}) fusion(f32[1024,704]{0,1:T(8,128)S(1)} %copy-done.3, f32[1024,704]{0,1:T(8,128)} %get-tuple-element.69, bf16[1024,2048]{1,0:T(8,128)(2,1)} %pick_rows.7.refs_2_.refs_3_.refs_4_.refs_5_, bf16[1,2048,704]{1,2,0:T(8,128)(2,1)} %param.25), kind=kOutput, calls=%fused_computation.16 | convolution fusion | flops 2959998976 | bytes 17170432 | tf_op jit(solution)/shard_map/dot_general | solution.py:25
  147.6 8.3 %weight_terms.4 = (bf16[4,704,256]{2,1,0:T(8,128)(2,1)}, bf16[4,704,256]{2,1,0:T(8,128)(2,1)}) custom-call(s32[8]{0:T(128)} %stack.115.refs_0_, bf16[704,1024]{1,0:T(8,128)(2,1)} %fusion.refs_1_, bf16[1024,2048]{1,0:T(8,128)(2,1)} %pick_rows.5.refs_2_.refs_3_.refs_4_.refs_5_, bf16[1024,2048]{1,0:T(8,128)(2,1)} %pick_rows.5.refs_2_.refs_3_.refs_4_.refs_5_, ...), custom_call_target="tpu_custom_call" | custom-call | bytes 1000000 | tf_op jit(solution)/shard_map/weight_terms/pallas_call | solution.py:301
  155.9 3.6 %collective-permute-start.35 = (bf16[4,704,256]{2,1,0:T(8,128)(2,1)}, bf16[4,704,256]{2,1,0:T(8,128)(2,1)}, u32[]{:S(2)}, u32[]{:S(2)}) collective-permute-start(bf16[4,704,256]{2,1,0:T(8,128)(2,1)} %get-tuple-element.36), channel_id=1, source_target_pairs={{0,4},{1,5},{2,6},{3,7},{4,0},{5,1},{6,2},{7,3},{8,12},{9,13},{10,... | collective-permute-start | bytes 4325384 | tf_op jit(solution)/shard_map/ppermute | solution.py:354
  159.5 8.3 %weight_terms.5 = (bf16[2,704,256]{2,1,0:T(8,128)(2,1)}, bf16[2,704,256]{2,1,0:T(8,128)(2,1)}, bf16[4,704,256]{2,1,0:T(8,128)(2,1)}) custom-call(s32[8]{0:T(128)} %stack.114.refs_0_, bf16[704,1024]{1,0:T(8,128)(2,1)} %bitcast.166, bf16[1024,2048]{1,0:T(8,128)(2,1)} %pick_rows.5.refs_2_.refs_3_.refs_4_.refs_5_, ...), custom_call_target="tpu_custom_call" | custom-call | bytes 1000000 | tf_op jit(solution)/shard_map/weight_terms/pallas_call | solution.py:301
  169.8 4.1 %all-to-all-start.1 = ((bf16[16,384,128]{2,1,0:T(8,128)(2,1)}), bf16[16,384,128]{2,1,0:T(8,128)(2,1)S(1)}, u32[]{:S(2)}, u32[]{:S(2)}) async-start(bf16[16,384,128]{2,1,0:T(8,128)(2,1)} %pack_rows.1), calls=%async_computation.1 | async-start | bytes 3145728 | tf_op jit(solution)/shard_map/all_to_all | solution.py:455
  179.9 7.2 %collective-permute-done.30 = bf16[2,704,256]{2,1,0:T(8,128)(2,1)} collective-permute-done((bf16[2,704,256]{2,1,0:T(8,128)(2,1)}, bf16[2,704,256]{2,1,0:T(8,128)(2,1)}, u32[]{:S(2)}, u32[]{:S(2)}) %collective-permute-start.30) | collective-permute-done | bytes 720928 | tf_op jit(solution)/shard_map/ppermute | solution.py:342
  198.1 6.7 %collective-permute-done.35 = bf16[4,704,256]{2,1,0:T(8,128)(2,1)} collective-permute-done((bf16[4,704,256]{2,1,0:T(8,128)(2,1)}, bf16[4,704,256]{2,1,0:T(8,128)(2,1)}, u32[]{:S(2)}, u32[]{:S(2)}) %collective-permute-start.35) | collective-permute-done | bytes 1441824 | tf_op jit(solution)/shard_map/ppermute | solution.py:354
  211.7 13.2 %attention_rows.1 = bf16[16,320,128]{2,1,0:T(8,128)(2,1)} custom-call(s32[64]{0:T(128)} %reshape.713.lists_ref, s32[16]{0:T(128)} %bitcast.178, s32[1]{0:T(128)} %bitcast.1.half_ref, bf16[16,384,128]{2,1,0:T(8,128)(2,1)} %copy-done.2), custom_call_target="tpu_custom_call" | custom-call | bytes 3000000 | tf_op jit(solution)/shard_map/attention_rows/pallas_call | solution.py:142
  225.0 4.7 %all-to-all-start.2 = ((bf16[16,320,128]{2,1,0:T(8,128)(2,1)}), bf16[16,320,128]{2,1,0:T(8,128)(2,1)}, u32[]{:S(2)}, u32[]{:S(2)}) async-start(bf16[16,320,128]{2,1,0:T(8,128)(2,1)} %attention_rows.1), calls=%async_computation.2 | async-start | bytes 2621440 | tf_op jit(solution)/shard_map/all_to_all | solution.py:466
  229.7 3.7 %collective-permute-start.34 = (bf16[704,256]{1,0:T(8,128)(2,1)}, bf16[704,256]{1,0:T(8,128)(2,1)S(1)}, u32[]{:S(2)}, u32[]{:S(2)}) collective-permute-start(bf16[704,256]{1,0:T(8,128)(2,1)} %fusion.18), channel_id=1, source_target_pairs={{0,4},{1,5},{2,6},{3,7},{4,0},{5,1},{6,2},{7,3},{8,12},{9,13},{10,... | collective-permute-start | bytes 1081352 | tf_op jit(solution)/shard_map/ppermute | solution.py:349
  240.2 16.3 %collective-permute-done.34 = bf16[704,256]{1,0:T(8,128)(2,1)S(1)} collective-permute-done((bf16[704,256]{1,0:T(8,128)(2,1)}, bf16[704,256]{1,0:T(8,128)(2,1)S(1)}, u32[]{:S(2)}, u32[]{:S(2)}) %collective-permute-start.34) | collective-permute-done | bytes 360480 | tf_op jit(solution)/shard_map/ppermute | solution.py:349
  (152 shorter events, 83.8 us)
Async XLA Ops:
  24.1 24.1 %collective-permute-start.15 = (bf16[128,2048]{1,0:T(8,128)(2,1)}, bf16[128,2048]{1,0:T(8,128)(2,1)}, u32[]{:S(2)}, u32[]{:S(2)}) collective-permute-start(bf16[128,2048]{1,0:T(8,128)(2,1)} %copy-done.7), channel_id=1, source_target_pairs={{0,32},{8,40},{16,48},{24,56},{32,64},{40,72},{48,80},{56,88},{64,... | collective-permute-start | bytes 1572872 | tf_op jit(solution)/shard_map/ppermute | solution.py:220
  38.3 21.5 %collective-permute-start.10 = (bf16[128,2048]{1,0:T(8,128)(2,1)}, bf16[128,2048]{1,0:T(8,128)(2,1)}, u32[]{:S(2)}, u32[]{:S(2)}) collective-permute-start(bf16[128,2048]{1,0:T(8,128)(2,1)} %collective-permute-done.2.refs_6_), channel_id=1, source_target_pairs={{0,8},{8,0},{16,24},{24,16},{32,40},{40,32},{48,56},{56,48},{64,72... | collective-permute-start | bytes 1572872 | tf_op jit(solution)/shard_map/ppermute | solution.py:220
  40.2 26.3 %collective-permute-start.13 = (bf16[128,2048]{1,0:T(8,128)(2,1)}, bf16[128,2048]{1,0:T(8,128)(2,1)}, u32[]{:S(2)}, u32[]{:S(2)}) collective-permute-start(bf16[128,2048]{1,0:T(8,128)(2,1)} %bitcast.160), channel_id=1, source_target_pairs={{0,16},{8,24},{16,0},{24,8},{32,48},{40,56},{48,32},{56,40},{64,80... | collective-permute-start | bytes 1572872 | tf_op jit(solution)/shard_map/ppermute | solution.py:220
  48.3 20.4 %collective-permute-start.17 = (bf16[128,2048]{1,0:T(8,128)(2,1)}, bf16[128,2048]{1,0:T(8,128)(2,1)}, u32[]{:S(2)}, u32[]{:S(2)}) collective-permute-start(bf16[128,2048]{1,0:T(8,128)(2,1)} %collective-permute-done.15.refs_2_), channel_id=1, source_target_pairs={{0,8},{8,0},{16,24},{24,16},{32,40},{40,32},{48,56},{56,48},{64,72... | collective-permute-start | bytes 1572872 | tf_op jit(solution)/shard_map/ppermute | solution.py:220
  59.8 32.0 %collective-permute-start.24 = (bf16[128,2048]{1,0:T(8,128)(2,1)S(1)}, bf16[128,2048]{1,0:T(8,128)(2,1)}, u32[]{:S(2)}, u32[]{:S(2)}) collective-permute-start(bf16[128,2048]{1,0:T(8,128)(2,1)S(1)} %bitcast.164), channel_id=1, source_target_pairs={{0,8},{8,0},{16,24},{24,16},{32,40},{40,32},{48,56},{56,48},{64,72... | collective-permute-start | bytes 1572872 | tf_op jit(solution)/shard_map/ppermute | solution.py:220
  66.5 25.3 %collective-permute-start.22 = (bf16[128,2048]{1,0:T(8,128)(2,1)S(1)}, bf16[128,2048]{1,0:T(8,128)(2,1)}, u32[]{:S(2)}, u32[]{:S(2)}) collective-permute-start(bf16[128,2048]{1,0:T(8,128)(2,1)S(1)} %bitcast.165), channel_id=1, source_target_pairs={{0,96},{8,104},{16,112},{24,120},{32,0},{40,8},{48,16},{56,24},{64... | collective-permute-start | bytes 1572872 | tf_op jit(solution)/shard_map/ppermute | solution.py:220
  68.1 28.2 %collective-permute-start.23 = (bf16[128,2048]{1,0:T(8,128)(2,1)}, bf16[128,2048]{1,0:T(8,128)(2,1)}, u32[]{:S(2)}, u32[]{:S(2)}) collective-permute-start(bf16[128,2048]{1,0:T(8,128)(2,1)} %collective-permute-done.13.refs_3_), channel_id=1, source_target_pairs={{0,32},{8,40},{16,48},{24,56},{32,64},{40,72},{48,80},{56,88},{64,... | collective-permute-start | bytes 1572872 | tf_op jit(solution)/shard_map/ppermute | solution.py:220
  68.6 23.2 %collective-permute-start.14 = (bf16[128,2048]{1,0:T(8,128)(2,1)}, bf16[128,2048]{1,0:T(8,128)(2,1)}, u32[]{:S(2)}, u32[]{:S(2)}) collective-permute-start(bf16[128,2048]{1,0:T(8,128)(2,1)} %collective-permute-done.13.refs_3_), channel_id=1, source_target_pairs={{0,96},{8,104},{16,112},{24,120},{32,0},{40,8},{48,16},{56,24},{64... | collective-permute-start | bytes 1572872 | tf_op jit(solution)/shard_map/ppermute | solution.py:220
  71.3 25.0 %collective-permute-start.25 = (bf16[128,2048]{1,0:T(8,128)(2,1)}, bf16[128,2048]{1,0:T(8,128)(2,1)}, u32[]{:S(2)}, u32[]{:S(2)}) collective-permute-start(bf16[128,2048]{1,0:T(8,128)(2,1)} %collective-permute-done.13.refs_3_), channel_id=1, source_target_pairs={{0,8},{8,0},{16,24},{24,16},{32,40},{40,32},{48,56},{56,48},{64,72... | collective-permute-start | bytes 1572872 | tf_op jit(solution)/shard_map/ppermute | solution.py:220
  96.3 21.0 %collective-permute-start.29 = (bf16[128,2048]{1,0:T(8,128)(2,1)}, bf16[128,2048]{1,0:T(8,128)(2,1)}, u32[]{:S(2)}, u32[]{:S(2)}) collective-permute-start(bf16[128,2048]{1,0:T(8,128)(2,1)} %collective-permute-done.14.refs_7_), channel_id=1, source_target_pairs={{0,8},{8,0},{16,24},{24,16},{32,40},{40,32},{48,56},{56,48},{64,72... | collective-permute-start | bytes 1572872 | tf_op jit(solution)/shard_map/ppermute | solution.py:220
  134.6 39.3 %collective-permute-start.40 = (bf16[2,704,256]{2,1,0:T(8,128)(2,1)}, bf16[2,704,256]{2,1,0:T(8,128)(2,1)}, u32[]{:S(2)}, u32[]{:S(2)}) collective-permute-start(bf16[2,704,256]{2,1,0:T(8,128)(2,1)} %get-tuple-element.33), channel_id=1, source_target_pairs={{0,1},{1,2},{2,3},{3,0},{4,5},{5,6},{6,7},{7,4},{8,9},{9,10},{10,1... | collective-permute-start | bytes 2162696 | tf_op jit(solution)/shard_map/ppermute | solution.py:342
  136.1 37.8 %collective-permute-start.42 = (bf16[2,704,256]{2,1,0:T(8,128)(2,1)}, bf16[2,704,256]{2,1,0:T(8,128)(2,1)}, u32[]{:S(2)}, u32[]{:S(2)}) collective-permute-start(bf16[2,704,256]{2,1,0:T(8,128)(2,1)} %get-tuple-element.47), channel_id=1, source_target_pairs={{0,3},{1,0},{2,1},{3,2},{4,7},{5,4},{6,5},{7,6},{8,11},{9,8},{10,9... | collective-permute-start | bytes 2162696 | tf_op jit(solution)/shard_map/ppermute | solution.py:343
  155.9 49.0 %collective-permute-start.35 = (bf16[4,704,256]{2,1,0:T(8,128)(2,1)}, bf16[4,704,256]{2,1,0:T(8,128)(2,1)}, u32[]{:S(2)}, u32[]{:S(2)}) collective-permute-start(bf16[4,704,256]{2,1,0:T(8,128)(2,1)} %get-tuple-element.36), channel_id=1, source_target_pairs={{0,4},{1,5},{2,6},{3,7},{4,0},{5,1},{6,2},{7,3},{8,12},{9,13},{10,... | collective-permute-start | bytes 4325384 | tf_op jit(solution)/shard_map/ppermute | solution.py:354
  169.8 40.8 %all-to-all-start.1 = ((bf16[16,384,128]{2,1,0:T(8,128)(2,1)}), bf16[16,384,128]{2,1,0:T(8,128)(2,1)S(1)}, u32[]{:S(2)}, u32[]{:S(2)}) async-start(bf16[16,384,128]{2,1,0:T(8,128)(2,1)} %pack_rows.1), calls=%async_computation.1 | async-start | bytes 3145728 | tf_op jit(solution)/shard_map/all_to_all | solution.py:455
  176.2 19.9 %collective-permute-start.43 = (bf16[704,256]{1,0:T(8,128)(2,1)}, bf16[704,256]{1,0:T(8,128)(2,1)S(1)}, u32[]{:S(2)}, u32[]{:S(2)}) collective-permute-start(bf16[704,256]{1,0:T(8,128)(2,1)} %get-tuple-element.57), channel_id=1, source_target_pairs={{0,3},{1,0},{2,1},{3,2},{4,7},{5,4},{6,5},{7,6},{8,11},{9,8},{10,9... | collective-permute-start | bytes 1081352 | tf_op jit(solution)/shard_map/ppermute | solution.py:347
  179.9 56.4 %collective-permute-start.41 = (bf16[704,256]{1,0:T(8,128)(2,1)}, bf16[704,256]{1,0:T(8,128)(2,1)S(1)}, u32[]{:S(2)}, u32[]{:S(2)}) collective-permute-start(bf16[704,256]{1,0:T(8,128)(2,1)} %get-tuple-element.56), channel_id=1, source_target_pairs={{0,1},{1,2},{2,3},{3,0},{4,5},{5,6},{6,7},{7,4},{8,9},{9,10},{10,1... | collective-permute-start | bytes 1081352 | tf_op jit(solution)/shard_map/ppermute | solution.py:346
  192.4 47.8 %collective-permute-start.31 = (bf16[704,256]{1,0:T(8,128)(2,1)}, bf16[704,256]{1,0:T(8,128)(2,1)}, u32[]{:S(2)}, u32[]{:S(2)}) collective-permute-start(bf16[704,256]{1,0:T(8,128)(2,1)} %get-tuple-element.58), channel_id=1, source_target_pairs={{0,1},{1,2},{2,3},{3,0},{4,5},{5,6},{6,7},{7,4},{8,9},{9,10},{10,1... | collective-permute-start | bytes 1081352 | tf_op jit(solution)/shard_map/ppermute | solution.py:346
  198.1 39.7 %collective-permute-start.44 = (bf16[704,256]{1,0:T(8,128)(2,1)}, bf16[704,256]{1,0:T(8,128)(2,1)}, u32[]{:S(2)}, u32[]{:S(2)}) collective-permute-start(bf16[704,256]{1,0:T(8,128)(2,1)} %fusion.15), channel_id=1, source_target_pairs={{0,4},{1,5},{2,6},{3,7},{4,0},{5,1},{6,2},{7,3},{8,12},{9,13},{10,... | collective-permute-start | bytes 1081352 | tf_op jit(solution)/shard_map/ppermute | solution.py:349
  206.4 23.2 %collective-permute-start.36 = (bf16[352,256]{1,0:T(8,128)(2,1)S(1)}, bf16[352,256]{1,0:T(8,128)(2,1)S(1)}, u32[]{:S(2)}, u32[]{:S(2)}) collective-permute-start(bf16[352,256]{1,0:T(8,128)(2,1)S(1)} %get-tuple-element.52), channel_id=1, source_target_pairs={{0,1},{1,2},{2,3},{3,0},{4,5},{5,6},{6,7},{7,4},{8,9},{9,10},{10,1... | collective-permute-start | bytes 540680 | tf_op jit(solution)/shard_map/ppermute | solution.py:361
  208.0 25.3 %collective-permute-start.38 = (bf16[352,256]{1,0:T(8,128)(2,1)S(1)}, bf16[352,256]{1,0:T(8,128)(2,1)S(1)}, u32[]{:S(2)}, u32[]{:S(2)}) collective-permute-start(bf16[352,256]{1,0:T(8,128)(2,1)S(1)} %get-tuple-element.53), channel_id=1, source_target_pairs={{0,3},{1,0},{2,1},{3,2},{4,7},{5,4},{6,5},{7,6},{8,11},{9,8},{10,9... | collective-permute-start | bytes 540680 | tf_op jit(solution)/shard_map/ppermute | solution.py:362
  225.0 35.7 %all-to-all-start.2 = ((bf16[16,320,128]{2,1,0:T(8,128)(2,1)}), bf16[16,320,128]{2,1,0:T(8,128)(2,1)}, u32[]{:S(2)}, u32[]{:S(2)}) async-start(bf16[16,320,128]{2,1,0:T(8,128)(2,1)} %attention_rows.1), calls=%async_computation.2 | async-start | bytes 2621440 | tf_op jit(solution)/shard_map/all_to_all | solution.py:466
  229.7 26.7 %collective-permute-start.34 = (bf16[704,256]{1,0:T(8,128)(2,1)}, bf16[704,256]{1,0:T(8,128)(2,1)S(1)}, u32[]{:S(2)}, u32[]{:S(2)}) collective-permute-start(bf16[704,256]{1,0:T(8,128)(2,1)} %fusion.18), channel_id=1, source_target_pairs={{0,4},{1,5},{2,6},{3,7},{4,0},{5,1},{6,2},{7,3},{8,12},{9,13},{10,... | collective-permute-start | bytes 1081352 | tf_op jit(solution)/shard_map/ppermute | solution.py:349
  234.7 23.8 %collective-permute-start.37 = (bf16[704,256]{1,0:T(8,128)(2,1)S(1)}, bf16[704,256]{1,0:T(8,128)(2,1)S(1)}, u32[]{:S(2)}, u32[]{:S(2)}) collective-permute-start(bf16[704,256]{1,0:T(8,128)(2,1)S(1)} %pad_maximum_fusion.1), channel_id=1, source_target_pairs={{0,1},{1,2},{2,3},{3,0},{4,5},{5,6},{6,7},{7,4},{8,9},{9,10},{10,1... | collective-permute-start | bytes 1081352 | tf_op jit(solution)/shard_map/ppermute | solution.py:365
  236.3 22.3 %collective-permute-start.39 = (bf16[704,256]{1,0:T(8,128)(2,1)S(1)}, bf16[704,256]{1,0:T(8,128)(2,1)S(1)}, u32[]{:S(2)}, u32[]{:S(2)}) collective-permute-start(bf16[704,256]{1,0:T(8,128)(2,1)S(1)} %pad_maximum_fusion.2), channel_id=1, source_target_pairs={{0,3},{1,0},{2,1},{3,2},{4,7},{5,4},{6,5},{7,6},{8,11},{9,8},{10,9... | collective-permute-start | bytes 1081352 | tf_op jit(solution)/shard_map/ppermute | solution.py:366
  (38 other events, 597.9 us)
where the time goes:
time: 267 us; the launch traced here: 263 us
  waiting for transfers between devices  86.7 us (32%)
  Pallas kernels  63.8 us (24%)
  starting transfers between devices  54.5 us (20%)
  matrix products  24.2 us (9%)
  other arithmetic  23.7 us (9%)
  local copies, waits for them, and re-layouts  8.94 us (3%)
    ppermute x30, waiting for transfers between devices, pass_on(): return lax.ppermute(value, 'ctx', move)  44.7 us
    pallas_call x3, Pallas kernels, weight_terms(): pl.pallas_call(lambda *refs: term_kernel(per_step, homes, *refs), grid_sp...  24.9 us
    dot_general x3, matrix products, dot_nn(): lax.dot_general(a, b, (((1,), (0,)), ((), ())), preferred_element_type=jn...  24.2 us
    ppermute x30, starting transfers between devices, pass_on(): return lax.ppermute(value, 'ctx', move)  20.7 us
    pallas_call x4, Pallas kernels, pick_rows(): pl.pallas_call(lambda *refs: pick_kernel(count, scaled, *refs), grid=(wid...  17.9 us
    ppermute x2, waiting for transfers between devices, sum_ring_first(): arrived = lax.ppermute(across, 'dp', FAR_SWAP)  16.3 us
    pallas_call x1, Pallas kernels, attention_rows(): pl.pallas_call(attention_kernel, in_specs=[smem, smem, smem, vmem], out_s...  13.2 us
    ppermute x2, waiting for transfers between devices, sum_ring_first(): from_below = lax.ppermute(upward, 'dp', X_UP)  7.16 us
  transfers between devices with their start and end apart: 48, of which 12 were waited for; matrix products, arithmetic and copies ran while one was open for 20% of the time, Pallas kernels for 19%

commit v1 on v0

--- a/solution.py
+++ b/solution.py
@@ -210,10 +210,6 @@
 X_UP = sequence_moves(lambda z, x: (z, x + 1))
 X_DOWN = sequence_moves(lambda z, x: (z, x - 1))
 FAR_SWAP = sequence_moves(lambda z, x: (z + 1, x))
-
-
-def after(value, *others):
-    return lax.optimization_barrier((value, *others))[0]
 
 
 def pass_on(value, move):
@@ -358,8 +354,10 @@
         return add_terms(same[place, rows], arrived[place, rows])
 
     head, tail = slice(0, cut), slice(cut, None)
-    up_far = lax.ppermute(kept(0, head).astype(jnp.bfloat16), "dp", X_UP)
-    down_far = lax.ppermute(kept(0, tail).astype(jnp.bfloat16), "dp", X_DOWN)
+    far_head = kept(0, head).astype(jnp.bfloat16)
+    far_tail = kept(0, tail).astype(jnp.bfloat16)
+    up_far = lax.ppermute(far_head, "dp", X_UP)
+    down_far = lax.ppermute(far_tail, "dp", X_DOWN)
     next_sum = jnp.concatenate([kept(1, head) + up_far.astype(jnp.float32), kept(1, tail)])
     back_sum = jnp.concatenate([kept(2, head), kept(2, tail) + down_far.astype(jnp.float32)])
     from_below = lax.ppermute(next_sum.astype(jnp.bfloat16), "dp", X_UP)
@@ -392,50 +390,45 @@
     matches = route_experts[0][None, :, :] == all_experts[:, None, None]
     coef_out = jnp.sum(jnp.where(matches, route_weight[0][None], 0.0), axis=2)
     coef_in = lax.all_to_all(coef_out, "ctx", split_axis=0, concat_axis=0, tiled=True)
-    onehot, slot_coef = route_slots(coef_in[piece_sources(my_index)], capacity)
     keep = len(PIECE_STEPS) - LATE
+    early = 2 * keep
     halves = (slice(0, keep), slice(keep + LATE, 2 * keep + LATE))
     tails = (slice(keep, keep + LATE), slice(2 * keep + LATE, None))
+    onehot, slot_coef = route_slots(coef_in[piece_sources(my_index)], capacity)
     onehot, slot_coef = (
         jnp.concatenate([v[part] for part in halves + tails]) for v in (onehot, slot_coef)
     )
 
-    early = 2 * keep
-
-    def early_pick(mine, others, scaled, *gates):
-        slots = after(onehot[:early], *gates)
-        return pick_rows(slots, slot_coef[:early], mine + others, scaled, None, 0)
-
-    def late_pick(mine, others, scaled, buffer, *gates):
-        slots = after(onehot[early:], *gates)
+    def early_pick(mine, others, scaled):
+        return pick_rows(onehot[:early], slot_coef[:early], mine + others, scaled, None, 0)
+
+    def late_pick(mine, others, scaled, buffer):
         first = early * capacity
-        return pick_rows(slots, slot_coef[early:], mine + others, scaled, buffer, first)
+        return pick_rows(onehot[early:], slot_coef[early:], mine + others, scaled, buffer, first)
 
     beside, below, above = (pass_on(tokens_here, move) for move in (Z_SWAP, Y_UP, Y_DOWN))
-    below_beside, above_beside = pass_on(beside, Y_UP), pass_on(beside, Y_DOWN)
+    below_beside = pass_on(beside, Y_UP)
+    above_beside = pass_on(beside, Y_DOWN)
     far, far_beside = pass_on(below, Y_UP), pass_on(above_beside, Y_DOWN)
     near_rows = [tokens_here, beside, below, above, below_beside, above_beside]
     near_others = [pass_on(piece, CORE_SWAP) for piece in near_rows]
     far_rows = [far, far_beside]
     far_others = [pass_on(piece, CORE_SWAP) for piece in far_rows]
 
-    packed = pack_rows(
-        query_rows[0], key_rows[0], value_rows[0], after(grads_here, beside, below), out_weight
-    )
-
-    grads_out = after(grads_here, below_beside, above_beside)
-    g_beside, g_below, g_above = (pass_on(grads_out, move) for move in (Z_SWAP, Y_UP, Y_DOWN))
-    buffer = early_pick(near_rows, near_others, False, packed)
-    beside_out, below_out = after(g_beside, buffer), after(g_below, buffer)
-    g_below_beside, g_above_beside = pass_on(beside_out, Y_UP), pass_on(beside_out, Y_DOWN)
-    g_far = pass_on(below_out, Y_UP)
+    packed = pack_rows(query_rows[0], key_rows[0], value_rows[0], grads_here, out_weight)
+
+    g_beside, g_below, g_above = (pass_on(grads_here, move) for move in (Z_SWAP, Y_UP, Y_DOWN))
+    g_below_beside, g_above_beside = pass_on(g_beside, Y_UP), pass_on(g_beside, Y_DOWN)
+    g_far = pass_on(g_below, Y_UP)
+    g_far_beside = pass_on(g_above_beside, Y_DOWN)
+    buffer = early_pick(near_rows, near_others, False)
     rows_in = late_pick(far_rows, far_others, False, buffer)
-    gate_pre = dot_nn(rows_in, gate_weight[0])
-    g_far_beside = pass_on(after(g_above_beside, gate_pre), Y_DOWN)
-    up_pre = dot_nn(rows_in, up_weight[0])
+    gate_pre = lax.optimization_barrier(dot_nn(rows_in, gate_weight[0]))
     gate_sig = jax.nn.sigmoid(gate_pre)
     gate_act = gate_pre * gate_sig
+    up_pre = dot_nn(rows_in, up_weight[0])
     hidden = (gate_act * up_pre).astype(jnp.bfloat16)
+    up_pre, hidden = lax.optimization_barrier((up_pre, hidden))
     g_near = [grads_here, g_beside, g_below, g_above, g_below_beside, g_above_beside]
     g_near_others = [pass_on(piece, CORE_SWAP) for piece in g_near]
     g_buffer = early_pick(g_near, g_near_others, True)
@@ -446,23 +439,19 @@
     ring_order, across_order = term_order(RING_FIRST), term_order(ACROSS_FIRST)
     down_terms = weight_terms(ring_order, hidden.T, grads_in, (2, 2, 4))
     down_grad = sum_ring_first(*down_terms)
-    hidden_grad = dot_nn(after(grads_in, down_terms[0]), down_weight[0])
-    gate_delta = (hidden_grad * up_pre * gate_sig * (1.0 + gate_pre * (1.0 - gate_sig))).astype(
-        jnp.bfloat16
-    )
+    head_rows = lax.all_to_all(packed, "ctx", split_axis=0, concat_axis=0, tiled=True)
+    later_grads = lax.optimization_barrier((grads_in, down_terms[0]))[0]
+    hidden_grad = dot_nn(later_grads, down_weight[0])
+    gate_delta = (
+        hidden_grad * up_pre * gate_sig * (1.0 + gate_pre * (1.0 - gate_sig))
+    ).astype(jnp.bfloat16)
     up_delta = (hidden_grad * gate_act).astype(jnp.bfloat16)
-    packed = after(packed, gate_delta)
-    head_rows = lax.all_to_all(packed, "ctx", split_axis=0, concat_axis=0, tiled=True)
-    up_terms = weight_terms(across_order, up_delta.T, rows_in, (4, 4))
-    up_grad = sum_across_first(*up_terms)
-    gate_terms = weight_terms(ring_order, after(gate_delta, up_terms[0]).T, rows_in, (2, 2, 4))
+    up_grad = sum_across_first(*weight_terms(across_order, up_delta.T, rows_in, (4, 4)))
+    gate_terms = weight_terms(ring_order, gate_delta.T, rows_in, (2, 2, 4))
     gate_grad = sum_ring_first(*gate_terms)
 
     half = (my_index % 2).astype(jnp.int32).reshape(1)
-    head_rows = after(head_rows, gate_terms[0])
-    grad_rows = attention_rows(
-        block_lists.reshape(-1), block_lengths.reshape(-1), half, head_rows
-    )
+    grad_rows = attention_rows(block_lists.reshape(-1), block_lengths.reshape(-1), half, head_rows)
     returned = lax.all_to_all(grad_rows, "ctx", split_axis=0, concat_axis=0, tiled=True)
     query_grad, key_grad, value_grad = unpack_rows(returned)
     return (query_grad[None], key_grad[None], value_grad[None], gate_grad, up_grad, down_grad)

time: 267 us -> 248 us (0.929)
  other arithmetic: 23.7 us -> 16.2 us
  matrix products: 24.2 us -> 19.3 us
  local copies, waits for them, and re-layouts: 8.94 us -> 5.64 us
    ppermute x30, waiting for transfers between devices: 44.7 us -> 62.4 us  [pass_on(): return lax.ppermute(value, 'ctx', move)]
    ppermute x2, waiting for transfers between devices: 16.3 us -> 1.81 us  [sum_ring_first(): arrived = lax.ppermute(across, 'dp', FAR_SWAP)]
    all_to_all x1, waiting for transfers between devices: 7.08 us -> 0.01 us  [per_device(): lax.all_to_all(coef_out, 'ctx', split_axis=0, concat_axis=0, tiled=True)]
    ppermute x1, waiting for transfers between devices: 6.73 us -> 0.01 us  [sum_across_first(): arrived = lax.ppermute(other, 'dp', FAR_SWAP)]
    dot_general x3, matrix products: 24.2 us -> 19.3 us  [dot_nn(): lax.dot_general(a, b, (((1,), (0,)), ((), ())), preferred_element_type=jn...]
    ppermute x2, waiting for transfers between devices: 3.32 us -> 7.03 us  [sum_ring_first(): down_other = lax.ppermute(send_down, 'dp', X_DOWN)]
    convert_element_type x2 -> x1, other arithmetic: 3.67 us -> 0.17 us  [sum_across_first(): far_head = kept(0, head).astype(jnp.bfloat16)]
    unnamed x31 -> x41, local copies, waits for them, and re-layouts: 5.35 us -> 1.94 us
  transfers between devices with their start and end apart: 48 -> 48, of which waited for: 12 -> 16; matrix products, arithmetic and copies ran while one was open for 20% -> 16% of each run, Pallas kernels for 19% -> 26%
where the time goes in v1:
time: 248 us; the launch traced here: 246 us
  waiting for transfers between devices  86.8 us (35%)
  Pallas kernels  63.7 us (26%)
  starting transfers between devices  53.2 us (21%)
  matrix products  19.3 us (8%)
  other arithmetic  16.2 us (7%)
  local copies, waits for them, and re-layouts  5.64 us (2%)
    ppermute x30, waiting for transfers between devices, pass_on(): return lax.ppermute(value, 'ctx', move)  62.4 us
    pallas_call x3, Pallas kernels, weight_terms(): pl.pallas_call(lambda *refs: term_kernel(per_step, homes, *refs), grid_sp...  24.9 us
    ppermute x30, starting transfers between devices, pass_on(): return lax.ppermute(value, 'ctx', move)  20.4 us
    dot_general x3, matrix products, dot_nn(): lax.dot_general(a, b, (((1,), (0,)), ((), ())), preferred_element_type=jn...  19.3 us
    pallas_call x4, Pallas kernels, pick_rows(): pl.pallas_call(lambda *refs: pick_kernel(count, scaled, *refs), grid=(wid...  18 us
    pallas_call x1, Pallas kernels, attention_rows(): pl.pallas_call(attention_kernel, in_specs=[smem, smem, smem, vmem], out_s...  13.2 us
    ppermute x2, waiting for transfers between devices, sum_ring_first(): from_below = lax.ppermute(upward, 'dp', X_UP)  10 us
    ppermute x2, waiting for transfers between devices, sum_ring_first(): down_other = lax.ppermute(send_down, 'dp', X_DOWN)  7.03 us
  transfers between devices with their start and end apart: 48, of which 16 were waited for; matrix products, arithmetic and copies ran while one was open for 16% of the time, Pallas kernels for 26%

profile of v1, /device:TPU:2, one launch (start us, length us, event | category | flops | bytes accessed | tf_op | source)
XLA Modules:
  0.0 246.0 jit_solution(9984919584357110186)
XLA Ops:
  6.0 9.7 %collective-permute-done.2.refs_3_ = bf16[128,2048]{1,0:T(8,128)(2,1)S(1)} collective-permute-done((bf16[128,2048]{1,0:T(8,128)(2,1)}, bf16[128,2048]{1,0:T(8,128)(2,1)S(1)}, u32[]{:S(2)}, u32[]{:S(2)}) %collective-permute-start.2) | collective-permute-done | bytes 524320 | tf_op jit(solution)/shard_map/ppermute | solution.py:216
  21.5 4.3 %all-to-all-start.2 = ((f32[16,1,128]{2,1,0:T(1,128)}), f32[16,1,128]{2,1,0:T(1,128)S(1)}, u32[]{:S(2)}, u32[]{:S(2)}) async-start(f32[16,1,128]{2,1,0:T(1,128)} %bitcast.18), calls=%async_computation.2 | async-start | bytes 16384 | tf_op jit(solution)/shard_map/all_to_all | solution.py:392
  26.1 3.0 %collective-permute-start.3 = (bf16[128,2048]{1,0:T(8,128)(2,1)}, bf16[128,2048]{1,0:T(8,128)(2,1)}, u32[]{:S(2)}, u32[]{:S(2)}) collective-permute-start(bf16[128,2048]{1,0:T(8,128)(2,1)} %copy-done.8), channel_id=1, source_target_pairs={{0,96},{8,104},{16,112},{24,120},{32,0},{40,8},{48,16},{56,24},{64... | collective-permute-start | bytes 1572872 | tf_op jit(solution)/shard_map/ppermute | solution.py:216
  32.4 5.4 %pack_rows.1 = bf16[16,384,128]{2,1,0:T(8,128)(2,1)} custom-call(bf16[128,1024]{1,0:T(8,128)(2,1)} %bitcast.154, bf16[128,1024]{1,0:T(8,128)(2,1)} %bitcast.155, bf16[128,1024]{1,0:T(8,128)(2,1)} %bitcast.156, bf16[128,2048]{1,0:T(8,128)(2,1)} %bitcast.145, bf16[1024,2048]{1,0:T(8,128)(2,1)} %w_ref.1), custom_call_target="tpu_custom_call" | custom-call | flops 536870912 | bytes 7000000 | tf_op jit(solution)/shard_map/pack_rows/pallas_call | solution.py:47
  39.8 4.4 %all-to-all-start = ((bf16[16,384,128]{2,1,0:T(8,128)(2,1)}), bf16[16,384,128]{2,1,0:T(8,128)(2,1)}, u32[]{:S(2)}, u32[]{:S(2)}) async-start(bf16[16,384,128]{2,1,0:T(8,128)(2,1)} %pack_rows.1), calls=%async_computation | async-start | bytes 3145728 | tf_op jit(solution)/shard_map/all_to_all | solution.py:442
  49.8 27.3 %collective-permute-done.1.refs_2_ = bf16[128,2048]{1,0:T(8,128)(2,1)S(1)} collective-permute-done((bf16[128,2048]{1,0:T(8,128)(2,1)}, bf16[128,2048]{1,0:T(8,128)(2,1)S(1)}, u32[]{:S(2)}, u32[]{:S(2)}) %collective-permute-start.1) | collective-permute-done | bytes 524320 | tf_op jit(solution)/shard_map/ppermute | solution.py:216
  77.2 11.2 %collective-permute-done.23.refs_6_ = bf16[128,2048]{1,0:T(8,128)(2,1)} collective-permute-done((bf16[128,2048]{1,0:T(8,128)(2,1)}, bf16[128,2048]{1,0:T(8,128)(2,1)}, u32[]{:S(2)}, u32[]{:S(2)}) %collective-permute-start.23) | collective-permute-done | bytes 524320 | tf_op jit(solution)/shard_map/ppermute | solution.py:216
  91.2 7.8 %collective-permute-done.16.refs_2_ = bf16[128,2048]{1,0:T(8,128)(2,1)S(1)} collective-permute-done((bf16[128,2048]{1,0:T(8,128)(2,1)}, bf16[128,2048]{1,0:T(8,128)(2,1)S(1)}, u32[]{:S(2)}, u32[]{:S(2)}) %collective-permute-start.16) | collective-permute-done | bytes 524320 | tf_op jit(solution)/shard_map/ppermute | solution.py:216
  101.4 3.3 %collective-permute-done.19.refs_3_ = bf16[128,2048]{1,0:T(8,128)(2,1)} collective-permute-done((bf16[128,2048]{1,0:T(8,128)(2,1)}, bf16[128,2048]{1,0:T(8,128)(2,1)}, u32[]{:S(2)}, u32[]{:S(2)}) %collective-permute-start.19) | collective-permute-done | bytes 524320 | tf_op jit(solution)/shard_map/ppermute | solution.py:216
  106.2 13.2 %attention_rows.1 = bf16[16,320,128]{2,1,0:T(8,128)(2,1)} custom-call(s32[64]{0:T(128)} %reshape.713.lists_ref, s32[16]{0:T(128)} %bitcast.159, s32[1]{0:T(128)} %bitcast.1.half_ref, bf16[16,384,128]{2,1,0:T(8,128)(2,1)} %all-to-all-done.rows_ref), custom_call_target="tpu_custom_call" | custom-call | bytes 3000000 | tf_op jit(solution)/shard_map/attention_rows/pallas_call | solution.py:142
  119.4 4.6 %all-to-all-start.1 = ((bf16[16,320,128]{2,1,0:T(8,128)(2,1)}), bf16[16,320,128]{2,1,0:T(8,128)(2,1)}, u32[]{:S(2)}, u32[]{:S(2)}) async-start(bf16[16,320,128]{2,1,0:T(8,128)(2,1)} %attention_rows.1), calls=%async_computation.1 | async-start | bytes 2621440 | tf_op jit(solution)/shard_map/all_to_all | solution.py:455
  124.0 6.2 %pick_rows.4.refs_6_ = bf16[1024,2048]{1,0:T(8,128)(2,1)} custom-call(bf16[12,64,128]{2,1,0:T(8,128)(2,1)} %pad_maximum_fusion.3.refs_0_, f32[12,64,1]{2,1,0:T(8,128)} %pad_maximum_fusion.refs_1_, bf16[128,2048]{1,0:T(8,128)(2,1)} %bitcast.146, bf16[128,2048]{1,0:T(8,128)(2,1)} %copy-done.8, bf16[128,2048]{1,0:T(8,128)(2,1)} %collective-permute-done.refs_4_, ...), custom_call_target="tpu_custom_call" | custom-call | flops 402653184 | bytes 9437184 | tf_op jit(solution)/shard_map/pick_rows/pallas_call | solution.py:254
  130.8 6.1 %pick_rows.6.refs_6_ = bf16[1024,2048]{1,0:T(8,128)(2,1)} custom-call(bf16[12,64,128]{2,1,0:T(8,128)(2,1)} %pad_maximum_fusion.3.refs_0_, f32[12,64,1]{2,1,0:T(8,128)} %pad_maximum_fusion.refs_1_, bf16[128,2048]{1,0:T(8,128)(2,1)} %bitcast.153, bf16[128,2048]{1,0:T(8,128)(2,1)} %collective-permute-done.17.refs_3_, ...), custom_call_target="tpu_custom_call" | custom-call | flops 402653184 | bytes 9437184 | tf_op jit(solution)/shard_map/pick_rows/pallas_call | solution.py:254
  139.8 6.0 %fusion.2 = f32[1024,704]{0,1:T(8,128)S(1)} fusion(bf16[1024,2048]{1,0:T(8,128)(2,1)} %pick_rows.7.refs_2_.refs_3_.refs_4_.refs_5_, bf16[1,2048,704]{1,2,0:T(8,128)(2,1)} %param.23), kind=kOutput, calls=%fused_computation.3 | convolution fusion | flops 2952790016 | bytes 9961472 | tf_op jit(solution)/shard_map/dot_general | solution.py:25
  145.8 4.9 %multiply_convert_fusion.2 = (bf16[1024,704]{0,1:T(8,128)(2,1)}, f32[1024,704]{0,1:T(8,128)}) fusion(f32[1024,704]{0,1:T(8,128)S(1)} %fusion.2, bf16[1024,2048]{1,0:T(8,128)(2,1)S(1)} %copy-done.2, bf16[1,2048,704]{1,2,0:T(8,128)(2,1)S(1)} %copy-done), kind=kOutput, calls=%fused_computation.9 | convolution fusion | flops 2957115392 | bytes 14286848 | tf_op jit(solution)/shard_map/dot_general | solution.py:25
  153.6 8.4 %weight_terms.3 = (bf16[2,704,256]{2,1,0:T(8,128)(2,1)}, bf16[2,704,256]{2,1,0:T(8,128)(2,1)}, bf16[4,704,256]{2,1,0:T(8,128)(2,1)}) custom-call(s32[8]{0:T(128)} %stack.97.refs_0_, bf16[704,1024]{1,0:T(8,128)(2,1)} %bitcast.147, bf16[1024,2048]{1,0:T(8,128)(2,1)} %pick_rows.5.refs_2_.refs_3_.refs_4_.refs_5_, ...), custom_call_target="tpu_custom_call" | custom-call | bytes 1000000 | tf_op jit(solution)/shard_map/weight_terms/pallas_call | solution.py:297
  163.9 8.4 %fusion.7 = (bf16[704,1024]{1,0:T(8,128)(2,1)}, bf16[704,1024]{1,0:T(8,128)(2,1)}) fusion(f32[1024,704]{0,1:T(8,128)} %copy-done.18, f32[1024,704]{0,1:T(8,128)} %get-tuple-element.26, bf16[1024,2048]{1,0:T(8,128)(2,1)} %pick_rows.5.refs_2_.refs_3_.refs_4_.refs_5_, bf16[1,2048,704]{1,2,0:T(8,128)(2,1)S(1)} %copy-done.17), kind=kOutput, calls=%fused_computation.12 | convolution fusion | flops 2962161664 | bytes 15728640 | tf_op jit(solution)/shard_map/dot_general | solution.py:25
  172.3 8.2 %weight_terms.5 = (bf16[4,704,256]{2,1,0:T(8,128)(2,1)}, bf16[4,704,256]{2,1,0:T(8,128)(2,1)}) custom-call(s32[8]{0:T(128)} %stack.115.refs_0_, bf16[704,1024]{1,0:T(8,128)(2,1)} %get-tuple-element.36.refs_1_, bf16[1024,2048]{1,0:T(8,128)(2,1)} %pick_rows.7.refs_2_.refs_3_.refs_4_.refs_5_, bf16[1024,2048]{1,0:T(8,128)(2,1)} %pick_rows.7.refs_2_.refs_3_.refs_4_.refs_5_, ...), custom_call_target="tpu_custom_call" | custom-call | bytes 1000000 | tf_op jit(solution)/shard_map/weight_terms/pallas_call | solution.py:297
  180.5 3.6 %collective-permute-start.35 = (bf16[4,704,256]{2,1,0:T(8,128)(2,1)}, bf16[4,704,256]{2,1,0:T(8,128)(2,1)S(1)}, u32[]{:S(2)}, u32[]{:S(2)}) collective-permute-start(bf16[4,704,256]{2,1,0:T(8,128)(2,1)} %get-tuple-element.31), channel_id=1, source_target_pairs={{0,4},{1,5},{2,6},{3,7},{4,0},{5,1},{6,2},{7,3},{8,12},{9,13},{10,... | collective-permute-start | bytes 4325384 | tf_op jit(solution)/shard_map/ppermute | solution.py:350
  184.1 8.3 %weight_terms.4 = (bf16[2,704,256]{2,1,0:T(8,128)(2,1)}, bf16[2,704,256]{2,1,0:T(8,128)(2,1)}, bf16[4,704,256]{2,1,0:T(8,128)(2,1)}) custom-call(s32[8]{0:T(128)} %stack.97.refs_0_, bf16[704,1024]{1,0:T(8,128)(2,1)} %get-tuple-element.37.refs_1_, bf16[1024,2048]{1,0:T(8,128)(2,1)} %pick_rows.7.refs_2_.refs_3_.refs_4_.refs_5_, ...), custom_call_target="tpu_custom_call" | custom-call | bytes 1000000 | tf_op jit(solution)/shard_map/weight_terms/pallas_call | solution.py:297
  196.5 3.0 %collective-permute-start.43 = (bf16[704,256]{1,0:T(8,128)(2,1)}, bf16[704,256]{1,0:T(8,128)(2,1)}, u32[]{:S(2)}, u32[]{:S(2)}) collective-permute-start(bf16[704,256]{1,0:T(8,128)(2,1)} %get-tuple-element.45), channel_id=1, source_target_pairs={{0,3},{1,0},{2,1},{3,2},{4,7},{5,4},{6,5},{7,6},{8,11},{9,8},{10,9... | collective-permute-start | bytes 1081352 | tf_op jit(solution)/shard_map/ppermute | solution.py:343
  201.7 10.0 %collective-permute-done.30 = bf16[2,704,256]{2,1,0:T(8,128)(2,1)} collective-permute-done((bf16[2,704,256]{2,1,0:T(8,128)(2,1)}, bf16[2,704,256]{2,1,0:T(8,128)(2,1)}, u32[]{:S(2)}, u32[]{:S(2)}) %collective-permute-start.30) | collective-permute-done | bytes 720928 | tf_op jit(solution)/shard_map/ppermute | solution.py:338
  216.9 4.0 %collective-permute-done.43 = bf16[704,256]{1,0:T(8,128)(2,1)} collective-permute-done((bf16[704,256]{1,0:T(8,128)(2,1)}, bf16[704,256]{1,0:T(8,128)(2,1)}, u32[]{:S(2)}, u32[]{:S(2)}) %collective-permute-start.43) | collective-permute-done | bytes 360480 | tf_op jit(solution)/shard_map/ppermute | solution.py:343
  223.9 3.0 %collective-permute-done.33 = bf16[704,256]{1,0:T(8,128)(2,1)S(1)} collective-permute-done((bf16[704,256]{1,0:T(8,128)(2,1)S(1)}, bf16[704,256]{1,0:T(8,128)(2,1)S(1)}, u32[]{:S(2)}, u32[]{:S(2)}) %collective-permute-start.33) | collective-permute-done | bytes 360480 | tf_op jit(solution)/shard_map/ppermute | solution.py:343
  (161 shorter events, 70.5 us)
Async XLA Ops:
  5.9 20.2 %collective-permute-start.9 = (bf16[128,2048]{1,0:T(8,128)(2,1)}, bf16[128,2048]{1,0:T(8,128)(2,1)}, u32[]{:S(2)}, u32[]{:S(2)}) collective-permute-start(bf16[128,2048]{1,0:T(8,128)(2,1)} %bitcast.144), channel_id=1, source_target_pairs={{0,8},{8,0},{16,24},{24,16},{32,40},{40,32},{48,56},{56,48},{64,72... | collective-permute-start | bytes 1572872 | tf_op jit(solution)/shard_map/ppermute | solution.py:216
  5.9 23.3 %collective-permute-start.17 = (bf16[128,2048]{1,0:T(8,128)(2,1)}, bf16[128,2048]{1,0:T(8,128)(2,1)}, u32[]{:S(2)}, u32[]{:S(2)}) collective-permute-start(bf16[128,2048]{1,0:T(8,128)(2,1)} %bitcast.149), channel_id=1, source_target_pairs={{0,16},{8,24},{16,0},{24,8},{32,48},{40,56},{48,32},{56,40},{64,80... | collective-permute-start | bytes 1572872 | tf_op jit(solution)/shard_map/ppermute | solution.py:216
  39.8 66.4 %all-to-all-start = ((bf16[16,384,128]{2,1,0:T(8,128)(2,1)}), bf16[16,384,128]{2,1,0:T(8,128)(2,1)}, u32[]{:S(2)}, u32[]{:S(2)}) async-start(bf16[16,384,128]{2,1,0:T(8,128)(2,1)} %pack_rows.1), calls=%async_computation | async-start | bytes 3145728 | tf_op jit(solution)/shard_map/all_to_all | solution.py:442
  45.1 32.0 %collective-permute-start.1 = (bf16[128,2048]{1,0:T(8,128)(2,1)}, bf16[128,2048]{1,0:T(8,128)(2,1)S(1)}, u32[]{:S(2)}, u32[]{:S(2)}) collective-permute-start(bf16[128,2048]{1,0:T(8,128)(2,1)} %collective-permute-done.refs_4_), channel_id=1, source_target_pairs={{0,32},{8,40},{16,48},{24,56},{32,64},{40,72},{48,80},{56,88},{64,... | collective-permute-start | bytes 1572872 | tf_op jit(solution)/shard_map/ppermute | solution.py:216
  46.9 30.2 %collective-permute-start.18 = (bf16[128,2048]{1,0:T(8,128)(2,1)}, bf16[128,2048]{1,0:T(8,128)(2,1)}, u32[]{:S(2)}, u32[]{:S(2)}) collective-permute-start(bf16[128,2048]{1,0:T(8,128)(2,1)} %collective-permute-done.17.refs_3_), channel_id=1, source_target_pairs={{0,96},{8,104},{16,112},{24,120},{32,0},{40,8},{48,16},{56,24},{64... | collective-permute-start | bytes 1572872 | tf_op jit(solution)/shard_map/ppermute | solution.py:216
  48.4 40.0 %collective-permute-start.23 = (bf16[128,2048]{1,0:T(8,128)(2,1)}, bf16[128,2048]{1,0:T(8,128)(2,1)}, u32[]{:S(2)}, u32[]{:S(2)}) collective-permute-start(bf16[128,2048]{1,0:T(8,128)(2,1)} %collective-permute-done.17.refs_3_), channel_id=1, source_target_pairs={{0,32},{8,40},{16,48},{24,56},{32,64},{40,72},{48,80},{56,88},{64,... | collective-permute-start | bytes 1572872 | tf_op jit(solution)/shard_map/ppermute | solution.py:216
  48.9 40.1 %collective-permute-start.25 = (bf16[128,2048]{1,0:T(8,128)(2,1)}, bf16[128,2048]{1,0:T(8,128)(2,1)S(1)}, u32[]{:S(2)}, u32[]{:S(2)}) collective-permute-start(bf16[128,2048]{1,0:T(8,128)(2,1)} %collective-permute-done.17.refs_3_), channel_id=1, source_target_pairs={{0,8},{8,0},{16,24},{24,16},{32,40},{40,32},{48,56},{56,48},{64,72... | collective-permute-start | bytes 1572872 | tf_op jit(solution)/shard_map/ppermute | solution.py:216
  48.9 40.6 %collective-permute-start.26 = (bf16[128,2048]{1,0:T(8,128)(2,1)}, bf16[128,2048]{1,0:T(8,128)(2,1)S(1)}, u32[]{:S(2)}, u32[]{:S(2)}) collective-permute-start(bf16[128,2048]{1,0:T(8,128)(2,1)} %collective-permute-done.15.refs_4_), channel_id=1, source_target_pairs={{0,8},{8,0},{16,24},{24,16},{32,40},{40,32},{48,56},{56,48},{64,72... | collective-permute-start | bytes 1572872 | tf_op jit(solution)/shard_map/ppermute | solution.py:216
  77.1 21.9 %collective-permute-start.16 = (bf16[128,2048]{1,0:T(8,128)(2,1)}, bf16[128,2048]{1,0:T(8,128)(2,1)S(1)}, u32[]{:S(2)}, u32[]{:S(2)}) collective-permute-start(bf16[128,2048]{1,0:T(8,128)(2,1)} %collective-permute-done.15.refs_4_), channel_id=1, source_target_pairs={{0,32},{8,40},{16,48},{24,56},{32,64},{40,72},{48,80},{56,88},{64,... | collective-permute-start | bytes 1572872 | tf_op jit(solution)/shard_map/ppermute | solution.py:216
  90.6 39.6 %collective-permute-start.4 = (bf16[128,2048]{1,0:T(8,128)(2,1)}, bf16[128,2048]{1,0:T(8,128)(2,1)}, u32[]{:S(2)}, u32[]{:S(2)}) collective-permute-start(bf16[128,2048]{1,0:T(8,128)(2,1)} %collective-permute-done.3.refs_7_), channel_id=1, source_target_pairs={{0,96},{8,104},{16,112},{24,120},{32,0},{40,8},{48,16},{56,24},{64... | collective-permute-start | bytes 1572872 | tf_op jit(solution)/shard_map/ppermute | solution.py:216
  99.0 31.7 %collective-permute-start.29 = (bf16[128,2048]{1,0:T(8,128)(2,1)}, bf16[128,2048]{1,0:T(8,128)(2,1)}, u32[]{:S(2)}, u32[]{:S(2)}) collective-permute-start(bf16[128,2048]{1,0:T(8,128)(2,1)} %collective-permute-done.18.refs_7_), channel_id=1, source_target_pairs={{0,8},{8,0},{16,24},{24,16},{32,40},{40,32},{48,56},{56,48},{64,72... | collective-permute-start | bytes 1572872 | tf_op jit(solution)/shard_map/ppermute | solution.py:216
  99.0 31.8 %collective-permute-start.28 = (bf16[128,2048]{1,0:T(8,128)(2,1)}, bf16[128,2048]{1,0:T(8,128)(2,1)}, u32[]{:S(2)}, u32[]{:S(2)}) collective-permute-start(bf16[128,2048]{1,0:T(8,128)(2,1)} %collective-permute-done.23.refs_6_), channel_id=1, source_target_pairs={{0,8},{8,0},{16,24},{24,16},{32,40},{40,32},{48,56},{56,48},{64,72... | collective-permute-start | bytes 1572872 | tf_op jit(solution)/shard_map/ppermute | solution.py:216
  101.0 35.9 %collective-permute-start.20 = (bf16[128,2048]{1,0:T(8,128)(2,1)}, bf16[128,2048]{1,0:T(8,128)(2,1)}, u32[]{:S(2)}, u32[]{:S(2)}) collective-permute-start(bf16[128,2048]{1,0:T(8,128)(2,1)} %copy-done.13), channel_id=1, source_target_pairs={{0,8},{8,0},{16,24},{24,16},{32,40},{40,32},{48,56},{56,48},{64,72... | collective-permute-start | bytes 1572872 | tf_op jit(solution)/shard_map/ppermute | solution.py:216
  104.7 32.3 %collective-permute-start.21 = (bf16[128,2048]{1,0:T(8,128)(2,1)}, bf16[128,2048]{1,0:T(8,128)(2,1)}, u32[]{:S(2)}, u32[]{:S(2)}) collective-permute-start(bf16[128,2048]{1,0:T(8,128)(2,1)} %collective-permute-done.19.refs_3_), channel_id=1, source_target_pairs={{0,8},{8,0},{16,24},{24,16},{32,40},{40,32},{48,56},{56,48},{64,72... | collective-permute-start | bytes 1572872 | tf_op jit(solution)/shard_map/ppermute | solution.py:216
  119.4 80.0 %all-to-all-start.1 = ((bf16[16,320,128]{2,1,0:T(8,128)(2,1)}), bf16[16,320,128]{2,1,0:T(8,128)(2,1)}, u32[]{:S(2)}, u32[]{:S(2)}) async-start(bf16[16,320,128]{2,1,0:T(8,128)(2,1)} %attention_rows.1), calls=%async_computation.1 | async-start | bytes 2621440 | tf_op jit(solution)/shard_map/all_to_all | solution.py:455
  130.2 20.5 %collective-permute-start.5 = (bf16[128,2048]{1,0:T(8,128)(2,1)S(1)}, bf16[128,2048]{1,0:T(8,128)(2,1)}, u32[]{:S(2)}, u32[]{:S(2)}) collective-permute-start(bf16[128,2048]{1,0:T(8,128)(2,1)S(1)} %copy-done.10), channel_id=1, source_target_pairs={{0,8},{8,0},{16,24},{24,16},{32,40},{40,32},{48,56},{56,48},{64,72... | collective-permute-start | bytes 1572872 | tf_op jit(solution)/shard_map/ppermute | solution.py:216
  130.7 20.1 %collective-permute-start.6 = (bf16[128,2048]{1,0:T(8,128)(2,1)}, bf16[128,2048]{1,0:T(8,128)(2,1)}, u32[]{:S(2)}, u32[]{:S(2)}) collective-permute-start(bf16[128,2048]{1,0:T(8,128)(2,1)} %collective-permute-done.4.refs_3_), channel_id=1, source_target_pairs={{0,8},{8,0},{16,24},{24,16},{32,40},{40,32},{48,56},{56,48},{64,72... | collective-permute-start | bytes 1572872 | tf_op jit(solution)/shard_map/ppermute | solution.py:216
  161.9 32.5 %collective-permute-start.40 = (bf16[2,704,256]{2,1,0:T(8,128)(2,1)}, bf16[2,704,256]{2,1,0:T(8,128)(2,1)}, u32[]{:S(2)}, u32[]{:S(2)}) collective-permute-start(bf16[2,704,256]{2,1,0:T(8,128)(2,1)} %get-tuple-element.24), channel_id=1, source_target_pairs={{0,1},{1,2},{2,3},{3,0},{4,5},{5,6},{6,7},{7,4},{8,9},{9,10},{10,1... | collective-permute-start | bytes 2162696 | tf_op jit(solution)/shard_map/ppermute | solution.py:338
  163.4 31.0 %collective-permute-start.42 = (bf16[2,704,256]{2,1,0:T(8,128)(2,1)}, bf16[2,704,256]{2,1,0:T(8,128)(2,1)}, u32[]{:S(2)}, u32[]{:S(2)}) collective-permute-start(bf16[2,704,256]{2,1,0:T(8,128)(2,1)} %get-tuple-element.33), channel_id=1, source_target_pairs={{0,3},{1,0},{2,1},{3,2},{4,7},{5,4},{6,5},{7,6},{8,11},{9,8},{10,9... | collective-permute-start | bytes 2162696 | tf_op jit(solution)/shard_map/ppermute | solution.py:339
  180.5 41.9 %collective-permute-start.35 = (bf16[4,704,256]{2,1,0:T(8,128)(2,1)}, bf16[4,704,256]{2,1,0:T(8,128)(2,1)S(1)}, u32[]{:S(2)}, u32[]{:S(2)}) collective-permute-start(bf16[4,704,256]{2,1,0:T(8,128)(2,1)} %get-tuple-element.31), channel_id=1, source_target_pairs={{0,4},{1,5},{2,6},{3,7},{4,0},{5,1},{6,2},{7,3},{8,12},{9,13},{10,... | collective-permute-start | bytes 4325384 | tf_op jit(solution)/shard_map/ppermute | solution.py:350
  192.4 19.3 %collective-permute-start.30 = (bf16[2,704,256]{2,1,0:T(8,128)(2,1)}, bf16[2,704,256]{2,1,0:T(8,128)(2,1)}, u32[]{:S(2)}, u32[]{:S(2)}) collective-permute-start(bf16[2,704,256]{2,1,0:T(8,128)(2,1)} %get-tuple-element.28), channel_id=1, source_target_pairs={{0,1},{1,2},{2,3},{3,0},{4,5},{5,6},{6,7},{7,4},{8,9},{9,10},{10,1... | collective-permute-start | bytes 2162696 | tf_op jit(solution)/shard_map/ppermute | solution.py:338
  196.5 24.5 %collective-permute-start.43 = (bf16[704,256]{1,0:T(8,128)(2,1)}, bf16[704,256]{1,0:T(8,128)(2,1)}, u32[]{:S(2)}, u32[]{:S(2)}) collective-permute-start(bf16[704,256]{1,0:T(8,128)(2,1)} %get-tuple-element.45), channel_id=1, source_target_pairs={{0,3},{1,0},{2,1},{3,2},{4,7},{5,4},{6,5},{7,6},{8,11},{9,8},{10,9... | collective-permute-start | bytes 1081352 | tf_op jit(solution)/shard_map/ppermute | solution.py:343
  201.7 33.0 %collective-permute-start.41 = (bf16[704,256]{1,0:T(8,128)(2,1)S(1)}, bf16[704,256]{1,0:T(8,128)(2,1)S(1)}, u32[]{:S(2)}, u32[]{:S(2)}) collective-permute-start(bf16[704,256]{1,0:T(8,128)(2,1)S(1)} %get-tuple-element.44), channel_id=1, source_target_pairs={{0,1},{1,2},{2,3},{3,0},{4,5},{5,6},{6,7},{7,4},{8,9},{9,10},{10,1... | collective-permute-start | bytes 1081352 | tf_op jit(solution)/shard_map/ppermute | solution.py:342
  216.4 20.9 %collective-permute-start.31 = (bf16[704,256]{1,0:T(8,128)(2,1)S(1)}, bf16[704,256]{1,0:T(8,128)(2,1)S(1)}, u32[]{:S(2)}, u32[]{:S(2)}) collective-permute-start(bf16[704,256]{1,0:T(8,128)(2,1)S(1)} %get-tuple-element.46), channel_id=1, source_target_pairs={{0,1},{1,2},{2,3},{3,0},{4,5},{5,6},{6,7},{7,4},{8,9},{9,10},{10,1... | collective-permute-start | bytes 1081352 | tf_op jit(solution)/shard_map/ppermute | solution.py:342
  (43 other events, 641.4 us)

commit v2 on v1

--- a/solution.py
+++ b/solution.py
@@ -14,7 +14,7 @@
 BLK = 128
 NSEL = 4
 HALF = BLK // 2
-TOGETHER = 2
+TOGETHER = 4
 
 
 def dot_nt(a, b):
@@ -209,6 +209,8 @@
 
 X_UP = sequence_moves(lambda z, x: (z, x + 1))
 X_DOWN = sequence_moves(lambda z, x: (z, x - 1))
+X_FAR = sequence_moves(lambda z, x: (z, x + 2))
+X_MOVES = (X_FAR, X_UP, X_DOWN)
 FAR_SWAP = sequence_moves(lambda z, x: (z + 1, x))
 
 
@@ -238,7 +240,7 @@
 
 def pick_rows(onehot, coef, pieces, scaled, buffer, first):
     count, (rows, width), slots = len(pieces), pieces[0].shape, onehot.shape[1]
-    tile = 1024 if len(pieces) <= 2 * LATE else 512
+    tile = 1024
     total = 2 * len(PIECE_STEPS) * slots
     in_specs = [
         pl.BlockSpec((count, slots, rows), lambda j: (0, 0, 0)),
@@ -323,8 +325,8 @@
     return jnp.stack([((z + dz) % 2) * 4 + (x + dx) % 4 for dx, dz in steps]).astype(jnp.int32)
 
 
-RING_FIRST = ((2, 0), (1, 1), (2, 1), (3, 0), (1, 0), (3, 1), (0, 1), (0, 0))
-ACROSS_FIRST = ((2, 1), (1, 1), (3, 1), (0, 1), (2, 0), (1, 0), (3, 0), (0, 0))
+X_FIRST = ((2, 0), (2, 1), (1, 0), (1, 1), (3, 0), (3, 1), (0, 0), (0, 1))
+Z_FIRST = ((2, 1), (1, 1), (3, 1), (0, 1), (2, 0), (1, 0), (3, 0), (0, 0))
 
 
 def add_terms(*terms):
@@ -334,35 +336,19 @@
     return total
 
 
-def sum_ring_first(upward, downward, rest):
-    from_below = lax.ppermute(upward, "dp", X_UP)
-    from_above = lax.ppermute(downward, "dp", X_DOWN)
-    send_up = add_terms(rest[0], from_below[0]).astype(jnp.bfloat16)
-    send_down = add_terms(rest[1], from_above[0]).astype(jnp.bfloat16)
-    up_same = lax.ppermute(send_up, "dp", X_UP)
-    down_other = lax.ppermute(send_down, "dp", X_DOWN)
-    across = add_terms(rest[2], from_below[1], down_other).astype(jnp.bfloat16)
-    arrived = lax.ppermute(across, "dp", FAR_SWAP)
-    return add_terms(rest[3], up_same, from_above[1], arrived).T[None]
-
-
-def sum_across_first(other, same):
-    arrived = lax.ppermute(other, "dp", FAR_SWAP)
-    cut = same.shape[1] // 2
-
-    def kept(place, rows):
-        return add_terms(same[place, rows], arrived[place, rows])
-
-    head, tail = slice(0, cut), slice(cut, None)
-    far_head = kept(0, head).astype(jnp.bfloat16)
-    far_tail = kept(0, tail).astype(jnp.bfloat16)
-    up_far = lax.ppermute(far_head, "dp", X_UP)
-    down_far = lax.ppermute(far_tail, "dp", X_DOWN)
-    next_sum = jnp.concatenate([kept(1, head) + up_far.astype(jnp.float32), kept(1, tail)])
-    back_sum = jnp.concatenate([kept(2, head), kept(2, tail) + down_far.astype(jnp.float32)])
-    from_below = lax.ppermute(next_sum.astype(jnp.bfloat16), "dp", X_UP)
-    from_above = lax.ppermute(back_sum.astype(jnp.bfloat16), "dp", X_DOWN)
-    return add_terms(kept(3, slice(None)), from_below, from_above).T[None]
+def sum_x_first(*terms):
+    arrived = [lax.ppermute(term, "dp", move) for term, move in zip(terms, X_MOVES)]
+    parts = [terms[-1], *arrived]
+    across = add_terms(*(part[1] for part in parts)).astype(jnp.bfloat16)
+    other = lax.ppermute(across, "dp", FAR_SWAP)
+    return add_terms(*(part[0] for part in parts), other).T[None]
+
+
+def sum_z_first(other, same):
+    joined = lax.ppermute(other, "dp", FAR_SWAP)
+    sums = [add_terms(same[k], joined[k]).astype(jnp.bfloat16) for k in range(len(X_MOVES))]
+    arrived = [lax.ppermute(term, "dp", move) for term, move in zip(sums, X_MOVES)]
+    return add_terms(same[-1], joined[-1], *arrived).T[None]
 
 
 def per_device(
@@ -436,9 +422,9 @@
     g_far_others = [pass_on(piece, CORE_SWAP) for piece in g_fars]
     grads_in = late_pick(g_fars, g_far_others, True, g_buffer)
 
-    ring_order, across_order = term_order(RING_FIRST), term_order(ACROSS_FIRST)
-    down_terms = weight_terms(ring_order, hidden.T, grads_in, (2, 2, 4))
-    down_grad = sum_ring_first(*down_terms)
+    x_order, z_order = term_order(X_FIRST), term_order(Z_FIRST)
+    down_terms = weight_terms(x_order, hidden.T, grads_in, (2, 2, 2, 2))
+    down_grad = sum_x_first(*down_terms)
     head_rows = lax.all_to_all(packed, "ctx", split_axis=0, concat_axis=0, tiled=True)
     later_grads = lax.optimization_barrier((grads_in, down_terms[0]))[0]
     hidden_grad = dot_nn(later_grads, down_weight[0])
@@ -446,9 +432,9 @@
         hidden_grad * up_pre * gate_sig * (1.0 + gate_pre * (1.0 - gate_sig))
     ).astype(jnp.bfloat16)
     up_delta = (hidden_grad * gate_act).astype(jnp.bfloat16)
-    up_grad = sum_across_first(*weight_terms(across_order, up_delta.T, rows_in, (4, 4)))
-    gate_terms = weight_terms(ring_order, gate_delta.T, rows_in, (2, 2, 4))
-    gate_grad = sum_ring_first(*gate_terms)
+    up_grad = sum_z_first(*weight_terms(z_order, up_delta.T, rows_in, (4, 4)))
+    gate_terms = weight_terms(x_order, gate_delta.T, rows_in, (2, 2, 2, 2))
+    gate_grad = sum_x_first(*gate_terms)
 
     half = (my_index % 2).astype(jnp.int32).reshape(1)
     grad_rows = attention_rows(block_lists.reshape(-1), block_lengths.reshape(-1), half, head_rows)

time: 248 us -> 255 us (1.028)
  waiting for transfers between devices: 86.8 us -> 101 us
  Pallas kernels: 63.7 us -> 59.1 us
  other arithmetic: 16.2 us -> 13.5 us
    ppermute x15 -> x12, waiting for transfers between devices: 24.4 us -> 38.7 us  [the longest x6 30.5 us: sum_x_first(): lax.ppermute(term, 'dp', move)]
    convert_element_type x5 -> x1, other arithmetic: 6.23 us -> 0.25 us  [sum_z_first(): add_terms(same[k], joined[k]).astype(jnp.bfloat16)]
    add x0 -> x2, other arithmetic: none -> 2.98 us  [add_terms(): total = total + term.astype(jnp.float32)]
    pallas_call x4, Pallas kernels: 18 us -> 15.3 us  [pick_rows(): pl.pallas_call(lambda *refs: pick_kernel(count, scaled, *refs), grid=(wid...]
    ppermute x15 -> x12, starting transfers between devices: 19.6 us -> 19.1 us  [the longest x6 8.27 us: sum_x_first(): lax.ppermute(term, 'dp', move)]
  transfers between devices with their start and end apart: 48 -> 45, of which waited for: 16 -> 16; matrix products, arithmetic and copies ran while one was open for 16% -> 14% of each run, Pallas kernels for 26% -> 23%
where the time goes in v2:
time: 255 us; the launch traced here: 253 us
  waiting for transfers between devices  101 us (40%)
  Pallas kernels  59.1 us (23%)
  starting transfers between devices  52.7 us (21%)
  matrix products  19.3 us (8%)
  other arithmetic  13.5 us (5%)
  local copies, waits for them, and re-layouts  6.43 us (3%)
    ppermute x30, waiting for transfers between devices, pass_on(): return lax.ppermute(value, 'ctx', move)  62.4 us
    ppermute x6, waiting for transfers between devices, sum_x_first(): lax.ppermute(term, 'dp', move)  30.5 us
    pallas_call x3, Pallas kernels, weight_terms(): pl.pallas_call(lambda *refs: term_kernel(per_step, homes, *refs), grid_sp...  24.7 us
    ppermute x30, starting transfers between devices, pass_on(): return lax.ppermute(value, 'ctx', move)  20.4 us
    dot_general x3, matrix products, dot_nn(): lax.dot_general(a, b, (((1,), (0,)), ((), ())), preferred_element_type=jn...  19.3 us
    pallas_call x4, Pallas kernels, pick_rows(): pl.pallas_call(lambda *refs: pick_kernel(count, scaled, *refs), grid=(wid...  15.3 us
    pallas_call x1, Pallas kernels, attention_rows(): pl.pallas_call(attention_kernel, in_specs=[smem, smem, smem, vmem], out_s...  11.3 us
    ppermute x6, starting transfers between devices, sum_x_first(): lax.ppermute(term, 'dp', move)  8.27 us
  transfers between devices with their start and end apart: 45, of which 16 were waited for; matrix products, arithmetic and copies ran while one was open for 14% of the time, Pallas kernels for 23%

profile of v2, /device:TPU:2, one launch (start us, length us, event | category | flops | bytes accessed | tf_op | source)
XLA Modules:
  0.0 253.3 jit_solution(17832623343191348488)
XLA Ops:
  6.0 9.7 %collective-permute-done.2.refs_3_ = bf16[128,2048]{1,0:T(8,128)(2,1)S(1)} collective-permute-done((bf16[128,2048]{1,0:T(8,128)(2,1)}, bf16[128,2048]{1,0:T(8,128)(2,1)S(1)}, u32[]{:S(2)}, u32[]{:S(2)}) %collective-permute-start.2) | collective-permute-done | bytes 524320 | tf_op jit(solution)/shard_map/ppermute | solution.py:218
  21.6 4.2 %all-to-all-start.2 = ((f32[16,1,128]{2,1,0:T(1,128)}), f32[16,1,128]{2,1,0:T(1,128)S(1)}, u32[]{:S(2)}, u32[]{:S(2)}) async-start(f32[16,1,128]{2,1,0:T(1,128)} %bitcast.18), calls=%async_computation.2 | async-start | bytes 16384 | tf_op jit(solution)/shard_map/all_to_all | solution.py:378
  32.4 5.4 %pack_rows.1 = bf16[16,384,128]{2,1,0:T(8,128)(2,1)} custom-call(bf16[128,1024]{1,0:T(8,128)(2,1)} %bitcast.126, bf16[128,1024]{1,0:T(8,128)(2,1)} %bitcast.127, bf16[128,1024]{1,0:T(8,128)(2,1)} %bitcast.128, bf16[128,2048]{1,0:T(8,128)(2,1)} %bitcast.117, bf16[1024,2048]{1,0:T(8,128)(2,1)} %w_ref.1), custom_call_target="tpu_custom_call" | custom-call | flops 536870912 | bytes 7000000 | tf_op jit(solution)/shard_map/pack_rows/pallas_call | solution.py:47
  39.7 4.4 %all-to-all-start = ((bf16[16,384,128]{2,1,0:T(8,128)(2,1)}), bf16[16,384,128]{2,1,0:T(8,128)(2,1)}, u32[]{:S(2)}, u32[]{:S(2)}) async-start(bf16[16,384,128]{2,1,0:T(8,128)(2,1)} %pack_rows.1), calls=%async_computation | async-start | bytes 3145728 | tf_op jit(solution)/shard_map/all_to_all | solution.py:428
  49.7 27.3 %collective-permute-done.1.refs_2_ = bf16[128,2048]{1,0:T(8,128)(2,1)S(1)} collective-permute-done((bf16[128,2048]{1,0:T(8,128)(2,1)}, bf16[128,2048]{1,0:T(8,128)(2,1)S(1)}, u32[]{:S(2)}, u32[]{:S(2)}) %collective-permute-start.1) | collective-permute-done | bytes 524320 | tf_op jit(solution)/shard_map/ppermute | solution.py:218
  77.1 11.2 %collective-permute-done.23.refs_6_ = bf16[128,2048]{1,0:T(8,128)(2,1)} collective-permute-done((bf16[128,2048]{1,0:T(8,128)(2,1)}, bf16[128,2048]{1,0:T(8,128)(2,1)}, u32[]{:S(2)}, u32[]{:S(2)}) %collective-permute-start.23) | collective-permute-done | bytes 524320 | tf_op jit(solution)/shard_map/ppermute | solution.py:218
  91.2 7.8 %collective-permute-done.16.refs_2_ = bf16[128,2048]{1,0:T(8,128)(2,1)S(1)} collective-permute-done((bf16[128,2048]{1,0:T(8,128)(2,1)}, bf16[128,2048]{1,0:T(8,128)(2,1)S(1)}, u32[]{:S(2)}, u32[]{:S(2)}) %collective-permute-start.16) | collective-permute-done | bytes 524320 | tf_op jit(solution)/shard_map/ppermute | solution.py:218
  106.2 11.3 %attention_rows.1 = bf16[16,320,128]{2,1,0:T(8,128)(2,1)} custom-call(s32[64]{0:T(128)} %reshape.703.lists_ref, s32[16]{0:T(128)} %bitcast.131, s32[1]{0:T(128)} %bitcast.1.half_ref, bf16[16,384,128]{2,1,0:T(8,128)(2,1)} %all-to-all-done.rows_ref), custom_call_target="tpu_custom_call" | custom-call | bytes 3000000 | tf_op jit(solution)/shard_map/attention_rows/pallas_call | solution.py:142
  117.5 4.6 %all-to-all-start.1 = ((bf16[16,320,128]{2,1,0:T(8,128)(2,1)}), bf16[16,320,128]{2,1,0:T(8,128)(2,1)}, u32[]{:S(2)}, u32[]{:S(2)}) async-start(bf16[16,320,128]{2,1,0:T(8,128)(2,1)} %attention_rows.1), calls=%async_computation.1 | async-start | bytes 2621440 | tf_op jit(solution)/shard_map/all_to_all | solution.py:441
  122.1 4.9 %pick_rows.4.refs_6_ = bf16[1024,2048]{1,0:T(8,128)(2,1)} custom-call(bf16[12,64,128]{2,1,0:T(8,128)(2,1)} %pad_maximum_fusion.1.refs_0_, f32[12,64,1]{2,1,0:T(8,128)} %pad_maximum_fusion.refs_1_, bf16[128,2048]{1,0:T(8,128)(2,1)} %bitcast.118, bf16[128,2048]{1,0:T(8,128)(2,1)} %copy-done.8, bf16[128,2048]{1,0:T(8,128)(2,1)} %collective-permute-done.refs_4_, ...), custom_call_target="tpu_custom_call" | custom-call | flops 402653184 | bytes 9437184 | tf_op jit(solution)/shard_map/pick_rows/pallas_call | solution.py:256
  127.6 4.8 %pick_rows.6.refs_6_ = bf16[1024,2048]{1,0:T(8,128)(2,1)} custom-call(bf16[12,64,128]{2,1,0:T(8,128)(2,1)} %pad_maximum_fusion.1.refs_0_, f32[12,64,1]{2,1,0:T(8,128)} %pad_maximum_fusion.refs_1_, bf16[128,2048]{1,0:T(8,128)(2,1)} %bitcast.125, bf16[128,2048]{1,0:T(8,128)(2,1)} %collective-permute-done.17.refs_3_, ...), custom_call_target="tpu_custom_call" | custom-call | flops 402653184 | bytes 9437184 | tf_op jit(solution)/shard_map/pick_rows/pallas_call | solution.py:256
  135.3 6.0 %fusion.2 = f32[1024,704]{0,1:T(8,128)S(1)} fusion(bf16[1024,2048]{1,0:T(8,128)(2,1)} %pick_rows.7.refs_2_.refs_3_.refs_4_.refs_5_, bf16[1,2048,704]{1,2,0:T(8,128)(2,1)} %param.23), kind=kOutput, calls=%fused_computation.3 | convolution fusion | flops 2952790016 | bytes 9961472 | tf_op jit(solution)/shard_map/dot_general | solution.py:25
  141.3 4.9 %multiply_convert_fusion.2 = (bf16[1024,704]{0,1:T(8,128)(2,1)}, f32[1024,704]{0,1:T(8,128)}) fusion(f32[1024,704]{0,1:T(8,128)S(1)} %fusion.2, bf16[1024,2048]{1,0:T(8,128)(2,1)S(1)} %copy-done.2, bf16[1,2048,704]{1,2,0:T(8,128)(2,1)S(1)} %copy-done), kind=kOutput, calls=%fused_computation.9 | convolution fusion | flops 2957115392 | bytes 14286848 | tf_op jit(solution)/shard_map/dot_general | solution.py:25
  149.1 8.3 %weight_terms.3 = (bf16[2,704,256]{2,1,0:T(8,128)(2,1)}, bf16[2,704,256]{2,1,0:T(8,128)(2,1)}, bf16[2,704,256]{2,1,0:T(8,128)(2,1)}, bf16[2,704,256]{2,1,0:T(8,128)(2,1)}) custom-call(s32[8]{0:T(128)} %stack.97.refs_0_, bf16[704,1024]{1,0:T(8,128)(2,1)} %bitcast.119, bf16[1024,2048]{1,0:T(8,128)(2,1)} %pick_rows.5.refs_2_.refs_3_.refs_4_.refs_5_, ...), custom_call_target="tpu_custom_call" | custom-call | bytes 1000000 | tf_op jit(solution)/shard_map/weight_terms/pallas_call | solution.py:299
  159.5 8.4 %fusion.7 = (bf16[704,1024]{1,0:T(8,128)(2,1)}, bf16[704,1024]{1,0:T(8,128)(2,1)}) fusion(f32[1024,704]{0,1:T(8,128)} %copy-done.18, f32[1024,704]{0,1:T(8,128)} %get-tuple-element.28, bf16[1024,2048]{1,0:T(8,128)(2,1)} %pick_rows.5.refs_2_.refs_3_.refs_4_.refs_5_, bf16[1,2048,704]{1,2,0:T(8,128)(2,1)S(1)} %copy-done.17), kind=kOutput, calls=%fused_computation.12 | convolution fusion | flops 2962161664 | bytes 15728640 | tf_op jit(solution)/shard_map/dot_general | solution.py:25
  167.9 8.2 %weight_terms.5 = (bf16[4,704,256]{2,1,0:T(8,128)(2,1)}, bf16[4,704,256]{2,1,0:T(8,128)(2,1)}) custom-call(s32[8]{0:T(128)} %stack.115.refs_0_, bf16[704,1024]{1,0:T(8,128)(2,1)} %get-tuple-element.40.refs_1_, bf16[1024,2048]{1,0:T(8,128)(2,1)} %pick_rows.7.refs_2_.refs_3_.refs_4_.refs_5_, bf16[1024,2048]{1,0:T(8,128)(2,1)} %pick_rows.7.refs_2_.refs_3_.refs_4_.refs_5_, ...), custom_call_target="tpu_custom_call" | custom-call | bytes 1000000 | tf_op jit(solution)/shard_map/weight_terms/pallas_call | solution.py:299
  176.1 3.6 %collective-permute-start.34 = (bf16[4,704,256]{2,1,0:T(8,128)(2,1)}, bf16[4,704,256]{2,1,0:T(8,128)(2,1)S(1)}, u32[]{:S(2)}, u32[]{:S(2)}) collective-permute-start(bf16[4,704,256]{2,1,0:T(8,128)(2,1)} %get-tuple-element.34), channel_id=1, source_target_pairs={{0,4},{1,5},{2,6},{3,7},{4,0},{5,1},{6,2},{7,3},{8,12},{9,13},{10,... | collective-permute-start | bytes 4325384 | tf_op jit(solution)/shard_map/ppermute | solution.py:348
  181.7 8.2 %weight_terms.4 = (bf16[2,704,256]{2,1,0:T(8,128)(2,1)}, bf16[2,704,256]{2,1,0:T(8,128)(2,1)}, bf16[2,704,256]{2,1,0:T(8,128)(2,1)}, bf16[2,704,256]{2,1,0:T(8,128)(2,1)}) custom-call(s32[8]{0:T(128)} %stack.97.refs_0_, bf16[704,1024]{1,0:T(8,128)(2,1)} %get-tuple-element.41.refs_1_, bf16[1024,2048]{1,0:T(8,128)(2,1)} %pick_rows.7.refs_2_.refs_3_.refs_4_.refs_5_, ...), custom_call_target="tpu_custom_call" | custom-call | bytes 1000000 | tf_op jit(solution)/shard_map/weight_terms/pallas_call | solution.py:299
  196.3 3.5 %collective-permute-done.40 = bf16[2,704,256]{2,1,0:T(8,128)(2,1)} collective-permute-done((bf16[2,704,256]{2,1,0:T(8,128)(2,1)}, bf16[2,704,256]{2,1,0:T(8,128)(2,1)}, u32[]{:S(2)}, u32[]{:S(2)}) %collective-permute-start.40) | collective-permute-done | bytes 720928 | tf_op jit(solution)/shard_map/ppermute | solution.py:340
  201.8 14.2 %collective-permute-done.30 = bf16[2,704,256]{2,1,0:T(8,128)(2,1)} collective-permute-done((bf16[2,704,256]{2,1,0:T(8,128)(2,1)}, bf16[2,704,256]{2,1,0:T(8,128)(2,1)}, u32[]{:S(2)}, u32[]{:S(2)}) %collective-permute-start.30) | collective-permute-done | bytes 720928 | tf_op jit(solution)/shard_map/ppermute | solution.py:340
  216.0 8.1 %collective-permute-done.31 = bf16[2,704,256]{2,1,0:T(8,128)(2,1)} collective-permute-done((bf16[2,704,256]{2,1,0:T(8,128)(2,1)}, bf16[2,704,256]{2,1,0:T(8,128)(2,1)}, u32[]{:S(2)}, u32[]{:S(2)}) %collective-permute-start.31) | collective-permute-done | bytes 720928 | tf_op jit(solution)/shard_map/ppermute | solution.py:340
  224.1 4.7 %collective-permute-done.32 = bf16[2,704,256]{2,1,0:T(8,128)(2,1)} collective-permute-done((bf16[2,704,256]{2,1,0:T(8,128)(2,1)}, bf16[2,704,256]{2,1,0:T(8,128)(2,1)}, u32[]{:S(2)}, u32[]{:S(2)}) %collective-permute-start.32) | collective-permute-done | bytes 720928 | tf_op jit(solution)/shard_map/ppermute | solution.py:340
  232.5 3.6 %collective-permute-start.35 = (bf16[704,256]{1,0:T(8,128)(2,1)S(1)}, bf16[704,256]{1,0:T(8,128)(2,1)S(1)}, u32[]{:S(2)}, u32[]{:S(2)}) collective-permute-start(bf16[704,256]{1,0:T(8,128)(2,1)S(1)} %get-tuple-element.42), channel_id=1, source_target_pairs={{0,2},{1,3},{2,0},{3,1},{4,6},{5,7},{6,4},{7,5},{8,10},{9,11},{10,... | collective-permute-start | bytes 1081352 | tf_op jit(solution)/shard_map/ppermute | solution.py:350
  245.4 5.4 %collective-permute-done.36 = bf16[704,256]{1,0:T(8,128)(2,1)S(1)} collective-permute-done((bf16[704,256]{1,0:T(8,128)(2,1)S(1)}, bf16[704,256]{1,0:T(8,128)(2,1)S(1)}, u32[]{:S(2)}, u32[]{:S(2)}) %collective-permute-start.36) | collective-permute-done | bytes 360480 | tf_op jit(solution)/shard_map/ppermute | solution.py:350
  (150 shorter events, 69.3 us)
Async XLA Ops:
  5.9 20.2 %collective-permute-start.9 = (bf16[128,2048]{1,0:T(8,128)(2,1)}, bf16[128,2048]{1,0:T(8,128)(2,1)}, u32[]{:S(2)}, u32[]{:S(2)}) collective-permute-start(bf16[128,2048]{1,0:T(8,128)(2,1)} %bitcast.116), channel_id=1, source_target_pairs={{0,8},{8,0},{16,24},{24,16},{32,40},{40,32},{48,56},{56,48},{64,72... | collective-permute-start | bytes 1572872 | tf_op jit(solution)/shard_map/ppermute | solution.py:218
  5.9 23.3 %collective-permute-start.17 = (bf16[128,2048]{1,0:T(8,128)(2,1)}, bf16[128,2048]{1,0:T(8,128)(2,1)}, u32[]{:S(2)}, u32[]{:S(2)}) collective-permute-start(bf16[128,2048]{1,0:T(8,128)(2,1)} %bitcast.121), channel_id=1, source_target_pairs={{0,16},{8,24},{16,0},{24,8},{32,48},{40,56},{48,32},{56,40},{64,80... | collective-permute-start | bytes 1572872 | tf_op jit(solution)/shard_map/ppermute | solution.py:218
  39.7 66.4 %all-to-all-start = ((bf16[16,384,128]{2,1,0:T(8,128)(2,1)}), bf16[16,384,128]{2,1,0:T(8,128)(2,1)}, u32[]{:S(2)}, u32[]{:S(2)}) async-start(bf16[16,384,128]{2,1,0:T(8,128)(2,1)} %pack_rows.1), calls=%async_computation | async-start | bytes 3145728 | tf_op jit(solution)/shard_map/all_to_all | solution.py:428
  45.0 32.0 %collective-permute-start.1 = (bf16[128,2048]{1,0:T(8,128)(2,1)}, bf16[128,2048]{1,0:T(8,128)(2,1)S(1)}, u32[]{:S(2)}, u32[]{:S(2)}) collective-permute-start(bf16[128,2048]{1,0:T(8,128)(2,1)} %collective-permute-done.refs_4_), channel_id=1, source_target_pairs={{0,32},{8,40},{16,48},{24,56},{32,64},{40,72},{48,80},{56,88},{64,... | collective-permute-start | bytes 1572872 | tf_op jit(solution)/shard_map/ppermute | solution.py:218
  46.8 30.2 %collective-permute-start.18 = (bf16[128,2048]{1,0:T(8,128)(2,1)}, bf16[128,2048]{1,0:T(8,128)(2,1)}, u32[]{:S(2)}, u32[]{:S(2)}) collective-permute-start(bf16[128,2048]{1,0:T(8,128)(2,1)} %collective-permute-done.17.refs_3_), channel_id=1, source_target_pairs={{0,96},{8,104},{16,112},{24,120},{32,0},{40,8},{48,16},{56,24},{64... | collective-permute-start | bytes 1572872 | tf_op jit(solution)/shard_map/ppermute | solution.py:218
  48.3 40.0 %collective-permute-start.23 = (bf16[128,2048]{1,0:T(8,128)(2,1)}, bf16[128,2048]{1,0:T(8,128)(2,1)}, u32[]{:S(2)}, u32[]{:S(2)}) collective-permute-start(bf16[128,2048]{1,0:T(8,128)(2,1)} %collective-permute-done.17.refs_3_), channel_id=1, source_target_pairs={{0,32},{8,40},{16,48},{24,56},{32,64},{40,72},{48,80},{56,88},{64,... | collective-permute-start | bytes 1572872 | tf_op jit(solution)/shard_map/ppermute | solution.py:218
  48.9 40.1 %collective-permute-start.25 = (bf16[128,2048]{1,0:T(8,128)(2,1)}, bf16[128,2048]{1,0:T(8,128)(2,1)S(1)}, u32[]{:S(2)}, u32[]{:S(2)}) collective-permute-start(bf16[128,2048]{1,0:T(8,128)(2,1)} %collective-permute-done.17.refs_3_), channel_id=1, source_target_pairs={{0,8},{8,0},{16,24},{24,16},{32,40},{40,32},{48,56},{56,48},{64,72... | collective-permute-start | bytes 1572872 | tf_op jit(solution)/shard_map/ppermute | solution.py:218
  48.9 40.6 %collective-permute-start.26 = (bf16[128,2048]{1,0:T(8,128)(2,1)}, bf16[128,2048]{1,0:T(8,128)(2,1)S(1)}, u32[]{:S(2)}, u32[]{:S(2)}) collective-permute-start(bf16[128,2048]{1,0:T(8,128)(2,1)} %collective-permute-done.15.refs_4_), channel_id=1, source_target_pairs={{0,8},{8,0},{16,24},{24,16},{32,40},{40,32},{48,56},{56,48},{64,72... | collective-permute-start | bytes 1572872 | tf_op jit(solution)/shard_map/ppermute | solution.py:218
  77.0 21.9 %collective-permute-start.16 = (bf16[128,2048]{1,0:T(8,128)(2,1)}, bf16[128,2048]{1,0:T(8,128)(2,1)S(1)}, u32[]{:S(2)}, u32[]{:S(2)}) collective-permute-start(bf16[128,2048]{1,0:T(8,128)(2,1)} %collective-permute-done.15.refs_4_), channel_id=1, source_target_pairs={{0,32},{8,40},{16,48},{24,56},{32,64},{40,72},{48,80},{56,88},{64,... | collective-permute-start | bytes 1572872 | tf_op jit(solution)/shard_map/ppermute | solution.py:218
  90.5 36.5 %collective-permute-start.4 = (bf16[128,2048]{1,0:T(8,128)(2,1)}, bf16[128,2048]{1,0:T(8,128)(2,1)}, u32[]{:S(2)}, u32[]{:S(2)}) collective-permute-start(bf16[128,2048]{1,0:T(8,128)(2,1)} %collective-permute-done.3.refs_7_), channel_id=1, source_target_pairs={{0,96},{8,104},{16,112},{24,120},{32,0},{40,8},{48,16},{56,24},{64... | collective-permute-start | bytes 1572872 | tf_op jit(solution)/shard_map/ppermute | solution.py:218
  98.9 28.5 %collective-permute-start.29 = (bf16[128,2048]{1,0:T(8,128)(2,1)}, bf16[128,2048]{1,0:T(8,128)(2,1)}, u32[]{:S(2)}, u32[]{:S(2)}) collective-permute-start(bf16[128,2048]{1,0:T(8,128)(2,1)} %collective-permute-done.18.refs_7_), channel_id=1, source_target_pairs={{0,8},{8,0},{16,24},{24,16},{32,40},{40,32},{48,56},{56,48},{64,72... | collective-permute-start | bytes 1572872 | tf_op jit(solution)/shard_map/ppermute | solution.py:218
  99.0 28.7 %collective-permute-start.28 = (bf16[128,2048]{1,0:T(8,128)(2,1)}, bf16[128,2048]{1,0:T(8,128)(2,1)}, u32[]{:S(2)}, u32[]{:S(2)}) collective-permute-start(bf16[128,2048]{1,0:T(8,128)(2,1)} %collective-permute-done.23.refs_6_), channel_id=1, source_target_pairs={{0,8},{8,0},{16,24},{24,16},{32,40},{40,32},{48,56},{56,48},{64,72... | collective-permute-start | bytes 1572872 | tf_op jit(solution)/shard_map/ppermute | solution.py:218
  101.0 31.5 %collective-permute-start.20 = (bf16[128,2048]{1,0:T(8,128)(2,1)}, bf16[128,2048]{1,0:T(8,128)(2,1)}, u32[]{:S(2)}, u32[]{:S(2)}) collective-permute-start(bf16[128,2048]{1,0:T(8,128)(2,1)} %copy-done.13), channel_id=1, source_target_pairs={{0,8},{8,0},{16,24},{24,16},{32,40},{40,32},{48,56},{56,48},{64,72... | collective-permute-start | bytes 1572872 | tf_op jit(solution)/shard_map/ppermute | solution.py:218
  104.6 27.8 %collective-permute-start.21 = (bf16[128,2048]{1,0:T(8,128)(2,1)}, bf16[128,2048]{1,0:T(8,128)(2,1)}, u32[]{:S(2)}, u32[]{:S(2)}) collective-permute-start(bf16[128,2048]{1,0:T(8,128)(2,1)} %collective-permute-done.19.refs_3_), channel_id=1, source_target_pairs={{0,8},{8,0},{16,24},{24,16},{32,40},{40,32},{48,56},{56,48},{64,72... | collective-permute-start | bytes 1572872 | tf_op jit(solution)/shard_map/ppermute | solution.py:218
  117.5 76.5 %all-to-all-start.1 = ((bf16[16,320,128]{2,1,0:T(8,128)(2,1)}), bf16[16,320,128]{2,1,0:T(8,128)(2,1)}, u32[]{:S(2)}, u32[]{:S(2)}) async-start(bf16[16,320,128]{2,1,0:T(8,128)(2,1)} %attention_rows.1), calls=%async_computation.1 | async-start | bytes 2621440 | tf_op jit(solution)/shard_map/all_to_all | solution.py:441
  127.0 19.3 %collective-permute-start.5 = (bf16[128,2048]{1,0:T(8,128)(2,1)S(1)}, bf16[128,2048]{1,0:T(8,128)(2,1)}, u32[]{:S(2)}, u32[]{:S(2)}) collective-permute-start(bf16[128,2048]{1,0:T(8,128)(2,1)S(1)} %copy-done.10), channel_id=1, source_target_pairs={{0,8},{8,0},{16,24},{24,16},{32,40},{40,32},{48,56},{56,48},{64,72... | collective-permute-start | bytes 1572872 | tf_op jit(solution)/shard_map/ppermute | solution.py:218
  157.4 34.0 %collective-permute-start.38 = (bf16[2,704,256]{2,1,0:T(8,128)(2,1)}, bf16[2,704,256]{2,1,0:T(8,128)(2,1)}, u32[]{:S(2)}, u32[]{:S(2)}) collective-permute-start(bf16[2,704,256]{2,1,0:T(8,128)(2,1)} %get-tuple-element.26), channel_id=1, source_target_pairs={{0,2},{1,3},{2,0},{3,1},{4,6},{5,7},{6,4},{7,5},{8,10},{9,11},{10,... | collective-permute-start | bytes 2162696 | tf_op jit(solution)/shard_map/ppermute | solution.py:340
  159.5 34.5 %collective-permute-start.39 = (bf16[2,704,256]{2,1,0:T(8,128)(2,1)}, bf16[2,704,256]{2,1,0:T(8,128)(2,1)}, u32[]{:S(2)}, u32[]{:S(2)}) collective-permute-start(bf16[2,704,256]{2,1,0:T(8,128)(2,1)} %get-tuple-element.36), channel_id=1, source_target_pairs={{0,1},{1,2},{2,3},{3,0},{4,5},{5,6},{6,7},{7,4},{8,9},{9,10},{10,1... | collective-permute-start | bytes 2162696 | tf_op jit(solution)/shard_map/ppermute | solution.py:340
  176.1 55.3 %collective-permute-start.34 = (bf16[4,704,256]{2,1,0:T(8,128)(2,1)}, bf16[4,704,256]{2,1,0:T(8,128)(2,1)S(1)}, u32[]{:S(2)}, u32[]{:S(2)}) collective-permute-start(bf16[4,704,256]{2,1,0:T(8,128)(2,1)} %get-tuple-element.34), channel_id=1, source_target_pairs={{0,4},{1,5},{2,6},{3,7},{4,0},{5,1},{6,2},{7,3},{8,12},{9,13},{10,... | collective-permute-start | bytes 4325384 | tf_op jit(solution)/shard_map/ppermute | solution.py:348
  179.7 20.2 %collective-permute-start.40 = (bf16[2,704,256]{2,1,0:T(8,128)(2,1)}, bf16[2,704,256]{2,1,0:T(8,128)(2,1)}, u32[]{:S(2)}, u32[]{:S(2)}) collective-permute-start(bf16[2,704,256]{2,1,0:T(8,128)(2,1)} %get-tuple-element.37), channel_id=1, source_target_pairs={{0,3},{1,0},{2,1},{3,2},{4,7},{5,4},{6,5},{7,6},{8,11},{9,8},{10,9... | collective-permute-start | bytes 2162696 | tf_op jit(solution)/shard_map/ppermute | solution.py:340
  189.9 26.1 %collective-permute-start.30 = (bf16[2,704,256]{2,1,0:T(8,128)(2,1)}, bf16[2,704,256]{2,1,0:T(8,128)(2,1)}, u32[]{:S(2)}, u32[]{:S(2)}) collective-permute-start(bf16[2,704,256]{2,1,0:T(8,128)(2,1)} %get-tuple-element.30), channel_id=1, source_target_pairs={{0,2},{1,3},{2,0},{3,1},{4,6},{5,7},{6,4},{7,5},{8,10},{9,11},{10,... | collective-permute-start | bytes 2162696 | tf_op jit(solution)/shard_map/ppermute | solution.py:340
  191.4 32.7 %collective-permute-start.31 = (bf16[2,704,256]{2,1,0:T(8,128)(2,1)}, bf16[2,704,256]{2,1,0:T(8,128)(2,1)}, u32[]{:S(2)}, u32[]{:S(2)}) collective-permute-start(bf16[2,704,256]{2,1,0:T(8,128)(2,1)} %get-tuple-element.31), channel_id=1, source_target_pairs={{0,1},{1,2},{2,3},{3,0},{4,5},{5,6},{6,7},{7,4},{8,9},{9,10},{10,1... | collective-permute-start | bytes 2162696 | tf_op jit(solution)/shard_map/ppermute | solution.py:340
  194.0 34.7 %collective-permute-start.32 = (bf16[2,704,256]{2,1,0:T(8,128)(2,1)}, bf16[2,704,256]{2,1,0:T(8,128)(2,1)}, u32[]{:S(2)}, u32[]{:S(2)}) collective-permute-start(bf16[2,704,256]{2,1,0:T(8,128)(2,1)} %get-tuple-element.32), channel_id=1, source_target_pairs={{0,3},{1,0},{2,1},{3,2},{4,7},{5,4},{6,5},{7,6},{8,11},{9,8},{10,9... | collective-permute-start | bytes 2162696 | tf_op jit(solution)/shard_map/ppermute | solution.py:340
  201.4 36.8 %collective-permute-start.41 = (bf16[704,256]{1,0:T(8,128)(2,1)S(1)}, bf16[704,256]{1,0:T(8,128)(2,1)S(1)}, u32[]{:S(2)}, u32[]{:S(2)}) collective-permute-start(bf16[704,256]{1,0:T(8,128)(2,1)S(1)} %fusion.20), channel_id=1, source_target_pairs={{0,4},{1,5},{2,6},{3,7},{4,0},{5,1},{6,2},{7,3},{8,12},{9,13},{10,... | collective-permute-start | bytes 1081352 | tf_op jit(solution)/shard_map/ppermute | solution.py:343
  (40 other events, 655.8 us)

commit v3 on v2

--- a/solution.py
+++ b/solution.py
@@ -196,7 +196,7 @@
 Y_DOWN = chip_moves(lambda y, z, core: (y - 1, z, core))
 Z_SWAP = chip_moves(lambda y, z, core: (y, z + 1, core))
 CORE_SWAP = chip_moves(lambda y, z, core: (y, z, core + 1))
-PIECE_STEPS = ((0, 0), (0, 1), (-1, 0), (1, 0), (-1, 1), (1, 1), (-2, 0), (2, 1))
+PIECE_STEPS = ((0, 0), (0, 1), (-1, 0), (1, 0), (-1, 1), (-2, 0), (1, 1), (2, 1))
 LATE = 2
 
 
@@ -393,20 +393,20 @@
         return pick_rows(onehot[early:], slot_coef[early:], mine + others, scaled, buffer, first)
 
     beside, below, above = (pass_on(tokens_here, move) for move in (Z_SWAP, Y_UP, Y_DOWN))
-    below_beside = pass_on(beside, Y_UP)
+    below_beside, far = pass_on(below, Z_SWAP), pass_on(below, Y_UP)
     above_beside = pass_on(beside, Y_DOWN)
-    far, far_beside = pass_on(below, Y_UP), pass_on(above_beside, Y_DOWN)
-    near_rows = [tokens_here, beside, below, above, below_beside, above_beside]
+    far_beside = pass_on(above_beside, Y_DOWN)
+    near_rows = [tokens_here, beside, below, above, below_beside, far]
     near_others = [pass_on(piece, CORE_SWAP) for piece in near_rows]
-    far_rows = [far, far_beside]
+    far_rows = [above_beside, far_beside]
     far_others = [pass_on(piece, CORE_SWAP) for piece in far_rows]
 
     packed = pack_rows(query_rows[0], key_rows[0], value_rows[0], grads_here, out_weight)
 
     g_beside, g_below, g_above = (pass_on(grads_here, move) for move in (Z_SWAP, Y_UP, Y_DOWN))
-    g_below_beside, g_above_beside = pass_on(g_beside, Y_UP), pass_on(g_beside, Y_DOWN)
-    g_far = pass_on(g_below, Y_UP)
-    g_far_beside = pass_on(g_above_beside, Y_DOWN)
+    g_below_beside, g_far = pass_on(g_below, Z_SWAP), pass_on(g_below, Y_UP)
+    g_above_beside = pass_on(g_beside, Y_DOWN)
+    g_far_beside = pass_on(g_below_beside, Y_UP)
     buffer = early_pick(near_rows, near_others, False)
     rows_in = late_pick(far_rows, far_others, False, buffer)
     gate_pre = lax.optimization_barrier(dot_nn(rows_in, gate_weight[0]))
@@ -415,10 +415,10 @@
     up_pre = dot_nn(rows_in, up_weight[0])
     hidden = (gate_act * up_pre).astype(jnp.bfloat16)
     up_pre, hidden = lax.optimization_barrier((up_pre, hidden))
-    g_near = [grads_here, g_beside, g_below, g_above, g_below_beside, g_above_beside]
+    g_near = [grads_here, g_beside, g_below, g_above, g_below_beside, g_far]
     g_near_others = [pass_on(piece, CORE_SWAP) for piece in g_near]
     g_buffer = early_pick(g_near, g_near_others, True)
-    g_fars = [g_far, g_far_beside]
+    g_fars = [g_above_beside, g_far_beside]
     g_far_others = [pass_on(piece, CORE_SWAP) for piece in g_fars]
     grads_in = late_pick(g_fars, g_far_others, True, g_buffer)
 

time: 255 us -> 252 us (0.988)
  waiting for transfers between devices: 101 us -> 91.3 us
  starting transfers between devices: 52.7 us -> 58.7 us
    ppermute x30, waiting for transfers between devices: 62.4 us -> 52.6 us  [pass_on(): return lax.ppermute(value, 'ctx', move)]
    ppermute x30, starting transfers between devices: 20.4 us -> 25.6 us  [pass_on(): return lax.ppermute(value, 'ctx', move)]
  transfers between devices with their start and end apart: 45 -> 45, of which waited for: 16 -> 14; matrix products, arithmetic and copies ran while one was open for 14% -> 14% of each run, Pallas kernels for 23% -> 24%
where the time goes in v3:
time: 252 us; the launch traced here: 249 us
  waiting for transfers between devices  91.3 us (36%)
  Pallas kernels  59.1 us (23%)
  starting transfers between devices  58.7 us (23%)
  matrix products  19.3 us (8%)
  other arithmetic  13.5 us (5%)
  local copies, waits for them, and re-layouts  6.44 us (3%)
    ppermute x30, waiting for transfers between devices, pass_on(): return lax.ppermute(value, 'ctx', move)  52.6 us
    ppermute x6, waiting for transfers between devices, sum_x_first(): lax.ppermute(term, 'dp', move)  30.5 us
    ppermute x30, starting transfers between devices, pass_on(): return lax.ppermute(value, 'ctx', move)  25.6 us
    pallas_call x3, Pallas kernels, weight_terms(): pl.pallas_call(lambda *refs: term_kernel(per_step, homes, *refs), grid_sp...  24.7 us
    dot_general x3, matrix products, dot_nn(): lax.dot_general(a, b, (((1,), (0,)), ((), ())), preferred_element_type=jn...  19.3 us
    pallas_call x4, Pallas kernels, pick_rows(): pl.pallas_call(lambda *refs: pick_kernel(count, scaled, *refs), grid=(wid...  15.4 us
    pallas_call x1, Pallas kernels, attention_rows(): pl.pallas_call(attention_kernel, in_specs=[smem, smem, smem, vmem], out_s...  11.3 us
    ppermute x6, starting transfers between devices, sum_x_first(): lax.ppermute(term, 'dp', move)  8.26 us
  transfers between devices with their start and end apart: 45, of which 14 were waited for; matrix products, arithmetic and copies ran while one was open for 14% of the time, Pallas kernels for 24%

profile of v3, /device:TPU:2, one launch (start us, length us, event | category | flops | bytes accessed | tf_op | source)
XLA Modules:
  0.0 249.5 jit_solution(12255022314229266620)
XLA Ops:
  6.2 10.7 %collective-permute-done.2.refs_4_ = bf16[128,2048]{1,0:T(8,128)(2,1)S(1)} collective-permute-done((bf16[128,2048]{1,0:T(8,128)(2,1)}, bf16[128,2048]{1,0:T(8,128)(2,1)S(1)}, u32[]{:S(2)}, u32[]{:S(2)}) %collective-permute-start.2) | collective-permute-done | bytes 524320 | tf_op jit(solution)/shard_map/ppermute | solution.py:218
  22.7 3.5 %all-to-all-start.2 = ((f32[16,1,128]{2,1,0:T(1,128)}), f32[16,1,128]{2,1,0:T(1,128)S(1)}, u32[]{:S(2)}, u32[]{:S(2)}) async-start(f32[16,1,128]{2,1,0:T(1,128)} %bitcast.18), calls=%async_computation.2 | async-start | bytes 16384 | tf_op jit(solution)/shard_map/all_to_all | solution.py:378
  31.2 5.4 %pack_rows.1 = bf16[16,384,128]{2,1,0:T(8,128)(2,1)} custom-call(bf16[128,1024]{1,0:T(8,128)(2,1)} %bitcast.126, bf16[128,1024]{1,0:T(8,128)(2,1)} %bitcast.127, bf16[128,1024]{1,0:T(8,128)(2,1)} %bitcast.128, bf16[128,2048]{1,0:T(8,128)(2,1)} %bitcast.117, bf16[1024,2048]{1,0:T(8,128)(2,1)} %w_ref.1), custom_call_target="tpu_custom_call" | custom-call | flops 536870912 | bytes 7000000 | tf_op jit(solution)/shard_map/pack_rows/pallas_call | solution.py:47
  38.6 5.0 %all-to-all-start = ((bf16[16,384,128]{2,1,0:T(8,128)(2,1)}), bf16[16,384,128]{2,1,0:T(8,128)(2,1)}, u32[]{:S(2)}, u32[]{:S(2)}) async-start(bf16[16,384,128]{2,1,0:T(8,128)(2,1)} %pack_rows.1), calls=%async_computation | async-start | bytes 3145728 | tf_op jit(solution)/shard_map/all_to_all | solution.py:428
  52.7 22.7 %collective-permute-done.1.refs_2_ = bf16[128,2048]{1,0:T(8,128)(2,1)S(1)} collective-permute-done((bf16[128,2048]{1,0:T(8,128)(2,1)}, bf16[128,2048]{1,0:T(8,128)(2,1)S(1)}, u32[]{:S(2)}, u32[]{:S(2)}) %collective-permute-start.1) | collective-permute-done | bytes 524320 | tf_op jit(solution)/shard_map/ppermute | solution.py:218
  77.2 9.0 %collective-permute-done.16.refs_2_ = bf16[128,2048]{1,0:T(8,128)(2,1)} collective-permute-done((bf16[128,2048]{1,0:T(8,128)(2,1)}, bf16[128,2048]{1,0:T(8,128)(2,1)}, u32[]{:S(2)}, u32[]{:S(2)}) %collective-permute-start.16) | collective-permute-done | bytes 524320 | tf_op jit(solution)/shard_map/ppermute | solution.py:218
  90.7 9.1 %collective-permute-done.17.refs_3_ = bf16[128,2048]{1,0:T(8,128)(2,1)} collective-permute-done((bf16[128,2048]{1,0:T(8,128)(2,1)}, bf16[128,2048]{1,0:T(8,128)(2,1)}, u32[]{:S(2)}, u32[]{:S(2)}) %collective-permute-start.17) | collective-permute-done | bytes 524320 | tf_op jit(solution)/shard_map/ppermute | solution.py:218
  101.3 11.3 %attention_rows.1 = bf16[16,320,128]{2,1,0:T(8,128)(2,1)} custom-call(s32[64]{0:T(128)} %reshape.703.lists_ref, s32[16]{0:T(128)} %bitcast.131, s32[1]{0:T(128)} %bitcast.1.half_ref, bf16[16,384,128]{2,1,0:T(8,128)(2,1)} %all-to-all-done.rows_ref), custom_call_target="tpu_custom_call" | custom-call | bytes 3000000 | tf_op jit(solution)/shard_map/attention_rows/pallas_call | solution.py:142
  112.7 5.6 %all-to-all-start.1 = ((bf16[16,320,128]{2,1,0:T(8,128)(2,1)}), bf16[16,320,128]{2,1,0:T(8,128)(2,1)}, u32[]{:S(2)}, u32[]{:S(2)}) async-start(bf16[16,320,128]{2,1,0:T(8,128)(2,1)} %attention_rows.1), calls=%async_computation.1 | async-start | bytes 2621440 | tf_op jit(solution)/shard_map/all_to_all | solution.py:441
  118.3 4.9 %pick_rows.4.refs_6_ = bf16[1024,2048]{1,0:T(8,128)(2,1)} custom-call(bf16[12,64,128]{2,1,0:T(8,128)(2,1)} %pad_maximum_fusion.1.refs_0_, f32[12,64,1]{2,1,0:T(8,128)} %pad_maximum_fusion.refs_1_, bf16[128,2048]{1,0:T(8,128)(2,1)} %bitcast.118, bf16[128,2048]{1,0:T(8,128)(2,1)} %collective-permute-done.refs_3_, bf16[128,2048]{1,0:T(8,128)(2,1)} %copy-done.8, ...), custom_call_target="tpu_custom_call" | custom-call | flops 402653184 | bytes 9437184 | tf_op jit(solution)/shard_map/pick_rows/pallas_call | solution.py:256
  123.8 4.8 %pick_rows.6.refs_6_ = bf16[1024,2048]{1,0:T(8,128)(2,1)} custom-call(bf16[12,64,128]{2,1,0:T(8,128)(2,1)} %pad_maximum_fusion.1.refs_0_, f32[12,64,1]{2,1,0:T(8,128)} %pad_maximum_fusion.refs_1_, bf16[128,2048]{1,0:T(8,128)(2,1)} %bitcast.125, bf16[128,2048]{1,0:T(8,128)(2,1)} %collective-permute-done.15.refs_3_, ...), custom_call_target="tpu_custom_call" | custom-call | flops 402653184 | bytes 9437184 | tf_op jit(solution)/shard_map/pick_rows/pallas_call | solution.py:256
  131.5 6.0 %fusion.2 = f32[1024,704]{0,1:T(8,128)S(1)} fusion(bf16[1024,2048]{1,0:T(8,128)(2,1)} %pick_rows.7.refs_2_.refs_3_.refs_4_.refs_5_, bf16[1,2048,704]{1,2,0:T(8,128)(2,1)} %param.23), kind=kOutput, calls=%fused_computation.3 | convolution fusion | flops 2952790016 | bytes 9961472 | tf_op jit(solution)/shard_map/dot_general | solution.py:25
  137.5 4.9 %multiply_convert_fusion.2 = (bf16[1024,704]{0,1:T(8,128)(2,1)}, f32[1024,704]{0,1:T(8,128)}) fusion(f32[1024,704]{0,1:T(8,128)S(1)} %fusion.2, bf16[1024,2048]{1,0:T(8,128)(2,1)S(1)} %copy-done.2, bf16[1,2048,704]{1,2,0:T(8,128)(2,1)S(1)} %copy-done), kind=kOutput, calls=%fused_computation.9 | convolution fusion | flops 2957115392 | bytes 14286848 | tf_op jit(solution)/shard_map/dot_general | solution.py:25
  145.3 8.3 %weight_terms.3 = (bf16[2,704,256]{2,1,0:T(8,128)(2,1)}, bf16[2,704,256]{2,1,0:T(8,128)(2,1)}, bf16[2,704,256]{2,1,0:T(8,128)(2,1)}, bf16[2,704,256]{2,1,0:T(8,128)(2,1)}) custom-call(s32[8]{0:T(128)} %stack.97.refs_0_, bf16[704,1024]{1,0:T(8,128)(2,1)} %bitcast.119, bf16[1024,2048]{1,0:T(8,128)(2,1)} %pick_rows.5.refs_2_.refs_3_.refs_4_.refs_5_, ...), custom_call_target="tpu_custom_call" | custom-call | bytes 1000000 | tf_op jit(solution)/shard_map/weight_terms/pallas_call | solution.py:299
  155.7 8.4 %fusion.7 = (bf16[704,1024]{1,0:T(8,128)(2,1)}, bf16[704,1024]{1,0:T(8,128)(2,1)}) fusion(f32[1024,704]{0,1:T(8,128)} %copy-done.17, f32[1024,704]{0,1:T(8,128)} %get-tuple-element.28, bf16[1024,2048]{1,0:T(8,128)(2,1)} %pick_rows.5.refs_2_.refs_3_.refs_4_.refs_5_, bf16[1,2048,704]{1,2,0:T(8,128)(2,1)S(1)} %copy-done.16), kind=kOutput, calls=%fused_computation.12 | convolution fusion | flops 2962161664 | bytes 15728640 | tf_op jit(solution)/shard_map/dot_general | solution.py:25
  164.1 8.2 %weight_terms.5 = (bf16[4,704,256]{2,1,0:T(8,128)(2,1)}, bf16[4,704,256]{2,1,0:T(8,128)(2,1)}) custom-call(s32[8]{0:T(128)} %stack.115.refs_0_, bf16[704,1024]{1,0:T(8,128)(2,1)} %get-tuple-element.40.refs_1_, bf16[1024,2048]{1,0:T(8,128)(2,1)} %pick_rows.7.refs_2_.refs_3_.refs_4_.refs_5_, bf16[1024,2048]{1,0:T(8,128)(2,1)} %pick_rows.7.refs_2_.refs_3_.refs_4_.refs_5_, ...), custom_call_target="tpu_custom_call" | custom-call | bytes 1000000 | tf_op jit(solution)/shard_map/weight_terms/pallas_call | solution.py:299
  172.3 3.6 %collective-permute-start.34 = (bf16[4,704,256]{2,1,0:T(8,128)(2,1)}, bf16[4,704,256]{2,1,0:T(8,128)(2,1)S(1)}, u32[]{:S(2)}, u32[]{:S(2)}) collective-permute-start(bf16[4,704,256]{2,1,0:T(8,128)(2,1)} %get-tuple-element.34), channel_id=1, source_target_pairs={{0,4},{1,5},{2,6},{3,7},{4,0},{5,1},{6,2},{7,3},{8,12},{9,13},{10,... | collective-permute-start | bytes 4325384 | tf_op jit(solution)/shard_map/ppermute | solution.py:348
  177.9 8.2 %weight_terms.4 = (bf16[2,704,256]{2,1,0:T(8,128)(2,1)}, bf16[2,704,256]{2,1,0:T(8,128)(2,1)}, bf16[2,704,256]{2,1,0:T(8,128)(2,1)}, bf16[2,704,256]{2,1,0:T(8,128)(2,1)}) custom-call(s32[8]{0:T(128)} %stack.97.refs_0_, bf16[704,1024]{1,0:T(8,128)(2,1)} %get-tuple-element.41.refs_1_, bf16[1024,2048]{1,0:T(8,128)(2,1)} %pick_rows.7.refs_2_.refs_3_.refs_4_.refs_5_, ...), custom_call_target="tpu_custom_call" | custom-call | bytes 1000000 | tf_op jit(solution)/shard_map/weight_terms/pallas_call | solution.py:299
  192.5 3.5 %collective-permute-done.40 = bf16[2,704,256]{2,1,0:T(8,128)(2,1)} collective-permute-done((bf16[2,704,256]{2,1,0:T(8,128)(2,1)}, bf16[2,704,256]{2,1,0:T(8,128)(2,1)}, u32[]{:S(2)}, u32[]{:S(2)}) %collective-permute-start.40) | collective-permute-done | bytes 720928 | tf_op jit(solution)/shard_map/ppermute | solution.py:340
  198.0 14.2 %collective-permute-done.30 = bf16[2,704,256]{2,1,0:T(8,128)(2,1)} collective-permute-done((bf16[2,704,256]{2,1,0:T(8,128)(2,1)}, bf16[2,704,256]{2,1,0:T(8,128)(2,1)}, u32[]{:S(2)}, u32[]{:S(2)}) %collective-permute-start.30) | collective-permute-done | bytes 720928 | tf_op jit(solution)/shard_map/ppermute | solution.py:340
  212.2 8.1 %collective-permute-done.31 = bf16[2,704,256]{2,1,0:T(8,128)(2,1)} collective-permute-done((bf16[2,704,256]{2,1,0:T(8,128)(2,1)}, bf16[2,704,256]{2,1,0:T(8,128)(2,1)}, u32[]{:S(2)}, u32[]{:S(2)}) %collective-permute-start.31) | collective-permute-done | bytes 720928 | tf_op jit(solution)/shard_map/ppermute | solution.py:340
  220.3 4.6 %collective-permute-done.32 = bf16[2,704,256]{2,1,0:T(8,128)(2,1)} collective-permute-done((bf16[2,704,256]{2,1,0:T(8,128)(2,1)}, bf16[2,704,256]{2,1,0:T(8,128)(2,1)}, u32[]{:S(2)}, u32[]{:S(2)}) %collective-permute-start.32) | collective-permute-done | bytes 720928 | tf_op jit(solution)/shard_map/ppermute | solution.py:340
  228.7 3.6 %collective-permute-start.35 = (bf16[704,256]{1,0:T(8,128)(2,1)S(1)}, bf16[704,256]{1,0:T(8,128)(2,1)S(1)}, u32[]{:S(2)}, u32[]{:S(2)}) collective-permute-start(bf16[704,256]{1,0:T(8,128)(2,1)S(1)} %get-tuple-element.42), channel_id=1, source_target_pairs={{0,2},{1,3},{2,0},{3,1},{4,6},{5,7},{6,4},{7,5},{8,10},{9,11},{10,... | collective-permute-start | bytes 1081352 | tf_op jit(solution)/shard_map/ppermute | solution.py:350
  241.6 5.4 %collective-permute-done.36 = bf16[704,256]{1,0:T(8,128)(2,1)S(1)} collective-permute-done((bf16[704,256]{1,0:T(8,128)(2,1)S(1)}, bf16[704,256]{1,0:T(8,128)(2,1)S(1)}, u32[]{:S(2)}, u32[]{:S(2)}) %collective-permute-start.36) | collective-permute-done | bytes 360480 | tf_op jit(solution)/shard_map/ppermute | solution.py:350
  (148 shorter events, 69.4 us)
Async XLA Ops:
  5.9 20.6 %collective-permute-start.9 = (bf16[128,2048]{1,0:T(8,128)(2,1)}, bf16[128,2048]{1,0:T(8,128)(2,1)}, u32[]{:S(2)}, u32[]{:S(2)}) collective-permute-start(bf16[128,2048]{1,0:T(8,128)(2,1)} %bitcast.116), channel_id=1, source_target_pairs={{0,8},{8,0},{16,24},{24,16},{32,40},{40,32},{48,56},{56,48},{64,72... | collective-permute-start | bytes 1572872 | tf_op jit(solution)/shard_map/ppermute | solution.py:218
  5.9 22.3 %collective-permute-start.20 = (bf16[128,2048]{1,0:T(8,128)(2,1)}, bf16[128,2048]{1,0:T(8,128)(2,1)}, u32[]{:S(2)}, u32[]{:S(2)}) collective-permute-start(bf16[128,2048]{1,0:T(8,128)(2,1)} %bitcast.121), channel_id=1, source_target_pairs={{0,32},{8,40},{16,48},{24,56},{32,64},{40,72},{48,80},{56,88},{64,... | collective-permute-start | bytes 1572872 | tf_op jit(solution)/shard_map/ppermute | solution.py:218
  28.2 19.4 %collective-permute-start.8 = (bf16[128,2048]{1,0:T(8,128)(2,1)}, bf16[128,2048]{1,0:T(8,128)(2,1)}, u32[]{:S(2)}, u32[]{:S(2)}) collective-permute-start(bf16[128,2048]{1,0:T(8,128)(2,1)} %copy-done.8), channel_id=1, source_target_pairs={{0,32},{8,40},{16,48},{24,56},{32,64},{40,72},{48,80},{56,88},{64,... | collective-permute-start | bytes 1572872 | tf_op jit(solution)/shard_map/ppermute | solution.py:218
  29.7 19.4 %collective-permute-start.11 = (bf16[128,2048]{1,0:T(8,128)(2,1)}, bf16[128,2048]{1,0:T(8,128)(2,1)}, u32[]{:S(2)}, u32[]{:S(2)}) collective-permute-start(bf16[128,2048]{1,0:T(8,128)(2,1)} %copy-done.8), channel_id=1, source_target_pairs={{0,8},{8,0},{16,24},{24,16},{32,40},{40,32},{48,56},{56,48},{64,72... | collective-permute-start | bytes 1572872 | tf_op jit(solution)/shard_map/ppermute | solution.py:218
  38.6 62.7 %all-to-all-start = ((bf16[16,384,128]{2,1,0:T(8,128)(2,1)}), bf16[16,384,128]{2,1,0:T(8,128)(2,1)}, u32[]{:S(2)}, u32[]{:S(2)}) async-start(bf16[16,384,128]{2,1,0:T(8,128)(2,1)} %pack_rows.1), calls=%async_computation | async-start | bytes 3145728 | tf_op jit(solution)/shard_map/all_to_all | solution.py:428
  44.4 30.9 %collective-permute-start.1 = (bf16[128,2048]{1,0:T(8,128)(2,1)}, bf16[128,2048]{1,0:T(8,128)(2,1)S(1)}, u32[]{:S(2)}, u32[]{:S(2)}) collective-permute-start(bf16[128,2048]{1,0:T(8,128)(2,1)} %collective-permute-done.refs_3_), channel_id=1, source_target_pairs={{0,96},{8,104},{16,112},{24,120},{32,0},{40,8},{48,16},{56,24},{64... | collective-permute-start | bytes 1572872 | tf_op jit(solution)/shard_map/ppermute | solution.py:218
  47.6 27.8 %collective-permute-start.22 = (bf16[128,2048]{1,0:T(8,128)(2,1)}, bf16[128,2048]{1,0:T(8,128)(2,1)}, u32[]{:S(2)}, u32[]{:S(2)}) collective-permute-start(bf16[128,2048]{1,0:T(8,128)(2,1)} %collective-permute-done.20.refs_4_), channel_id=1, source_target_pairs={{0,16},{8,24},{16,0},{24,8},{32,48},{40,56},{48,32},{56,40},{64,80... | collective-permute-start | bytes 1572872 | tf_op jit(solution)/shard_map/ppermute | solution.py:218
  49.0 27.0 %collective-permute-start.23 = (bf16[128,2048]{1,0:T(8,128)(2,1)}, bf16[128,2048]{1,0:T(8,128)(2,1)}, u32[]{:S(2)}, u32[]{:S(2)}) collective-permute-start(bf16[128,2048]{1,0:T(8,128)(2,1)} %collective-permute-done.20.refs_4_), channel_id=1, source_target_pairs={{0,32},{8,40},{16,48},{24,56},{32,64},{40,72},{48,80},{56,88},{64,... | collective-permute-start | bytes 1572872 | tf_op jit(solution)/shard_map/ppermute | solution.py:218
  49.0 27.6 %collective-permute-start.26 = (bf16[128,2048]{1,0:T(8,128)(2,1)}, bf16[128,2048]{1,0:T(8,128)(2,1)S(1)}, u32[]{:S(2)}, u32[]{:S(2)}) collective-permute-start(bf16[128,2048]{1,0:T(8,128)(2,1)} %collective-permute-done.20.refs_4_), channel_id=1, source_target_pairs={{0,8},{8,0},{16,24},{24,16},{32,40},{40,32},{48,56},{56,48},{64,72... | collective-permute-start | bytes 1572872 | tf_op jit(solution)/shard_map/ppermute | solution.py:218
  49.2 37.0 %collective-permute-start.16 = (bf16[128,2048]{1,0:T(8,128)(2,1)}, bf16[128,2048]{1,0:T(8,128)(2,1)}, u32[]{:S(2)}, u32[]{:S(2)}) collective-permute-start(bf16[128,2048]{1,0:T(8,128)(2,1)} %collective-permute-done.15.refs_3_), channel_id=1, source_target_pairs={{0,96},{8,104},{16,112},{24,120},{32,0},{40,8},{48,16},{56,24},{64... | collective-permute-start | bytes 1572872 | tf_op jit(solution)/shard_map/ppermute | solution.py:218
  88.2 35.0 %collective-permute-start.4 = (bf16[128,2048]{1,0:T(8,128)(2,1)}, bf16[128,2048]{1,0:T(8,128)(2,1)}, u32[]{:S(2)}, u32[]{:S(2)}) collective-permute-start(bf16[128,2048]{1,0:T(8,128)(2,1)} %collective-permute-done.3.refs_6_), channel_id=1, source_target_pairs={{0,32},{8,40},{16,48},{24,56},{32,64},{40,72},{48,80},{56,88},{64,... | collective-permute-start | bytes 1572872 | tf_op jit(solution)/shard_map/ppermute | solution.py:218
  88.3 35.4 %collective-permute-start.28 = (bf16[128,2048]{1,0:T(8,128)(2,1)}, bf16[128,2048]{1,0:T(8,128)(2,1)}, u32[]{:S(2)}, u32[]{:S(2)}) collective-permute-start(bf16[128,2048]{1,0:T(8,128)(2,1)} %collective-permute-done.22.refs_6_), channel_id=1, source_target_pairs={{0,8},{8,0},{16,24},{24,16},{32,40},{40,32},{48,56},{56,48},{64,72... | collective-permute-start | bytes 1572872 | tf_op jit(solution)/shard_map/ppermute | solution.py:218
  88.4 35.4 %collective-permute-start.29 = (bf16[128,2048]{1,0:T(8,128)(2,1)}, bf16[128,2048]{1,0:T(8,128)(2,1)}, u32[]{:S(2)}, u32[]{:S(2)}) collective-permute-start(bf16[128,2048]{1,0:T(8,128)(2,1)} %collective-permute-done.23.refs_7_), channel_id=1, source_target_pairs={{0,8},{8,0},{16,24},{24,16},{32,40},{40,32},{48,56},{56,48},{64,72... | collective-permute-start | bytes 1572872 | tf_op jit(solution)/shard_map/ppermute | solution.py:218
  90.4 38.3 %collective-permute-start.18 = (bf16[128,2048]{1,0:T(8,128)(2,1)}, bf16[128,2048]{1,0:T(8,128)(2,1)}, u32[]{:S(2)}, u32[]{:S(2)}) collective-permute-start(bf16[128,2048]{1,0:T(8,128)(2,1)} %collective-permute-done.16.refs_2_), channel_id=1, source_target_pairs={{0,8},{8,0},{16,24},{24,16},{32,40},{40,32},{48,56},{56,48},{64,72... | collective-permute-start | bytes 1572872 | tf_op jit(solution)/shard_map/ppermute | solution.py:218
  99.8 28.8 %collective-permute-start.19 = (bf16[128,2048]{1,0:T(8,128)(2,1)}, bf16[128,2048]{1,0:T(8,128)(2,1)}, u32[]{:S(2)}, u32[]{:S(2)}) collective-permute-start(bf16[128,2048]{1,0:T(8,128)(2,1)} %collective-permute-done.17.refs_3_), channel_id=1, source_target_pairs={{0,8},{8,0},{16,24},{24,16},{32,40},{40,32},{48,56},{56,48},{64,72... | collective-permute-start | bytes 1572872 | tf_op jit(solution)/shard_map/ppermute | solution.py:218
  112.7 77.5 %all-to-all-start.1 = ((bf16[16,320,128]{2,1,0:T(8,128)(2,1)}), bf16[16,320,128]{2,1,0:T(8,128)(2,1)}, u32[]{:S(2)}, u32[]{:S(2)}) async-start(bf16[16,320,128]{2,1,0:T(8,128)(2,1)} %attention_rows.1), calls=%async_computation.1 | async-start | bytes 2621440 | tf_op jit(solution)/shard_map/all_to_all | solution.py:441
  153.6 33.9 %collective-permute-start.38 = (bf16[2,704,256]{2,1,0:T(8,128)(2,1)}, bf16[2,704,256]{2,1,0:T(8,128)(2,1)}, u32[]{:S(2)}, u32[]{:S(2)}) collective-permute-start(bf16[2,704,256]{2,1,0:T(8,128)(2,1)} %get-tuple-element.26), channel_id=1, source_target_pairs={{0,2},{1,3},{2,0},{3,1},{4,6},{5,7},{6,4},{7,5},{8,10},{9,11},{10,... | collective-permute-start | bytes 2162696 | tf_op jit(solution)/shard_map/ppermute | solution.py:340
  155.7 34.4 %collective-permute-start.39 = (bf16[2,704,256]{2,1,0:T(8,128)(2,1)}, bf16[2,704,256]{2,1,0:T(8,128)(2,1)}, u32[]{:S(2)}, u32[]{:S(2)}) collective-permute-start(bf16[2,704,256]{2,1,0:T(8,128)(2,1)} %get-tuple-element.36), channel_id=1, source_target_pairs={{0,1},{1,2},{2,3},{3,0},{4,5},{5,6},{6,7},{7,4},{8,9},{9,10},{10,1... | collective-permute-start | bytes 2162696 | tf_op jit(solution)/shard_map/ppermute | solution.py:340
  172.3 55.3 %collective-permute-start.34 = (bf16[4,704,256]{2,1,0:T(8,128)(2,1)}, bf16[4,704,256]{2,1,0:T(8,128)(2,1)S(1)}, u32[]{:S(2)}, u32[]{:S(2)}) collective-permute-start(bf16[4,704,256]{2,1,0:T(8,128)(2,1)} %get-tuple-element.34), channel_id=1, source_target_pairs={{0,4},{1,5},{2,6},{3,7},{4,0},{5,1},{6,2},{7,3},{8,12},{9,13},{10,... | collective-permute-start | bytes 4325384 | tf_op jit(solution)/shard_map/ppermute | solution.py:348
  175.9 20.2 %collective-permute-start.40 = (bf16[2,704,256]{2,1,0:T(8,128)(2,1)}, bf16[2,704,256]{2,1,0:T(8,128)(2,1)}, u32[]{:S(2)}, u32[]{:S(2)}) collective-permute-start(bf16[2,704,256]{2,1,0:T(8,128)(2,1)} %get-tuple-element.37), channel_id=1, source_target_pairs={{0,3},{1,0},{2,1},{3,2},{4,7},{5,4},{6,5},{7,6},{8,11},{9,8},{10,9... | collective-permute-start | bytes 2162696 | tf_op jit(solution)/shard_map/ppermute | solution.py:340
  186.1 26.1 %collective-permute-start.30 = (bf16[2,704,256]{2,1,0:T(8,128)(2,1)}, bf16[2,704,256]{2,1,0:T(8,128)(2,1)}, u32[]{:S(2)}, u32[]{:S(2)}) collective-permute-start(bf16[2,704,256]{2,1,0:T(8,128)(2,1)} %get-tuple-element.30), channel_id=1, source_target_pairs={{0,2},{1,3},{2,0},{3,1},{4,6},{5,7},{6,4},{7,5},{8,10},{9,11},{10,... | collective-permute-start | bytes 2162696 | tf_op jit(solution)/shard_map/ppermute | solution.py:340
  187.5 32.8 %collective-permute-start.31 = (bf16[2,704,256]{2,1,0:T(8,128)(2,1)}, bf16[2,704,256]{2,1,0:T(8,128)(2,1)}, u32[]{:S(2)}, u32[]{:S(2)}) collective-permute-start(bf16[2,704,256]{2,1,0:T(8,128)(2,1)} %get-tuple-element.31), channel_id=1, source_target_pairs={{0,1},{1,2},{2,3},{3,0},{4,5},{5,6},{6,7},{7,4},{8,9},{9,10},{10,1... | collective-permute-start | bytes 2162696 | tf_op jit(solution)/shard_map/ppermute | solution.py:340
  190.2 34.7 %collective-permute-start.32 = (bf16[2,704,256]{2,1,0:T(8,128)(2,1)}, bf16[2,704,256]{2,1,0:T(8,128)(2,1)}, u32[]{:S(2)}, u32[]{:S(2)}) collective-permute-start(bf16[2,704,256]{2,1,0:T(8,128)(2,1)} %get-tuple-element.32), channel_id=1, source_target_pairs={{0,3},{1,0},{2,1},{3,2},{4,7},{5,4},{6,5},{7,6},{8,11},{9,8},{10,9... | collective-permute-start | bytes 2162696 | tf_op jit(solution)/shard_map/ppermute | solution.py:340
  197.5 36.8 %collective-permute-start.41 = (bf16[704,256]{1,0:T(8,128)(2,1)S(1)}, bf16[704,256]{1,0:T(8,128)(2,1)S(1)}, u32[]{:S(2)}, u32[]{:S(2)}) collective-permute-start(bf16[704,256]{1,0:T(8,128)(2,1)S(1)} %fusion.20), channel_id=1, source_target_pairs={{0,4},{1,5},{2,6},{3,7},{4,0},{5,1},{6,2},{7,3},{8,12},{9,13},{10,... | collective-permute-start | bytes 1081352 | tf_op jit(solution)/shard_map/ppermute | solution.py:343
  (39 other events, 622.0 us)

commit v4 on v3

--- a/solution.py
+++ b/solution.py
@@ -220,10 +220,12 @@
 
 def piece_sources(my_index):
     y, z, core = my_index // 4, (my_index // 2) % 2, my_index % 2
+    keep = len(PIECE_STEPS) - LATE
     places = []
-    for step in range(2):
-        for dy, dz in PIECE_STEPS:
-            places.append(((y + dy + 4) % 4) * 4 + ((z + dz) % 2) * 2 + (core + step) % 2)
+    for steps in (PIECE_STEPS[:keep], PIECE_STEPS[keep:]):
+        for other in range(2):
+            for dy, dz in steps:
+                places.append(((y + dy + 4) % 4) * 4 + ((z + dz) % 2) * 2 + (core + other) % 2)
     return jnp.stack(places)
 
 
@@ -241,10 +243,10 @@
 def pick_rows(onehot, coef, pieces, scaled, buffer, first):
     count, (rows, width), slots = len(pieces), pieces[0].shape, onehot.shape[1]
     tile = 1024
-    total = 2 * len(PIECE_STEPS) * slots
+    place = first // count
     in_specs = [
-        pl.BlockSpec((count, slots, rows), lambda j: (0, 0, 0)),
-        pl.BlockSpec((count, slots, 1), lambda j: (0, 0, 0)),
+        pl.BlockSpec((count, slots, rows), lambda j: (place, 0, 0)),
+        pl.BlockSpec((count, slots, 1), lambda j: (place, 0, 0)),
     ] + [pl.BlockSpec((rows, tile), lambda j: (0, j))] * count
     operands = [onehot, coef, *pieces]
     aliases = {}
@@ -257,8 +259,8 @@
         lambda *refs: pick_kernel(count, scaled, *refs),
         grid=(width // tile,),
         in_specs=in_specs,
-        out_specs=pl.BlockSpec((block, tile), lambda j: (first // block, j)),
-        out_shape=jax.ShapeDtypeStruct((total, width), jnp.bfloat16),
+        out_specs=pl.BlockSpec((block, tile), lambda j: (place, j)),
+        out_shape=jax.ShapeDtypeStruct((onehot.shape[0] * slots, width), jnp.bfloat16),
         input_output_aliases=aliases,
         cost_estimate=pl.CostEstimate(
             flops=2 * block * rows * width,
@@ -376,21 +378,14 @@
     matches = route_experts[0][None, :, :] == all_experts[:, None, None]
     coef_out = jnp.sum(jnp.where(matches, route_weight[0][None], 0.0), axis=2)
     coef_in = lax.all_to_all(coef_out, "ctx", split_axis=0, concat_axis=0, tiled=True)
-    keep = len(PIECE_STEPS) - LATE
-    early = 2 * keep
-    halves = (slice(0, keep), slice(keep + LATE, 2 * keep + LATE))
-    tails = (slice(keep, keep + LATE), slice(2 * keep + LATE, None))
+    early = 2 * (len(PIECE_STEPS) - LATE)
     onehot, slot_coef = route_slots(coef_in[piece_sources(my_index)], capacity)
-    onehot, slot_coef = (
-        jnp.concatenate([v[part] for part in halves + tails]) for v in (onehot, slot_coef)
-    )
 
     def early_pick(mine, others, scaled):
-        return pick_rows(onehot[:early], slot_coef[:early], mine + others, scaled, None, 0)
+        return pick_rows(onehot, slot_coef, mine + others, scaled, None, 0)
 
     def late_pick(mine, others, scaled, buffer):
-        first = early * capacity
-        return pick_rows(onehot[early:], slot_coef[early:], mine + others, scaled, buffer, first)
+        return pick_rows(onehot, slot_coef, mine + others, scaled, buffer, early)
 
     beside, below, above = (pass_on(tokens_here, move) for move in (Z_SWAP, Y_UP, Y_DOWN))
     below_beside, far = pass_on(below, Z_SWAP), pass_on(below, Y_UP)

time: 252 us -> 252 us (level)
  waiting for transfers between devices: 91.3 us -> 95.7 us
  starting transfers between devices: 58.7 us -> 54.9 us
    all_to_all x1, waiting for transfers between devices: 0.01 us -> 4.38 us  [per_device(): lax.all_to_all(coef_out, 'ctx', split_axis=0, concat_axis=0, tiled=True)]
    ppermute x30, starting transfers between devices: 25.6 us -> 22.6 us  [pass_on(): return lax.ppermute(value, 'ctx', move)]
where the time goes in v4:
time: 252 us; the launch traced here: 250 us
  waiting for transfers between devices  95.7 us (38%)
  Pallas kernels  59.1 us (23%)
  starting transfers between devices  54.9 us (22%)
  matrix products  19.3 us (8%)
  other arithmetic  12.1 us (5%)
  local copies, waits for them, and re-layouts  7.35 us (3%)
    ppermute x30, waiting for transfers between devices, pass_on(): return lax.ppermute(value, 'ctx', move)  52.5 us
    ppermute x6, waiting for transfers between devices, sum_x_first(): lax.ppermute(term, 'dp', move)  30.5 us
    pallas_call x3, Pallas kernels, weight_terms(): pl.pallas_call(lambda *refs: term_kernel(per_step, homes, *refs), grid_sp...  24.7 us
    ppermute x30, starting transfers between devices, pass_on(): return lax.ppermute(value, 'ctx', move)  22.6 us
    dot_general x3, matrix products, dot_nn(): lax.dot_general(a, b, (((1,), (0,)), ((), ())), preferred_element_type=jn...  19.3 us
    pallas_call x4, Pallas kernels, pick_rows(): pl.pallas_call(lambda *refs: pick_kernel(count, scaled, *refs), grid=(wid...  15.3 us
    pallas_call x1, Pallas kernels, attention_rows(): pl.pallas_call(attention_kernel, in_specs=[smem, smem, smem, vmem], out_s...  11.3 us
    ppermute x6, starting transfers between devices, sum_x_first(): lax.ppermute(term, 'dp', move)  8.25 us
  transfers between devices with their start and end apart: 45, of which 14 were waited for; matrix products, arithmetic and copies ran while one was open for 14% of the time, Pallas kernels for 24%

profile of v4, /device:TPU:2, one launch (start us, length us, event | category | flops | bytes accessed | tf_op | source)
XLA Modules:
  0.0 249.6 jit_solution(5840277453044119940)
XLA Ops:
  6.2 10.7 %collective-permute-done.2.refs_4_ = bf16[128,2048]{1,0:T(8,128)(2,1)S(1)} collective-permute-done((bf16[128,2048]{1,0:T(8,128)(2,1)}, bf16[128,2048]{1,0:T(8,128)(2,1)S(1)}, u32[]{:S(2)}, u32[]{:S(2)}) %collective-permute-start.2) | collective-permute-done | bytes 524320 | tf_op jit(solution)/shard_map/ppermute | solution.py:218
  20.9 6.2 %collective-permute-done.20.refs_4_ = bf16[128,2048]{1,0:T(8,128)(2,1)S(1)} collective-permute-done((bf16[128,2048]{1,0:T(8,128)(2,1)}, bf16[128,2048]{1,0:T(8,128)(2,1)S(1)}, u32[]{:S(2)}, u32[]{:S(2)}) %collective-permute-start.20) | collective-permute-done | bytes 524320 | tf_op jit(solution)/shard_map/ppermute | solution.py:218
  27.4 4.6 %collective-permute-done.15.refs_3_ = bf16[128,2048]{1,0:T(8,128)(2,1)} collective-permute-done((bf16[128,2048]{1,0:T(8,128)(2,1)}, bf16[128,2048]{1,0:T(8,128)(2,1)}, u32[]{:S(2)}, u32[]{:S(2)}) %collective-permute-start.15) | collective-permute-done | bytes 524320 | tf_op jit(solution)/shard_map/ppermute | solution.py:218
  32.7 7.7 %collective-permute-done.3.refs_6_ = bf16[128,2048]{1,0:T(8,128)(2,1)S(1)} collective-permute-done((bf16[128,2048]{1,0:T(8,128)(2,1)S(1)}, bf16[128,2048]{1,0:T(8,128)(2,1)S(1)}, u32[]{:S(2)}, u32[]{:S(2)}) %collective-permute-start.3) | collective-permute-done | bytes 524320 | tf_op jit(solution)/shard_map/ppermute | solution.py:218
  54.2 5.4 %pack_rows.1 = bf16[16,384,128]{2,1,0:T(8,128)(2,1)} custom-call(bf16[128,1024]{1,0:T(8,128)(2,1)} %bitcast.119, bf16[128,1024]{1,0:T(8,128)(2,1)} %bitcast.120, bf16[128,1024]{1,0:T(8,128)(2,1)} %bitcast.121, bf16[128,2048]{1,0:T(8,128)(2,1)} %bitcast.110, bf16[1024,2048]{1,0:T(8,128)(2,1)} %w_ref.1), custom_call_target="tpu_custom_call" | custom-call | flops 536870912 | bytes 7000000 | tf_op jit(solution)/shard_map/pack_rows/pallas_call | solution.py:47
  59.6 4.4 %all-to-all-done.2 = f32[16,1,128]{2,1,0:T(1,128)S(1)} async-done(((f32[16,1,128]{2,1,0:T(1,128)}), f32[16,1,128]{2,1,0:T(1,128)S(1)}, u32[]{:S(2)}, u32[]{:S(2)}) %all-to-all-start.2) | async-done | bytes 8224 | tf_op jit(solution)/shard_map/all_to_all | solution.py:380
  64.0 4.5 %all-to-all-start = ((bf16[16,384,128]{2,1,0:T(8,128)(2,1)}), bf16[16,384,128]{2,1,0:T(8,128)(2,1)}, u32[]{:S(2)}, u32[]{:S(2)}) async-start(bf16[16,384,128]{2,1,0:T(8,128)(2,1)} %pack_rows.1), calls=%async_computation | async-start | bytes 3145728 | tf_op jit(solution)/shard_map/all_to_all | solution.py:423
  76.5 23.2 %collective-permute-done.17.refs_3_ = bf16[128,2048]{1,0:T(8,128)(2,1)S(1)} collective-permute-done((bf16[128,2048]{1,0:T(8,128)(2,1)}, bf16[128,2048]{1,0:T(8,128)(2,1)S(1)}, u32[]{:S(2)}, u32[]{:S(2)}) %collective-permute-start.17) | collective-permute-done | bytes 524320 | tf_op jit(solution)/shard_map/ppermute | solution.py:218
  101.8 11.3 %attention_rows.1 = bf16[16,320,128]{2,1,0:T(8,128)(2,1)} custom-call(s32[64]{0:T(128)} %reshape.699.lists_ref, s32[16]{0:T(128)} %bitcast.125, s32[1]{0:T(128)} %bitcast.1.half_ref, bf16[16,384,128]{2,1,0:T(8,128)(2,1)} %all-to-all-done.rows_ref), custom_call_target="tpu_custom_call" | custom-call | bytes 3000000 | tf_op jit(solution)/shard_map/attention_rows/pallas_call | solution.py:142
  113.2 5.3 %all-to-all-start.1 = ((bf16[16,320,128]{2,1,0:T(8,128)(2,1)}), bf16[16,320,128]{2,1,0:T(8,128)(2,1)}, u32[]{:S(2)}, u32[]{:S(2)}) async-start(bf16[16,320,128]{2,1,0:T(8,128)(2,1)} %attention_rows.1), calls=%async_computation.1 | async-start | bytes 2621440 | tf_op jit(solution)/shard_map/all_to_all | solution.py:436
  118.5 4.9 %pick_rows.4.refs_6_ = bf16[1024,2048]{1,0:T(8,128)(2,1)} custom-call(bf16[16,64,128]{2,1,0:T(8,128)(2,1)} %fusion.15.refs_0_, f32[16,64,1]{2,1,0:T(8,128)} %copy.41.refs_1_, bf16[128,2048]{1,0:T(8,128)(2,1)} %bitcast.111, bf16[128,2048]{1,0:T(8,128)(2,1)} %collective-permute-done.refs_3_, bf16[128,2048]{1,0:T(8,128)(2,1)} %copy-done.9, ...), custom_call_target="tpu_custom_call" | custom-call | flops 402653184 | bytes 9437184 | tf_op jit(solution)/shard_map/pick_rows/pallas_call | solution.py:258
  123.9 4.8 %pick_rows.6.refs_6_ = bf16[1024,2048]{1,0:T(8,128)(2,1)} custom-call(bf16[16,64,128]{2,1,0:T(8,128)(2,1)} %fusion.15.refs_0_, f32[16,64,1]{2,1,0:T(8,128)} %copy.41.refs_1_, bf16[128,2048]{1,0:T(8,128)(2,1)} %bitcast.118, bf16[128,2048]{1,0:T(8,128)(2,1)} %collective-permute-done.15.refs_3_, bf16[128,2048]{1,0:T(8,128)(2,1)} %copy-done.7, ...), custom_call_target="tpu_custom_call" | custom-call | flops 402653184 | bytes 9437184 | tf_op jit(solution)/shard_map/pick_rows/pallas_call | solution.py:258
  131.6 6.0 %fusion.2 = f32[1024,704]{0,1:T(8,128)S(1)} fusion(bf16[1024,2048]{1,0:T(8,128)(2,1)} %pick_rows.7.refs_2_.refs_3_.refs_4_.refs_5_, bf16[1,2048,704]{1,2,0:T(8,128)(2,1)} %param.23), kind=kOutput, calls=%fused_computation.3 | convolution fusion | flops 2952790016 | bytes 9961472 | tf_op jit(solution)/shard_map/dot_general | solution.py:25
  137.7 4.9 %multiply_convert_fusion.2 = (bf16[1024,704]{0,1:T(8,128)(2,1)}, f32[1024,704]{0,1:T(8,128)}) fusion(f32[1024,704]{0,1:T(8,128)S(1)} %fusion.2, bf16[1024,2048]{1,0:T(8,128)(2,1)S(1)} %copy-done.2, bf16[1,2048,704]{1,2,0:T(8,128)(2,1)S(1)} %copy-done), kind=kOutput, calls=%fused_computation.9 | convolution fusion | flops 2957115392 | bytes 14286848 | tf_op jit(solution)/shard_map/dot_general | solution.py:25
  145.4 8.3 %weight_terms.3 = (bf16[2,704,256]{2,1,0:T(8,128)(2,1)}, bf16[2,704,256]{2,1,0:T(8,128)(2,1)}, bf16[2,704,256]{2,1,0:T(8,128)(2,1)}, bf16[2,704,256]{2,1,0:T(8,128)(2,1)}) custom-call(s32[8]{0:T(128)} %stack.97.refs_0_, bf16[704,1024]{1,0:T(8,128)(2,1)} %bitcast.112, bf16[1024,2048]{1,0:T(8,128)(2,1)} %pick_rows.5.refs_2_.refs_3_.refs_4_.refs_5_, ...), custom_call_target="tpu_custom_call" | custom-call | bytes 1000000 | tf_op jit(solution)/shard_map/weight_terms/pallas_call | solution.py:301
  155.9 8.4 %fusion.7 = (bf16[704,1024]{1,0:T(8,128)(2,1)}, bf16[704,1024]{1,0:T(8,128)(2,1)}) fusion(f32[1024,704]{0,1:T(8,128)} %copy-done.21, f32[1024,704]{0,1:T(8,128)} %get-tuple-element.28, bf16[1024,2048]{1,0:T(8,128)(2,1)} %pick_rows.5.refs_2_.refs_3_.refs_4_.refs_5_, bf16[1,2048,704]{1,2,0:T(8,128)(2,1)S(1)} %copy-done.20), kind=kOutput, calls=%fused_computation.12 | convolution fusion | flops 2962161664 | bytes 15728640 | tf_op jit(solution)/shard_map/dot_general | solution.py:25
  164.3 8.2 %weight_terms.5 = (bf16[4,704,256]{2,1,0:T(8,128)(2,1)}, bf16[4,704,256]{2,1,0:T(8,128)(2,1)}) custom-call(s32[8]{0:T(128)} %stack.115.refs_0_, bf16[704,1024]{1,0:T(8,128)(2,1)} %get-tuple-element.40.refs_1_, bf16[1024,2048]{1,0:T(8,128)(2,1)} %pick_rows.7.refs_2_.refs_3_.refs_4_.refs_5_, bf16[1024,2048]{1,0:T(8,128)(2,1)} %pick_rows.7.refs_2_.refs_3_.refs_4_.refs_5_, ...), custom_call_target="tpu_custom_call" | custom-call | bytes 1000000 | tf_op jit(solution)/shard_map/weight_terms/pallas_call | solution.py:301
  178.0 8.2 %weight_terms.4 = (bf16[2,704,256]{2,1,0:T(8,128)(2,1)}, bf16[2,704,256]{2,1,0:T(8,128)(2,1)}, bf16[2,704,256]{2,1,0:T(8,128)(2,1)}, bf16[2,704,256]{2,1,0:T(8,128)(2,1)}) custom-call(s32[8]{0:T(128)} %stack.97.refs_0_, bf16[704,1024]{1,0:T(8,128)(2,1)} %get-tuple-element.41.refs_1_, bf16[1024,2048]{1,0:T(8,128)(2,1)} %pick_rows.7.refs_2_.refs_3_.refs_4_.refs_5_, ...), custom_call_target="tpu_custom_call" | custom-call | bytes 1000000 | tf_op jit(solution)/shard_map/weight_terms/pallas_call | solution.py:301
  192.6 3.6 %collective-permute-done.40 = bf16[2,704,256]{2,1,0:T(8,128)(2,1)} collective-permute-done((bf16[2,704,256]{2,1,0:T(8,128)(2,1)}, bf16[2,704,256]{2,1,0:T(8,128)(2,1)}, u32[]{:S(2)}, u32[]{:S(2)}) %collective-permute-start.40) | collective-permute-done | bytes 720928 | tf_op jit(solution)/shard_map/ppermute | solution.py:342
  198.2 14.2 %collective-permute-done.30 = bf16[2,704,256]{2,1,0:T(8,128)(2,1)} collective-permute-done((bf16[2,704,256]{2,1,0:T(8,128)(2,1)}, bf16[2,704,256]{2,1,0:T(8,128)(2,1)}, u32[]{:S(2)}, u32[]{:S(2)}) %collective-permute-start.30) | collective-permute-done | bytes 720928 | tf_op jit(solution)/shard_map/ppermute | solution.py:342
  212.3 8.1 %collective-permute-done.31 = bf16[2,704,256]{2,1,0:T(8,128)(2,1)} collective-permute-done((bf16[2,704,256]{2,1,0:T(8,128)(2,1)}, bf16[2,704,256]{2,1,0:T(8,128)(2,1)}, u32[]{:S(2)}, u32[]{:S(2)}) %collective-permute-start.31) | collective-permute-done | bytes 720928 | tf_op jit(solution)/shard_map/ppermute | solution.py:342
  220.4 4.6 %collective-permute-done.32 = bf16[2,704,256]{2,1,0:T(8,128)(2,1)} collective-permute-done((bf16[2,704,256]{2,1,0:T(8,128)(2,1)}, bf16[2,704,256]{2,1,0:T(8,128)(2,1)}, u32[]{:S(2)}, u32[]{:S(2)}) %collective-permute-start.32) | collective-permute-done | bytes 720928 | tf_op jit(solution)/shard_map/ppermute | solution.py:342
  228.8 3.6 %collective-permute-start.35 = (bf16[704,256]{1,0:T(8,128)(2,1)S(1)}, bf16[704,256]{1,0:T(8,128)(2,1)S(1)}, u32[]{:S(2)}, u32[]{:S(2)}) collective-permute-start(bf16[704,256]{1,0:T(8,128)(2,1)S(1)} %get-tuple-element.42), channel_id=1, source_target_pairs={{0,2},{1,3},{2,0},{3,1},{4,6},{5,7},{6,4},{7,5},{8,10},{9,11},{10,... | collective-permute-start | bytes 1081352 | tf_op jit(solution)/shard_map/ppermute | solution.py:352
  241.7 5.4 %collective-permute-done.36 = bf16[704,256]{1,0:T(8,128)(2,1)S(1)} collective-permute-done((bf16[704,256]{1,0:T(8,128)(2,1)S(1)}, bf16[704,256]{1,0:T(8,128)(2,1)S(1)}, u32[]{:S(2)}, u32[]{:S(2)}) %collective-permute-start.36) | collective-permute-done | bytes 360480 | tf_op jit(solution)/shard_map/ppermute | solution.py:352
  (146 shorter events, 71.7 us)
Async XLA Ops:
  5.9 21.2 %collective-permute-start.20 = (bf16[128,2048]{1,0:T(8,128)(2,1)}, bf16[128,2048]{1,0:T(8,128)(2,1)S(1)}, u32[]{:S(2)}, u32[]{:S(2)}) collective-permute-start(bf16[128,2048]{1,0:T(8,128)(2,1)} %bitcast.114), channel_id=1, source_target_pairs={{0,32},{8,40},{16,48},{24,56},{32,64},{40,72},{48,80},{56,88},{64,... | collective-permute-start | bytes 1572872 | tf_op jit(solution)/shard_map/ppermute | solution.py:218
  20.7 19.7 %collective-permute-start.3 = (bf16[128,2048]{1,0:T(8,128)(2,1)S(1)}, bf16[128,2048]{1,0:T(8,128)(2,1)S(1)}, u32[]{:S(2)}, u32[]{:S(2)}) collective-permute-start(bf16[128,2048]{1,0:T(8,128)(2,1)S(1)} %collective-permute-done.2.refs_4_), channel_id=1, source_target_pairs={{0,16},{8,24},{16,0},{24,8},{32,48},{40,56},{48,32},{56,40},{64,80... | collective-permute-start | bytes 1572872 | tf_op jit(solution)/shard_map/ppermute | solution.py:218
  40.4 30.5 %collective-permute-start.1 = (bf16[128,2048]{1,0:T(8,128)(2,1)}, bf16[128,2048]{1,0:T(8,128)(2,1)}, u32[]{:S(2)}, u32[]{:S(2)}) collective-permute-start(bf16[128,2048]{1,0:T(8,128)(2,1)} %collective-permute-done.refs_3_), channel_id=1, source_target_pairs={{0,96},{8,104},{16,112},{24,120},{32,0},{40,8},{48,16},{56,24},{64... | collective-permute-start | bytes 1572872 | tf_op jit(solution)/shard_map/ppermute | solution.py:218
  42.2 28.9 %collective-permute-start.22 = (bf16[128,2048]{1,0:T(8,128)(2,1)S(1)}, bf16[128,2048]{1,0:T(8,128)(2,1)}, u32[]{:S(2)}, u32[]{:S(2)}) collective-permute-start(bf16[128,2048]{1,0:T(8,128)(2,1)S(1)} %collective-permute-done.20.refs_4_), channel_id=1, source_target_pairs={{0,16},{8,24},{16,0},{24,8},{32,48},{40,56},{48,32},{56,40},{64,80... | collective-permute-start | bytes 1572872 | tf_op jit(solution)/shard_map/ppermute | solution.py:218
  43.9 27.6 %collective-permute-start.23 = (bf16[128,2048]{1,0:T(8,128)(2,1)S(1)}, bf16[128,2048]{1,0:T(8,128)(2,1)}, u32[]{:S(2)}, u32[]{:S(2)}) collective-permute-start(bf16[128,2048]{1,0:T(8,128)(2,1)S(1)} %collective-permute-done.20.refs_4_), channel_id=1, source_target_pairs={{0,32},{8,40},{16,48},{24,56},{32,64},{40,72},{48,80},{56,88},{64,... | collective-permute-start | bytes 1572872 | tf_op jit(solution)/shard_map/ppermute | solution.py:218
  44.2 27.4 %collective-permute-start.26 = (bf16[128,2048]{1,0:T(8,128)(2,1)S(1)}, bf16[128,2048]{1,0:T(8,128)(2,1)}, u32[]{:S(2)}, u32[]{:S(2)}) collective-permute-start(bf16[128,2048]{1,0:T(8,128)(2,1)S(1)} %collective-permute-done.20.refs_4_), channel_id=1, source_target_pairs={{0,8},{8,0},{16,24},{24,16},{32,40},{40,32},{48,56},{56,48},{64,72... | collective-permute-start | bytes 1572872 | tf_op jit(solution)/shard_map/ppermute | solution.py:218
  45.7 26.2 %collective-permute-start.16 = (bf16[128,2048]{1,0:T(8,128)(2,1)}, bf16[128,2048]{1,0:T(8,128)(2,1)}, u32[]{:S(2)}, u32[]{:S(2)}) collective-permute-start(bf16[128,2048]{1,0:T(8,128)(2,1)} %collective-permute-done.15.refs_3_), channel_id=1, source_target_pairs={{0,96},{8,104},{16,112},{24,120},{32,0},{40,8},{48,16},{56,24},{64... | collective-permute-start | bytes 1572872 | tf_op jit(solution)/shard_map/ppermute | solution.py:218
  64.0 37.8 %all-to-all-start = ((bf16[16,384,128]{2,1,0:T(8,128)(2,1)}), bf16[16,384,128]{2,1,0:T(8,128)(2,1)}, u32[]{:S(2)}, u32[]{:S(2)}) async-start(bf16[16,384,128]{2,1,0:T(8,128)(2,1)} %pack_rows.1), calls=%async_computation | async-start | bytes 3145728 | tf_op jit(solution)/shard_map/all_to_all | solution.py:423
  72.0 27.8 %collective-permute-start.17 = (bf16[128,2048]{1,0:T(8,128)(2,1)}, bf16[128,2048]{1,0:T(8,128)(2,1)S(1)}, u32[]{:S(2)}, u32[]{:S(2)}) collective-permute-start(bf16[128,2048]{1,0:T(8,128)(2,1)} %collective-permute-done.16.refs_2_), channel_id=1, source_target_pairs={{0,96},{8,104},{16,112},{24,120},{32,0},{40,8},{48,16},{56,24},{64... | collective-permute-start | bytes 1572872 | tf_op jit(solution)/shard_map/ppermute | solution.py:218
  75.7 47.6 %collective-permute-start.4 = (bf16[128,2048]{1,0:T(8,128)(2,1)}, bf16[128,2048]{1,0:T(8,128)(2,1)}, u32[]{:S(2)}, u32[]{:S(2)}) collective-permute-start(bf16[128,2048]{1,0:T(8,128)(2,1)} %copy-done.13), channel_id=1, source_target_pairs={{0,32},{8,40},{16,48},{24,56},{32,64},{40,72},{48,80},{56,88},{64,... | collective-permute-start | bytes 1572872 | tf_op jit(solution)/shard_map/ppermute | solution.py:218
  75.8 53.0 %collective-permute-start.18 = (bf16[128,2048]{1,0:T(8,128)(2,1)}, bf16[128,2048]{1,0:T(8,128)(2,1)}, u32[]{:S(2)}, u32[]{:S(2)}) collective-permute-start(bf16[128,2048]{1,0:T(8,128)(2,1)} %collective-permute-done.16.refs_2_), channel_id=1, source_target_pairs={{0,8},{8,0},{16,24},{24,16},{32,40},{40,32},{48,56},{56,48},{64,72... | collective-permute-start | bytes 1572872 | tf_op jit(solution)/shard_map/ppermute | solution.py:218
  75.9 47.9 %collective-permute-start.28 = (bf16[128,2048]{1,0:T(8,128)(2,1)}, bf16[128,2048]{1,0:T(8,128)(2,1)}, u32[]{:S(2)}, u32[]{:S(2)}) collective-permute-start(bf16[128,2048]{1,0:T(8,128)(2,1)} %collective-permute-done.22.refs_6_), channel_id=1, source_target_pairs={{0,8},{8,0},{16,24},{24,16},{32,40},{40,32},{48,56},{56,48},{64,72... | collective-permute-start | bytes 1572872 | tf_op jit(solution)/shard_map/ppermute | solution.py:218
  76.4 47.5 %collective-permute-start.29 = (bf16[128,2048]{1,0:T(8,128)(2,1)}, bf16[128,2048]{1,0:T(8,128)(2,1)}, u32[]{:S(2)}, u32[]{:S(2)}) collective-permute-start(bf16[128,2048]{1,0:T(8,128)(2,1)} %collective-permute-done.23.refs_7_), channel_id=1, source_target_pairs={{0,8},{8,0},{16,24},{24,16},{32,40},{40,32},{48,56},{56,48},{64,72... | collective-permute-start | bytes 1572872 | tf_op jit(solution)/shard_map/ppermute | solution.py:218
  99.7 29.0 %collective-permute-start.19 = (bf16[128,2048]{1,0:T(8,128)(2,1)S(1)}, bf16[128,2048]{1,0:T(8,128)(2,1)}, u32[]{:S(2)}, u32[]{:S(2)}) collective-permute-start(bf16[128,2048]{1,0:T(8,128)(2,1)S(1)} %collective-permute-done.17.refs_3_), channel_id=1, source_target_pairs={{0,8},{8,0},{16,24},{24,16},{32,40},{40,32},{48,56},{56,48},{64,72... | collective-permute-start | bytes 1572872 | tf_op jit(solution)/shard_map/ppermute | solution.py:218
  113.2 77.2 %all-to-all-start.1 = ((bf16[16,320,128]{2,1,0:T(8,128)(2,1)}), bf16[16,320,128]{2,1,0:T(8,128)(2,1)}, u32[]{:S(2)}, u32[]{:S(2)}) async-start(bf16[16,320,128]{2,1,0:T(8,128)(2,1)} %attention_rows.1), calls=%async_computation.1 | async-start | bytes 2621440 | tf_op jit(solution)/shard_map/all_to_all | solution.py:436
  123.3 19.3 %collective-permute-start.5 = (bf16[128,2048]{1,0:T(8,128)(2,1)}, bf16[128,2048]{1,0:T(8,128)(2,1)}, u32[]{:S(2)}, u32[]{:S(2)}) collective-permute-start(bf16[128,2048]{1,0:T(8,128)(2,1)} %collective-permute-done.1.refs_2_), channel_id=1, source_target_pairs={{0,8},{8,0},{16,24},{24,16},{32,40},{40,32},{48,56},{56,48},{64,72... | collective-permute-start | bytes 1572872 | tf_op jit(solution)/shard_map/ppermute | solution.py:218
  153.8 33.9 %collective-permute-start.38 = (bf16[2,704,256]{2,1,0:T(8,128)(2,1)}, bf16[2,704,256]{2,1,0:T(8,128)(2,1)}, u32[]{:S(2)}, u32[]{:S(2)}) collective-permute-start(bf16[2,704,256]{2,1,0:T(8,128)(2,1)} %get-tuple-element.26), channel_id=1, source_target_pairs={{0,2},{1,3},{2,0},{3,1},{4,6},{5,7},{6,4},{7,5},{8,10},{9,11},{10,... | collective-permute-start | bytes 2162696 | tf_op jit(solution)/shard_map/ppermute | solution.py:342
  155.9 34.4 %collective-permute-start.39 = (bf16[2,704,256]{2,1,0:T(8,128)(2,1)}, bf16[2,704,256]{2,1,0:T(8,128)(2,1)}, u32[]{:S(2)}, u32[]{:S(2)}) collective-permute-start(bf16[2,704,256]{2,1,0:T(8,128)(2,1)} %get-tuple-element.36), channel_id=1, source_target_pairs={{0,1},{1,2},{2,3},{3,0},{4,5},{5,6},{6,7},{7,4},{8,9},{9,10},{10,1... | collective-permute-start | bytes 2162696 | tf_op jit(solution)/shard_map/ppermute | solution.py:342
  172.4 55.3 %collective-permute-start.34 = (bf16[4,704,256]{2,1,0:T(8,128)(2,1)}, bf16[4,704,256]{2,1,0:T(8,128)(2,1)S(1)}, u32[]{:S(2)}, u32[]{:S(2)}) collective-permute-start(bf16[4,704,256]{2,1,0:T(8,128)(2,1)} %get-tuple-element.34), channel_id=1, source_target_pairs={{0,4},{1,5},{2,6},{3,7},{4,0},{5,1},{6,2},{7,3},{8,12},{9,13},{10,... | collective-permute-start | bytes 4325384 | tf_op jit(solution)/shard_map/ppermute | solution.py:350
  176.0 20.2 %collective-permute-start.40 = (bf16[2,704,256]{2,1,0:T(8,128)(2,1)}, bf16[2,704,256]{2,1,0:T(8,128)(2,1)}, u32[]{:S(2)}, u32[]{:S(2)}) collective-permute-start(bf16[2,704,256]{2,1,0:T(8,128)(2,1)} %get-tuple-element.37), channel_id=1, source_target_pairs={{0,3},{1,0},{2,1},{3,2},{4,7},{5,4},{6,5},{7,6},{8,11},{9,8},{10,9... | collective-permute-start | bytes 2162696 | tf_op jit(solution)/shard_map/ppermute | solution.py:342
  186.2 26.1 %collective-permute-start.30 = (bf16[2,704,256]{2,1,0:T(8,128)(2,1)}, bf16[2,704,256]{2,1,0:T(8,128)(2,1)}, u32[]{:S(2)}, u32[]{:S(2)}) collective-permute-start(bf16[2,704,256]{2,1,0:T(8,128)(2,1)} %get-tuple-element.30), channel_id=1, source_target_pairs={{0,2},{1,3},{2,0},{3,1},{4,6},{5,7},{6,4},{7,5},{8,10},{9,11},{10,... | collective-permute-start | bytes 2162696 | tf_op jit(solution)/shard_map/ppermute | solution.py:342
  187.7 32.7 %collective-permute-start.31 = (bf16[2,704,256]{2,1,0:T(8,128)(2,1)}, bf16[2,704,256]{2,1,0:T(8,128)(2,1)}, u32[]{:S(2)}, u32[]{:S(2)}) collective-permute-start(bf16[2,704,256]{2,1,0:T(8,128)(2,1)} %get-tuple-element.31), channel_id=1, source_target_pairs={{0,1},{1,2},{2,3},{3,0},{4,5},{5,6},{6,7},{7,4},{8,9},{9,10},{10,1... | collective-permute-start | bytes 2162696 | tf_op jit(solution)/shard_map/ppermute | solution.py:342
  190.3 34.7 %collective-permute-start.32 = (bf16[2,704,256]{2,1,0:T(8,128)(2,1)}, bf16[2,704,256]{2,1,0:T(8,128)(2,1)}, u32[]{:S(2)}, u32[]{:S(2)}) collective-permute-start(bf16[2,704,256]{2,1,0:T(8,128)(2,1)} %get-tuple-element.32), channel_id=1, source_target_pairs={{0,3},{1,0},{2,1},{3,2},{4,7},{5,4},{6,5},{7,6},{8,11},{9,8},{10,9... | collective-permute-start | bytes 2162696 | tf_op jit(solution)/shard_map/ppermute | solution.py:342
  197.8 36.7 %collective-permute-start.41 = (bf16[704,256]{1,0:T(8,128)(2,1)S(1)}, bf16[704,256]{1,0:T(8,128)(2,1)S(1)}, u32[]{:S(2)}, u32[]{:S(2)}) collective-permute-start(bf16[704,256]{1,0:T(8,128)(2,1)S(1)} %fusion.20), channel_id=1, source_target_pairs={{0,4},{1,5},{2,6},{3,7},{4,0},{5,1},{6,2},{7,3},{8,12},{9,13},{10,... | collective-permute-start | bytes 1081352 | tf_op jit(solution)/shard_map/ppermute | solution.py:345
  (43 other events, 685.1 us)

commit v5 on v4

--- a/solution.py
+++ b/solution.py
@@ -405,11 +405,12 @@
     buffer = early_pick(near_rows, near_others, False)
     rows_in = late_pick(far_rows, far_others, False, buffer)
     gate_pre = lax.optimization_barrier(dot_nn(rows_in, gate_weight[0]))
+    up_pre = dot_nn(rows_in, up_weight[0])
     gate_sig = jax.nn.sigmoid(gate_pre)
     gate_act = gate_pre * gate_sig
-    up_pre = dot_nn(rows_in, up_weight[0])
     hidden = (gate_act * up_pre).astype(jnp.bfloat16)
-    up_pre, hidden = lax.optimization_barrier((up_pre, hidden))
+    gate_slope = up_pre * gate_sig * (1.0 + gate_pre * (1.0 - gate_sig))
+    hidden, gate_act, gate_slope = lax.optimization_barrier((hidden, gate_act, gate_slope))
     g_near = [grads_here, g_beside, g_below, g_above, g_below_beside, g_far]
     g_near_others = [pass_on(piece, CORE_SWAP) for piece in g_near]
     g_buffer = early_pick(g_near, g_near_others, True)
@@ -423,9 +424,7 @@
     head_rows = lax.all_to_all(packed, "ctx", split_axis=0, concat_axis=0, tiled=True)
     later_grads = lax.optimization_barrier((grads_in, down_terms[0]))[0]
     hidden_grad = dot_nn(later_grads, down_weight[0])
-    gate_delta = (
-        hidden_grad * up_pre * gate_sig * (1.0 + gate_pre * (1.0 - gate_sig))
-    ).astype(jnp.bfloat16)
+    gate_delta = (hidden_grad * gate_slope).astype(jnp.bfloat16)
     up_delta = (hidden_grad * gate_act).astype(jnp.bfloat16)
     up_grad = sum_z_first(*weight_terms(z_order, up_delta.T, rows_in, (4, 4)))
     gate_terms = weight_terms(x_order, gate_delta.T, rows_in, (2, 2, 2, 2))

time: 252 us -> 253 us (level)
  other arithmetic: 12.1 us -> 17.1 us
    mul x0 -> x1, other arithmetic: none -> 3.94 us  [per_device(): gate_slope = up_pre * gate_sig * (1.0 + gate_pre * (1.0 - gate_sig))]
  transfers between devices with their start and end apart: 45 -> 45, of which waited for: 14 -> 15; matrix products, arithmetic and copies ran while one was open for 14% -> 15% of each run, Pallas kernels for 24% -> 23%
where the time goes in v5:
time: 253 us; the launch traced here: 252 us
  waiting for transfers between devices  95.7 us (38%)
  Pallas kernels  58.9 us (23%)
  starting transfers between devices  55.8 us (22%)
  other arithmetic  17.1 us (7%)
  matrix products  16.8 us (7%)
  local copies, waits for them, and re-layouts  6.58 us (3%)
    ppermute x30, waiting for transfers between devices, pass_on(): return lax.ppermute(value, 'ctx', move)  52.6 us
    ppermute x6, waiting for transfers between devices, sum_x_first(): lax.ppermute(term, 'dp', move)  29.7 us
    pallas_call x3, Pallas kernels, weight_terms(): pl.pallas_call(lambda *refs: term_kernel(per_step, homes, *refs), grid_sp...  24.6 us
    ppermute x30, starting transfers between devices, pass_on(): return lax.ppermute(value, 'ctx', move)  22.6 us
    dot_general x3, matrix products, dot_nn(): lax.dot_general(a, b, (((1,), (0,)), ((), ())), preferred_element_type=jn...  16.8 us
    pallas_call x4, Pallas kernels, pick_rows(): pl.pallas_call(lambda *refs: pick_kernel(count, scaled, *refs), grid=(wid...  15.3 us
    pallas_call x1, Pallas kernels, attention_rows(): pl.pallas_call(attention_kernel, in_specs=[smem, smem, smem, vmem], out_s...  11.4 us
    ppermute x3, waiting for transfers between devices, sum_z_first(): lax.ppermute(term, 'dp', move)  9.01 us
  transfers between devices with their start and end apart: 45, of which 15 were waited for; matrix products, arithmetic and copies ran while one was open for 15% of the time, Pallas kernels for 23%

profile of v5, /device:TPU:2, one launch (start us, length us, event | category | flops | bytes accessed | tf_op | source)
XLA Modules:
  0.0 252.1 jit_solution(9949893467588327221)
XLA Ops:
  6.2 10.7 %collective-permute-done.2.refs_4_ = bf16[128,2048]{1,0:T(8,128)(2,1)S(1)} collective-permute-done((bf16[128,2048]{1,0:T(8,128)(2,1)}, bf16[128,2048]{1,0:T(8,128)(2,1)S(1)}, u32[]{:S(2)}, u32[]{:S(2)}) %collective-permute-start.2) | collective-permute-done | bytes 524320 | tf_op jit(solution)/shard_map/ppermute | solution.py:218
  20.9 6.2 %collective-permute-done.20.refs_4_ = bf16[128,2048]{1,0:T(8,128)(2,1)S(1)} collective-permute-done((bf16[128,2048]{1,0:T(8,128)(2,1)}, bf16[128,2048]{1,0:T(8,128)(2,1)S(1)}, u32[]{:S(2)}, u32[]{:S(2)}) %collective-permute-start.20) | collective-permute-done | bytes 524320 | tf_op jit(solution)/shard_map/ppermute | solution.py:218
  27.4 4.6 %collective-permute-done.15.refs_3_ = bf16[128,2048]{1,0:T(8,128)(2,1)} collective-permute-done((bf16[128,2048]{1,0:T(8,128)(2,1)}, bf16[128,2048]{1,0:T(8,128)(2,1)}, u32[]{:S(2)}, u32[]{:S(2)}) %collective-permute-start.15) | collective-permute-done | bytes 524320 | tf_op jit(solution)/shard_map/ppermute | solution.py:218
  32.7 7.7 %collective-permute-done.3.refs_6_ = bf16[128,2048]{1,0:T(8,128)(2,1)S(1)} collective-permute-done((bf16[128,2048]{1,0:T(8,128)(2,1)S(1)}, bf16[128,2048]{1,0:T(8,128)(2,1)S(1)}, u32[]{:S(2)}, u32[]{:S(2)}) %collective-permute-start.3) | collective-permute-done | bytes 524320 | tf_op jit(solution)/shard_map/ppermute | solution.py:218
  50.8 3.5 %all-to-all-start.2 = ((f32[16,1,128]{2,1,0:T(1,128)}), f32[16,1,128]{2,1,0:T(1,128)S(1)}, u32[]{:S(2)}, u32[]{:S(2)}) async-start(f32[16,1,128]{2,1,0:T(1,128)} %bitcast.18), calls=%async_computation.2 | async-start | bytes 16384 | tf_op jit(solution)/shard_map/all_to_all | solution.py:380
  54.3 5.4 %pack_rows.1 = bf16[16,384,128]{2,1,0:T(8,128)(2,1)} custom-call(bf16[128,1024]{1,0:T(8,128)(2,1)} %bitcast.117, bf16[128,1024]{1,0:T(8,128)(2,1)} %bitcast.118, bf16[128,1024]{1,0:T(8,128)(2,1)} %bitcast.119, bf16[128,2048]{1,0:T(8,128)(2,1)} %bitcast.109, bf16[1024,2048]{1,0:T(8,128)(2,1)} %w_ref.1), custom_call_target="tpu_custom_call" | custom-call | flops 536870912 | bytes 7000000 | tf_op jit(solution)/shard_map/pack_rows/pallas_call | solution.py:47
  59.7 4.3 %all-to-all-done.2 = f32[16,1,128]{2,1,0:T(1,128)S(1)} async-done(((f32[16,1,128]{2,1,0:T(1,128)}), f32[16,1,128]{2,1,0:T(1,128)S(1)}, u32[]{:S(2)}, u32[]{:S(2)}) %all-to-all-start.2) | async-done | bytes 8224 | tf_op jit(solution)/shard_map/all_to_all | solution.py:380
  64.0 4.5 %all-to-all-start = ((bf16[16,384,128]{2,1,0:T(8,128)(2,1)}), bf16[16,384,128]{2,1,0:T(8,128)(2,1)}, u32[]{:S(2)}, u32[]{:S(2)}) async-start(bf16[16,384,128]{2,1,0:T(8,128)(2,1)} %pack_rows.1), calls=%async_computation | async-start | bytes 3145728 | tf_op jit(solution)/shard_map/all_to_all | solution.py:424
  76.5 23.3 %collective-permute-done.17.refs_3_ = bf16[128,2048]{1,0:T(8,128)(2,1)} collective-permute-done((bf16[128,2048]{1,0:T(8,128)(2,1)}, bf16[128,2048]{1,0:T(8,128)(2,1)}, u32[]{:S(2)}, u32[]{:S(2)}) %collective-permute-start.17) | collective-permute-done | bytes 524320 | tf_op jit(solution)/shard_map/ppermute | solution.py:218
  101.9 11.4 %attention_rows.1 = bf16[16,320,128]{2,1,0:T(8,128)(2,1)} custom-call(s32[64]{0:T(128)} %reshape.699.lists_ref, s32[16]{0:T(128)} %bitcast.123, s32[1]{0:T(128)} %bitcast.1.half_ref, bf16[16,384,128]{2,1,0:T(8,128)(2,1)} %all-to-all-done.rows_ref), custom_call_target="tpu_custom_call" | custom-call | bytes 3000000 | tf_op jit(solution)/shard_map/attention_rows/pallas_call | solution.py:142
  113.3 5.3 %all-to-all-start.1 = ((bf16[16,320,128]{2,1,0:T(8,128)(2,1)}), bf16[16,320,128]{2,1,0:T(8,128)(2,1)}, u32[]{:S(2)}, u32[]{:S(2)}) async-start(bf16[16,320,128]{2,1,0:T(8,128)(2,1)} %attention_rows.1), calls=%async_computation.1 | async-start | bytes 2621440 | tf_op jit(solution)/shard_map/all_to_all | solution.py:435
  118.6 4.8 %pick_rows.4.refs_6_ = bf16[1024,2048]{1,0:T(8,128)(2,1)} custom-call(bf16[16,64,128]{2,1,0:T(8,128)(2,1)} %fusion.15.refs_0_, f32[16,64,1]{2,1,0:T(8,128)} %copy.41.refs_1_, bf16[128,2048]{1,0:T(8,128)(2,1)} %bitcast.110, bf16[128,2048]{1,0:T(8,128)(2,1)} %collective-permute-done.refs_3_, bf16[128,2048]{1,0:T(8,128)(2,1)} %copy-done.7, ...), custom_call_target="tpu_custom_call" | custom-call | flops 402653184 | bytes 9437184 | tf_op jit(solution)/shard_map/pick_rows/pallas_call | solution.py:258
  124.0 4.8 %pick_rows.6.refs_6_ = bf16[1024,2048]{1,0:T(8,128)(2,1)} custom-call(bf16[16,64,128]{2,1,0:T(8,128)(2,1)} %fusion.15.refs_0_, f32[16,64,1]{2,1,0:T(8,128)} %copy.41.refs_1_, bf16[128,2048]{1,0:T(8,128)(2,1)} %bitcast.116, bf16[128,2048]{1,0:T(8,128)(2,1)} %collective-permute-done.15.refs_3_, bf16[128,2048]{1,0:T(8,128)(2,1)} %copy-done.5, ...), custom_call_target="tpu_custom_call" | custom-call | flops 402653184 | bytes 9437184 | tf_op jit(solution)/shard_map/pick_rows/pallas_call | solution.py:258
  131.7 6.0 %fusion.2 = f32[1024,704]{0,1:T(8,128)S(1)} fusion(bf16[1024,2048]{1,0:T(8,128)(2,1)} %pick_rows.7.refs_2_.refs_3_.refs_4_.refs_5_, bf16[1,2048,704]{1,2,0:T(8,128)(2,1)} %param.24), kind=kOutput, calls=%fused_computation.3 | convolution fusion | flops 2952790016 | bytes 9961472 | tf_op jit(solution)/shard_map/dot_general | solution.py:25
  140.9 3.9 %add_multiply_fusion = (f32[1024,704]{0,1:T(8,128)}, bf16[1024,704]{0,1:T(8,128)(2,1)}, f32[1024,704]{0,1:T(8,128)}) fusion(f32[1024,704]{0,1:T(8,128)S(1)} %fusion.4, f32[1024,704]{0,1:T(8,128)S(1)} %fusion.2), kind=kLoop, calls=%fused_computation.9 | loop fusion | flops 7929856 | bytes 12976128 | tf_op jit(solution)/shard_map/mul | solution.py:412
  147.7 8.2 %weight_terms.3 = (bf16[2,704,256]{2,1,0:T(8,128)(2,1)}, bf16[2,704,256]{2,1,0:T(8,128)(2,1)}, bf16[2,704,256]{2,1,0:T(8,128)(2,1)}, bf16[2,704,256]{2,1,0:T(8,128)(2,1)}) custom-call(s32[8]{0:T(128)} %stack.97.refs_0_, bf16[704,1024]{1,0:T(8,128)(2,1)} %bitcast.104, bf16[1024,2048]{1,0:T(8,128)(2,1)} %pick_rows.5.refs_2_.refs_3_.refs_4_.refs_5_, ...), custom_call_target="tpu_custom_call" | custom-call | bytes 1000000 | tf_op jit(solution)/shard_map/weight_terms/pallas_call | solution.py:301
  158.0 7.6 %fusion.8 = (bf16[704,1024]{1,0:T(8,128)(2,1)}, bf16[704,1024]{1,0:T(8,128)(2,1)}) fusion(f32[1024,704]{0,1:T(8,128)} %get-tuple-element.34, f32[1024,704]{0,1:T(8,128)} %get-tuple-element.29, bf16[1024,2048]{1,0:T(8,128)(2,1)} %pick_rows.5.refs_2_.refs_3_.refs_4_.refs_5_, bf16[1,2048,704]{1,2,0:T(8,128)(2,1)S(1)} %copy-done), kind=kOutput, calls=%fused_computation.14 | convolution fusion | flops 2955673600 | bytes 15728640 | tf_op jit(solution)/shard_map/dot_general | solution.py:25
  165.6 8.2 %weight_terms.5 = (bf16[4,704,256]{2,1,0:T(8,128)(2,1)}, bf16[4,704,256]{2,1,0:T(8,128)(2,1)}) custom-call(s32[8]{0:T(128)} %stack.115.refs_0_, bf16[704,1024]{1,0:T(8,128)(2,1)} %get-tuple-element.47.refs_1_, bf16[1024,2048]{1,0:T(8,128)(2,1)} %pick_rows.7.refs_2_.refs_3_.refs_4_.refs_5_, bf16[1024,2048]{1,0:T(8,128)(2,1)} %pick_rows.7.refs_2_.refs_3_.refs_4_.refs_5_, ...), custom_call_target="tpu_custom_call" | custom-call | bytes 1000000 | tf_op jit(solution)/shard_map/weight_terms/pallas_call | solution.py:301
  173.8 3.6 %collective-permute-start.34 = (bf16[4,704,256]{2,1,0:T(8,128)(2,1)}, bf16[4,704,256]{2,1,0:T(8,128)(2,1)}, u32[]{:S(2)}, u32[]{:S(2)}) collective-permute-start(bf16[4,704,256]{2,1,0:T(8,128)(2,1)} %get-tuple-element.36), channel_id=1, source_target_pairs={{0,4},{1,5},{2,6},{3,7},{4,0},{5,1},{6,2},{7,3},{8,12},{9,13},{10,... | collective-permute-start | bytes 4325384 | tf_op jit(solution)/shard_map/ppermute | solution.py:350
  179.4 8.2 %weight_terms.4 = (bf16[2,704,256]{2,1,0:T(8,128)(2,1)}, bf16[2,704,256]{2,1,0:T(8,128)(2,1)}, bf16[2,704,256]{2,1,0:T(8,128)(2,1)}, bf16[2,704,256]{2,1,0:T(8,128)(2,1)}) custom-call(s32[8]{0:T(128)} %stack.97.refs_0_, bf16[704,1024]{1,0:T(8,128)(2,1)} %get-tuple-element.48.refs_1_, bf16[1024,2048]{1,0:T(8,128)(2,1)} %pick_rows.7.refs_2_.refs_3_.refs_4_.refs_5_, ...), custom_call_target="tpu_custom_call" | custom-call | bytes 1000000 | tf_op jit(solution)/shard_map/weight_terms/pallas_call | solution.py:301
  200.3 13.3 %collective-permute-done.30 = bf16[2,704,256]{2,1,0:T(8,128)(2,1)} collective-permute-done((bf16[2,704,256]{2,1,0:T(8,128)(2,1)}, bf16[2,704,256]{2,1,0:T(8,128)(2,1)}, u32[]{:S(2)}, u32[]{:S(2)}) %collective-permute-start.30) | collective-permute-done | bytes 720928 | tf_op jit(solution)/shard_map/ppermute | solution.py:342
  213.7 8.8 %collective-permute-done.31 = bf16[2,704,256]{2,1,0:T(8,128)(2,1)} collective-permute-done((bf16[2,704,256]{2,1,0:T(8,128)(2,1)}, bf16[2,704,256]{2,1,0:T(8,128)(2,1)}, u32[]{:S(2)}, u32[]{:S(2)}) %collective-permute-start.31) | collective-permute-done | bytes 720928 | tf_op jit(solution)/shard_map/ppermute | solution.py:342
  222.5 3.9 %collective-permute-done.32 = bf16[2,704,256]{2,1,0:T(8,128)(2,1)} collective-permute-done((bf16[2,704,256]{2,1,0:T(8,128)(2,1)}, bf16[2,704,256]{2,1,0:T(8,128)(2,1)}, u32[]{:S(2)}, u32[]{:S(2)}) %collective-permute-start.32) | collective-permute-done | bytes 720928 | tf_op jit(solution)/shard_map/ppermute | solution.py:342
  243.9 5.2 %collective-permute-done.36 = bf16[704,256]{1,0:T(8,128)(2,1)S(1)} collective-permute-done((bf16[704,256]{1,0:T(8,128)(2,1)S(1)}, bf16[704,256]{1,0:T(8,128)(2,1)S(1)}, u32[]{:S(2)}, u32[]{:S(2)}) %collective-permute-start.36) | collective-permute-done | bytes 360480 | tf_op jit(solution)/shard_map/ppermute | solution.py:352
  (141 shorter events, 77.3 us)
Async XLA Ops:
  5.9 21.2 %collective-permute-start.20 = (bf16[128,2048]{1,0:T(8,128)(2,1)}, bf16[128,2048]{1,0:T(8,128)(2,1)S(1)}, u32[]{:S(2)}, u32[]{:S(2)}) collective-permute-start(bf16[128,2048]{1,0:T(8,128)(2,1)} %bitcast.112), channel_id=1, source_target_pairs={{0,32},{8,40},{16,48},{24,56},{32,64},{40,72},{48,80},{56,88},{64,... | collective-permute-start | bytes 1572872 | tf_op jit(solution)/shard_map/ppermute | solution.py:218
  40.4 30.5 %collective-permute-start.1 = (bf16[128,2048]{1,0:T(8,128)(2,1)}, bf16[128,2048]{1,0:T(8,128)(2,1)}, u32[]{:S(2)}, u32[]{:S(2)}) collective-permute-start(bf16[128,2048]{1,0:T(8,128)(2,1)} %collective-permute-done.refs_3_), channel_id=1, source_target_pairs={{0,96},{8,104},{16,112},{24,120},{32,0},{40,8},{48,16},{56,24},{64... | collective-permute-start | bytes 1572872 | tf_op jit(solution)/shard_map/ppermute | solution.py:218
  42.1 28.9 %collective-permute-start.22 = (bf16[128,2048]{1,0:T(8,128)(2,1)S(1)}, bf16[128,2048]{1,0:T(8,128)(2,1)}, u32[]{:S(2)}, u32[]{:S(2)}) collective-permute-start(bf16[128,2048]{1,0:T(8,128)(2,1)S(1)} %collective-permute-done.20.refs_4_), channel_id=1, source_target_pairs={{0,16},{8,24},{16,0},{24,8},{32,48},{40,56},{48,32},{56,40},{64,80... | collective-permute-start | bytes 1572872 | tf_op jit(solution)/shard_map/ppermute | solution.py:218
  43.9 27.6 %collective-permute-start.23 = (bf16[128,2048]{1,0:T(8,128)(2,1)S(1)}, bf16[128,2048]{1,0:T(8,128)(2,1)}, u32[]{:S(2)}, u32[]{:S(2)}) collective-permute-start(bf16[128,2048]{1,0:T(8,128)(2,1)S(1)} %collective-permute-done.20.refs_4_), channel_id=1, source_target_pairs={{0,32},{8,40},{16,48},{24,56},{32,64},{40,72},{48,80},{56,88},{64,... | collective-permute-start | bytes 1572872 | tf_op jit(solution)/shard_map/ppermute | solution.py:218
  44.2 27.4 %collective-permute-start.26 = (bf16[128,2048]{1,0:T(8,128)(2,1)S(1)}, bf16[128,2048]{1,0:T(8,128)(2,1)}, u32[]{:S(2)}, u32[]{:S(2)}) collective-permute-start(bf16[128,2048]{1,0:T(8,128)(2,1)S(1)} %collective-permute-done.20.refs_4_), channel_id=1, source_target_pairs={{0,8},{8,0},{16,24},{24,16},{32,40},{40,32},{48,56},{56,48},{64,72... | collective-permute-start | bytes 1572872 | tf_op jit(solution)/shard_map/ppermute | solution.py:218
  45.8 26.2 %collective-permute-start.16 = (bf16[128,2048]{1,0:T(8,128)(2,1)}, bf16[128,2048]{1,0:T(8,128)(2,1)}, u32[]{:S(2)}, u32[]{:S(2)}) collective-permute-start(bf16[128,2048]{1,0:T(8,128)(2,1)} %collective-permute-done.15.refs_3_), channel_id=1, source_target_pairs={{0,96},{8,104},{16,112},{24,120},{32,0},{40,8},{48,16},{56,24},{64... | collective-permute-start | bytes 1572872 | tf_op jit(solution)/shard_map/ppermute | solution.py:218
  64.0 37.9 %all-to-all-start = ((bf16[16,384,128]{2,1,0:T(8,128)(2,1)}), bf16[16,384,128]{2,1,0:T(8,128)(2,1)}, u32[]{:S(2)}, u32[]{:S(2)}) async-start(bf16[16,384,128]{2,1,0:T(8,128)(2,1)} %pack_rows.1), calls=%async_computation | async-start | bytes 3145728 | tf_op jit(solution)/shard_map/all_to_all | solution.py:424
  72.0 27.9 %collective-permute-start.17 = (bf16[128,2048]{1,0:T(8,128)(2,1)}, bf16[128,2048]{1,0:T(8,128)(2,1)}, u32[]{:S(2)}, u32[]{:S(2)}) collective-permute-start(bf16[128,2048]{1,0:T(8,128)(2,1)} %collective-permute-done.16.refs_2_), channel_id=1, source_target_pairs={{0,96},{8,104},{16,112},{24,120},{32,0},{40,8},{48,16},{56,24},{64... | collective-permute-start | bytes 1572872 | tf_op jit(solution)/shard_map/ppermute | solution.py:218
  75.8 47.7 %collective-permute-start.4 = (bf16[128,2048]{1,0:T(8,128)(2,1)}, bf16[128,2048]{1,0:T(8,128)(2,1)S(1)}, u32[]{:S(2)}, u32[]{:S(2)}) collective-permute-start(bf16[128,2048]{1,0:T(8,128)(2,1)} %copy-done.11), channel_id=1, source_target_pairs={{0,32},{8,40},{16,48},{24,56},{32,64},{40,72},{48,80},{56,88},{64,... | collective-permute-start | bytes 1572872 | tf_op jit(solution)/shard_map/ppermute | solution.py:218
  75.8 53.1 %collective-permute-start.18 = (bf16[128,2048]{1,0:T(8,128)(2,1)}, bf16[128,2048]{1,0:T(8,128)(2,1)}, u32[]{:S(2)}, u32[]{:S(2)}) collective-permute-start(bf16[128,2048]{1,0:T(8,128)(2,1)} %collective-permute-done.16.refs_2_), channel_id=1, source_target_pairs={{0,8},{8,0},{16,24},{24,16},{32,40},{40,32},{48,56},{56,48},{64,72... | collective-permute-start | bytes 1572872 | tf_op jit(solution)/shard_map/ppermute | solution.py:218
  75.9 47.9 %collective-permute-start.28 = (bf16[128,2048]{1,0:T(8,128)(2,1)}, bf16[128,2048]{1,0:T(8,128)(2,1)}, u32[]{:S(2)}, u32[]{:S(2)}) collective-permute-start(bf16[128,2048]{1,0:T(8,128)(2,1)} %collective-permute-done.22.refs_6_), channel_id=1, source_target_pairs={{0,8},{8,0},{16,24},{24,16},{32,40},{40,32},{48,56},{56,48},{64,72... | collective-permute-start | bytes 1572872 | tf_op jit(solution)/shard_map/ppermute | solution.py:218
  76.4 47.6 %collective-permute-start.29 = (bf16[128,2048]{1,0:T(8,128)(2,1)}, bf16[128,2048]{1,0:T(8,128)(2,1)}, u32[]{:S(2)}, u32[]{:S(2)}) collective-permute-start(bf16[128,2048]{1,0:T(8,128)(2,1)} %collective-permute-done.23.refs_7_), channel_id=1, source_target_pairs={{0,8},{8,0},{16,24},{24,16},{32,40},{40,32},{48,56},{56,48},{64,72... | collective-permute-start | bytes 1572872 | tf_op jit(solution)/shard_map/ppermute | solution.py:218
  99.8 29.0 %collective-permute-start.19 = (bf16[128,2048]{1,0:T(8,128)(2,1)}, bf16[128,2048]{1,0:T(8,128)(2,1)}, u32[]{:S(2)}, u32[]{:S(2)}) collective-permute-start(bf16[128,2048]{1,0:T(8,128)(2,1)} %collective-permute-done.17.refs_3_), channel_id=1, source_target_pairs={{0,8},{8,0},{16,24},{24,16},{32,40},{40,32},{48,56},{56,48},{64,72... | collective-permute-start | bytes 1572872 | tf_op jit(solution)/shard_map/ppermute | solution.py:218
  113.3 78.9 %all-to-all-start.1 = ((bf16[16,320,128]{2,1,0:T(8,128)(2,1)}), bf16[16,320,128]{2,1,0:T(8,128)(2,1)}, u32[]{:S(2)}, u32[]{:S(2)}) async-start(bf16[16,320,128]{2,1,0:T(8,128)(2,1)} %attention_rows.1), calls=%async_computation.1 | async-start | bytes 2621440 | tf_op jit(solution)/shard_map/all_to_all | solution.py:435
  123.4 21.5 %collective-permute-start.5 = (bf16[128,2048]{1,0:T(8,128)(2,1)}, bf16[128,2048]{1,0:T(8,128)(2,1)}, u32[]{:S(2)}, u32[]{:S(2)}) collective-permute-start(bf16[128,2048]{1,0:T(8,128)(2,1)} %collective-permute-done.1.refs_2_), channel_id=1, source_target_pairs={{0,8},{8,0},{16,24},{24,16},{32,40},{40,32},{48,56},{56,48},{64,72... | collective-permute-start | bytes 1572872 | tf_op jit(solution)/shard_map/ppermute | solution.py:218
  123.9 21.0 %collective-permute-start.6 = (bf16[128,2048]{1,0:T(8,128)(2,1)S(1)}, bf16[128,2048]{1,0:T(8,128)(2,1)}, u32[]{:S(2)}, u32[]{:S(2)}) collective-permute-start(bf16[128,2048]{1,0:T(8,128)(2,1)S(1)} %collective-permute-done.4.refs_3_), channel_id=1, source_target_pairs={{0,8},{8,0},{16,24},{24,16},{32,40},{40,32},{48,56},{56,48},{64,72... | collective-permute-start | bytes 1572872 | tf_op jit(solution)/shard_map/ppermute | solution.py:218
  155.9 33.2 %collective-permute-start.38 = (bf16[2,704,256]{2,1,0:T(8,128)(2,1)}, bf16[2,704,256]{2,1,0:T(8,128)(2,1)}, u32[]{:S(2)}, u32[]{:S(2)}) collective-permute-start(bf16[2,704,256]{2,1,0:T(8,128)(2,1)} %get-tuple-element.27), channel_id=1, source_target_pairs={{0,2},{1,3},{2,0},{3,1},{4,6},{5,7},{6,4},{7,5},{8,10},{9,11},{10,... | collective-permute-start | bytes 2162696 | tf_op jit(solution)/shard_map/ppermute | solution.py:342
  158.0 34.2 %collective-permute-start.39 = (bf16[2,704,256]{2,1,0:T(8,128)(2,1)}, bf16[2,704,256]{2,1,0:T(8,128)(2,1)}, u32[]{:S(2)}, u32[]{:S(2)}) collective-permute-start(bf16[2,704,256]{2,1,0:T(8,128)(2,1)} %get-tuple-element.38), channel_id=1, source_target_pairs={{0,1},{1,2},{2,3},{3,0},{4,5},{5,6},{6,7},{7,4},{8,9},{9,10},{10,1... | collective-permute-start | bytes 2162696 | tf_op jit(solution)/shard_map/ppermute | solution.py:342
  173.8 55.6 %collective-permute-start.34 = (bf16[4,704,256]{2,1,0:T(8,128)(2,1)}, bf16[4,704,256]{2,1,0:T(8,128)(2,1)}, u32[]{:S(2)}, u32[]{:S(2)}) collective-permute-start(bf16[4,704,256]{2,1,0:T(8,128)(2,1)} %get-tuple-element.36), channel_id=1, source_target_pairs={{0,4},{1,5},{2,6},{3,7},{4,0},{5,1},{6,2},{7,3},{8,12},{9,13},{10,... | collective-permute-start | bytes 4325384 | tf_op jit(solution)/shard_map/ppermute | solution.py:350
  177.4 20.2 %collective-permute-start.40 = (bf16[2,704,256]{2,1,0:T(8,128)(2,1)}, bf16[2,704,256]{2,1,0:T(8,128)(2,1)}, u32[]{:S(2)}, u32[]{:S(2)}) collective-permute-start(bf16[2,704,256]{2,1,0:T(8,128)(2,1)} %get-tuple-element.39), channel_id=1, source_target_pairs={{0,3},{1,0},{2,1},{3,2},{4,7},{5,4},{6,5},{7,6},{8,11},{9,8},{10,9... | collective-permute-start | bytes 2162696 | tf_op jit(solution)/shard_map/ppermute | solution.py:342
  187.6 26.1 %collective-permute-start.30 = (bf16[2,704,256]{2,1,0:T(8,128)(2,1)}, bf16[2,704,256]{2,1,0:T(8,128)(2,1)}, u32[]{:S(2)}, u32[]{:S(2)}) collective-permute-start(bf16[2,704,256]{2,1,0:T(8,128)(2,1)} %get-tuple-element.31), channel_id=1, source_target_pairs={{0,2},{1,3},{2,0},{3,1},{4,6},{5,7},{6,4},{7,5},{8,10},{9,11},{10,... | collective-permute-start | bytes 2162696 | tf_op jit(solution)/shard_map/ppermute | solution.py:342
  189.1 33.4 %collective-permute-start.31 = (bf16[2,704,256]{2,1,0:T(8,128)(2,1)}, bf16[2,704,256]{2,1,0:T(8,128)(2,1)}, u32[]{:S(2)}, u32[]{:S(2)}) collective-permute-start(bf16[2,704,256]{2,1,0:T(8,128)(2,1)} %get-tuple-element.32), channel_id=1, source_target_pairs={{0,1},{1,2},{2,3},{3,0},{4,5},{5,6},{6,7},{7,4},{8,9},{9,10},{10,1... | collective-permute-start | bytes 2162696 | tf_op jit(solution)/shard_map/ppermute | solution.py:342
  192.2 34.2 %collective-permute-start.32 = (bf16[2,704,256]{2,1,0:T(8,128)(2,1)}, bf16[2,704,256]{2,1,0:T(8,128)(2,1)}, u32[]{:S(2)}, u32[]{:S(2)}) collective-permute-start(bf16[2,704,256]{2,1,0:T(8,128)(2,1)} %get-tuple-element.33), channel_id=1, source_target_pairs={{0,3},{1,0},{2,1},{3,2},{4,7},{5,4},{6,5},{7,6},{8,11},{9,8},{10,9... | collective-permute-start | bytes 2162696 | tf_op jit(solution)/shard_map/ppermute | solution.py:342
  199.1 37.3 %collective-permute-start.41 = (bf16[704,256]{1,0:T(8,128)(2,1)S(1)}, bf16[704,256]{1,0:T(8,128)(2,1)S(1)}, u32[]{:S(2)}, u32[]{:S(2)}) collective-permute-start(bf16[704,256]{1,0:T(8,128)(2,1)S(1)} %fusion.20), channel_id=1, source_target_pairs={{0,4},{1,5},{2,6},{3,7},{4,0},{5,1},{6,2},{7,3},{8,12},{9,13},{10,... | collective-permute-start | bytes 1081352 | tf_op jit(solution)/shard_map/ppermute | solution.py:345
  (40 other events, 667.2 us)

commit v6 on v5

--- a/solution.py
+++ b/solution.py
@@ -63,7 +63,9 @@
     )(queries, keys, values, grads, out_weight)
 
 
-def attention_kernel(lists_ref, lengths_ref, half_ref, rows_ref, out_ref, key_acc, value_acc):
+def attention_kernel(
+    lists_ref, lengths_ref, half_ref, rows_ref, out_ref, give_ref, key_acc, value_acc
+):
     inv_root = 1.0 / math.sqrt(HD)
     blocks = rows_ref.shape[0]
     key_acc[...] = jnp.zeros_like(key_acc)
@@ -123,16 +125,18 @@
         results = [terms(i, scored[u][0], probs[u]) for u, i in enumerate(rows)]
         for u, i in enumerate(rows):
             query_sum, key_terms, value_terms = results[u]
-            out_ref[i, 2 * BLK :, :] = (query_sum * inv_root).astype(jnp.bfloat16)
+            out_ref[i, BLK:, :] = (query_sum * inv_root).astype(jnp.bfloat16)
             for n, block in enumerate(scored[u][0]):
                 key_acc[block] += key_terms[n]
                 value_acc[block] += value_terms[n]
         return carry
 
     lax.fori_loop(0, blocks // TOGETHER, some_blocks, 0)
-    for i in range(blocks):
-        out_ref[i, 0:BLK, :] = (key_acc[i] * inv_root).astype(jnp.bfloat16)
-        out_ref[i, BLK : 2 * BLK, :] = value_acc[i].astype(jnp.bfloat16)
+    for ref, half in ((out_ref, half_ref[0]), (give_ref, 1 - half_ref[0])):
+        rows = pl.ds(pl.multiple_of(half * HALF, HALF), HALF)
+        for i in range(blocks):
+            ref[i, 0:HALF, :] = (key_acc[i, rows, :] * inv_root).astype(jnp.bfloat16)
+            ref[i, HALF:BLK, :] = value_acc[i, rows, :].astype(jnp.bfloat16)
 
 
 def attention_rows(lists, lengths, half, rows):
@@ -142,8 +146,11 @@
     return pl.pallas_call(
         attention_kernel,
         in_specs=[smem, smem, smem, vmem],
-        out_specs=vmem,
-        out_shape=jax.ShapeDtypeStruct((blocks, 2 * BLK + HALF, HD), jnp.bfloat16),
+        out_specs=(vmem, vmem),
+        out_shape=(
+            jax.ShapeDtypeStruct((blocks, BLK + HALF, HD), jnp.bfloat16),
+            jax.ShapeDtypeStruct((blocks, BLK, HD), jnp.bfloat16),
+        ),
         scratch_shapes=[
             pltpu.VMEM((blocks, BLK, HD), jnp.float32),
             pltpu.VMEM((blocks, BLK, HD), jnp.float32),
@@ -154,17 +161,11 @@
 
 
 def unpack_kernel(rows_ref, query_ref, key_ref, value_ref):
-    for h in range(HEADS):
-        cols = slice(h * HD, (h + 1) * HD)
-
-        def both(rows):
-            first = rows_ref[2 * h, rows, :].astype(jnp.float32)
-            return (first + rows_ref[2 * h + 1, rows, :].astype(jnp.float32)).astype(jnp.bfloat16)
-
-        key_ref[:, cols] = both(slice(0, BLK))
-        value_ref[:, cols] = both(slice(BLK, 2 * BLK))
-        query_ref[0:HALF, cols] = rows_ref[2 * h, 2 * BLK :, :]
-        query_ref[HALF:BLK, cols] = rows_ref[2 * h + 1, 2 * BLK :, :]
+    for place in range(2 * HEADS):
+        head, half = place // 2, place % 2
+        cols, rows = slice(head * HD, (head + 1) * HD), slice(half * HALF, (half + 1) * HALF)
+        for k, ref in enumerate((key_ref, value_ref, query_ref)):
+            ref[rows, cols] = rows_ref[place, k * HALF : (k + 1) * HALF, :]
 
 
 def unpack_rows(rows):
@@ -280,26 +281,21 @@
     return chosen.astype(jnp.bfloat16), slot_coef
 
 
-def term_kernel(per_step, homes, order_ref, delta_ref, *refs):
+def term_kernel(per_step, order_ref, delta_ref, *refs):
     rows, out_refs = refs[:per_step], refs[per_step:]
-    step = pl.program_id(0)
-    values = [dot_nn(delta_ref[...], row[...]).astype(jnp.bfloat16) for row in rows]
-    for t in range(len(homes) // per_step):
-
-        @pl.when(step == t)
-        def _(t=t):
-            for u, value in enumerate(values):
-                array, place = homes[t * per_step + u]
-                out_refs[array][place] = value
-
-
-def weight_terms(order, delta, rows, stacks):
+    depth = per_step // len(out_refs)
+    for u, row in enumerate(rows):
+        out_refs[u // depth][u % depth] = dot_nn(delta_ref[...], row[...]).astype(jnp.bfloat16)
+
+
+def weight_terms(order, delta, rows, arrays):
     count, per_step = order.shape[0], 4
     hidden, slots = delta.shape
     tile = rows.shape[1] // count
-    homes = [(a, p) for a, depth in enumerate(stacks) for p in range(depth)]
+    depth = per_step // arrays
+    shape = jax.ShapeDtypeStruct((count // arrays, hidden, tile), jnp.bfloat16)
     return pl.pallas_call(
-        lambda *refs: term_kernel(per_step, homes, *refs),
+        lambda *refs: term_kernel(per_step, *refs),
         grid_spec=pltpu.PrefetchScalarGridSpec(
             num_scalar_prefetch=1,
             grid=(count // per_step,),
@@ -310,12 +306,9 @@
                 )
                 for u in range(per_step)
             ],
-            out_specs=[
-                pl.BlockSpec((depth, hidden, tile), lambda j, order_ref: (0, 0, 0))
-                for depth in stacks
-            ],
+            out_specs=[pl.BlockSpec((depth, hidden, tile), lambda j, order_ref: (j, 0, 0))] * arrays,
         ),
-        out_shape=[jax.ShapeDtypeStruct((depth, hidden, tile), jnp.bfloat16) for depth in stacks],
+        out_shape=[shape] * arrays,
         cost_estimate=pl.CostEstimate(flops=0, bytes_accessed=1_000_000, transcendentals=0),
         name="weight_terms",
     )(order, delta, *([rows] * per_step))
@@ -327,8 +320,8 @@
     return jnp.stack([((z + dz) % 2) * 4 + (x + dx) % 4 for dx, dz in steps]).astype(jnp.int32)
 
 
-X_FIRST = ((2, 0), (2, 1), (1, 0), (1, 1), (3, 0), (3, 1), (0, 0), (0, 1))
-Z_FIRST = ((2, 1), (1, 1), (3, 1), (0, 1), (2, 0), (1, 0), (3, 0), (0, 0))
+X_FIRST = ((2, 0), (1, 0), (3, 0), (0, 0), (2, 1), (1, 1), (3, 1), (0, 1))
+Z_FIRST = ((2, 1), (1, 1), (2, 0), (1, 0), (3, 1), (0, 1), (3, 0), (0, 0))
 
 
 def add_terms(*terms):
@@ -419,19 +412,24 @@
     grads_in = late_pick(g_fars, g_far_others, True, g_buffer)
 
     x_order, z_order = term_order(X_FIRST), term_order(Z_FIRST)
-    down_terms = weight_terms(x_order, hidden.T, grads_in, (2, 2, 2, 2))
+    down_terms = weight_terms(x_order, hidden.T, grads_in, 4)
     down_grad = sum_x_first(*down_terms)
     head_rows = lax.all_to_all(packed, "ctx", split_axis=0, concat_axis=0, tiled=True)
     later_grads = lax.optimization_barrier((grads_in, down_terms[0]))[0]
     hidden_grad = dot_nn(later_grads, down_weight[0])
     gate_delta = (hidden_grad * gate_slope).astype(jnp.bfloat16)
     up_delta = (hidden_grad * gate_act).astype(jnp.bfloat16)
-    up_grad = sum_z_first(*weight_terms(z_order, up_delta.T, rows_in, (4, 4)))
-    gate_terms = weight_terms(x_order, gate_delta.T, rows_in, (2, 2, 2, 2))
+    up_grad = sum_z_first(*weight_terms(z_order, up_delta.T, rows_in, 2))
+    gate_terms = weight_terms(x_order, gate_delta.T, rows_in, 4)
     gate_grad = sum_x_first(*gate_terms)
 
     half = (my_index % 2).astype(jnp.int32).reshape(1)
-    grad_rows = attention_rows(block_lists.reshape(-1), block_lengths.reshape(-1), half, head_rows)
+    kept, given = attention_rows(
+        block_lists.reshape(-1), block_lengths.reshape(-1), half, head_rows
+    )
+    taken = pass_on(given, CORE_SWAP)
+    summed = add_terms(kept[:, :BLK], taken).astype(jnp.bfloat16)
+    grad_rows = jnp.concatenate([summed, kept[:, BLK:]], axis=1)
     returned = lax.all_to_all(grad_rows, "ctx", split_axis=0, concat_axis=0, tiled=True)
     query_grad, key_grad, value_grad = unpack_rows(returned)
     return (query_grad[None], key_grad[None], value_grad[None], gate_grad, up_grad, down_grad)

time: 253 us -> 257 us (1.016)
  Pallas kernels: 58.9 us -> 55.8 us
    all_to_all x1, waiting for transfers between devices: 0.01 us -> 20.6 us  [per_device(): lax.all_to_all(grad_rows, 'ctx', split_axis=0, concat_axis=0, tiled=True)]
    ppermute x6, waiting for transfers between devices: 29.7 us -> 10.8 us  [sum_x_first(): lax.ppermute(term, 'dp', move)]
    pallas_call x3, Pallas kernels: 24.6 us -> 21.5 us  [weight_terms(): pl.pallas_call(lambda *refs: term_kernel(per_step, *refs), grid_spec=pltp...]
    ppermute x30 -> x31, starting transfers between devices: 22.6 us -> 23.1 us  [pass_on(): return lax.ppermute(value, 'ctx', move)]
    ppermute x30 -> x31, waiting for transfers between devices: 52.6 us -> 52.6 us  [pass_on(): return lax.ppermute(value, 'ctx', move)]
  transfers between devices with their start and end apart: 45 -> 46, of which waited for: 15 -> 13; matrix products, arithmetic and copies ran while one was open for 15% -> 16% of each run, Pallas kernels for 23% -> 22%
where the time goes in v6:
time: 257 us; the launch traced here: 255 us
  waiting for transfers between devices  97.2 us (38%)
  starting transfers between devices  56.5 us (22%)
  Pallas kernels  55.8 us (22%)
  other arithmetic  19.5 us (8%)
  matrix products  16.8 us (7%)
  local copies, waits for them, and re-layouts  7.58 us (3%)
    ppermute x31, waiting for transfers between devices, pass_on(): return lax.ppermute(value, 'ctx', move)  52.6 us
    ppermute x31, starting transfers between devices, pass_on(): return lax.ppermute(value, 'ctx', move)  23.1 us
    pallas_call x3, Pallas kernels, weight_terms(): pl.pallas_call(lambda *refs: term_kernel(per_step, *refs), grid_spec=pltp...  21.5 us
    all_to_all x1, waiting for transfers between devices, per_device(): lax.all_to_all(grad_rows, 'ctx', split_axis=0, concat_axis=0, tiled=True)  20.6 us
    dot_general x3, matrix products, dot_nn(): lax.dot_general(a, b, (((1,), (0,)), ((), ())), preferred_element_type=jn...  16.8 us
    pallas_call x4, Pallas kernels, pick_rows(): pl.pallas_call(lambda *refs: pick_kernel(count, scaled, *refs), grid=(wid...  15.3 us
    pallas_call x1, Pallas kernels, attention_rows(): pl.pallas_call(attention_kernel, in_specs=[smem, smem, smem, vmem], out_s...  11.3 us
    ppermute x6, waiting for transfers between devices, sum_x_first(): lax.ppermute(term, 'dp', move)  10.8 us
  transfers between devices with their start and end apart: 46, of which 13 were waited for; matrix products, arithmetic and copies ran while one was open for 16% of the time, Pallas kernels for 22%

profile of v6, /device:TPU:2, one launch (start us, length us, event | category | flops | bytes accessed | tf_op | source)
XLA Modules:
  0.0 254.6 jit_solution(5807904643139859300)
XLA Ops:
  6.2 10.7 %collective-permute-done.3.refs_4_ = bf16[128,2048]{1,0:T(8,128)(2,1)S(1)} collective-permute-done((bf16[128,2048]{1,0:T(8,128)(2,1)}, bf16[128,2048]{1,0:T(8,128)(2,1)S(1)}, u32[]{:S(2)}, u32[]{:S(2)}) %collective-permute-start.3) | collective-permute-done | bytes 524320 | tf_op jit(solution)/shard_map/ppermute | solution.py:219
  20.9 6.2 %collective-permute-done.21.refs_4_ = bf16[128,2048]{1,0:T(8,128)(2,1)S(1)} collective-permute-done((bf16[128,2048]{1,0:T(8,128)(2,1)}, bf16[128,2048]{1,0:T(8,128)(2,1)S(1)}, u32[]{:S(2)}, u32[]{:S(2)}) %collective-permute-start.21) | collective-permute-done | bytes 524320 | tf_op jit(solution)/shard_map/ppermute | solution.py:219
  27.4 4.6 %collective-permute-done.16.refs_3_ = bf16[128,2048]{1,0:T(8,128)(2,1)} collective-permute-done((bf16[128,2048]{1,0:T(8,128)(2,1)}, bf16[128,2048]{1,0:T(8,128)(2,1)}, u32[]{:S(2)}, u32[]{:S(2)}) %collective-permute-start.16) | collective-permute-done | bytes 524320 | tf_op jit(solution)/shard_map/ppermute | solution.py:219
  32.7 7.7 %collective-permute-done.4.refs_6_ = bf16[128,2048]{1,0:T(8,128)(2,1)S(1)} collective-permute-done((bf16[128,2048]{1,0:T(8,128)(2,1)S(1)}, bf16[128,2048]{1,0:T(8,128)(2,1)S(1)}, u32[]{:S(2)}, u32[]{:S(2)}) %collective-permute-start.4) | collective-permute-done | bytes 524320 | tf_op jit(solution)/shard_map/ppermute | solution.py:219
  54.2 5.4 %pack_rows.1 = bf16[16,384,128]{2,1,0:T(8,128)(2,1)} custom-call(bf16[128,1024]{1,0:T(8,128)(2,1)} %bitcast.117, bf16[128,1024]{1,0:T(8,128)(2,1)} %bitcast.118, bf16[128,1024]{1,0:T(8,128)(2,1)} %bitcast.119, bf16[128,2048]{1,0:T(8,128)(2,1)} %bitcast.109, bf16[1024,2048]{1,0:T(8,128)(2,1)} %w_ref.1), custom_call_target="tpu_custom_call" | custom-call | flops 536870912 | bytes 7000000 | tf_op jit(solution)/shard_map/pack_rows/pallas_call | solution.py:47
  59.6 4.3 %all-to-all-done.2 = f32[16,1,128]{2,1,0:T(1,128)S(1)} async-done(((f32[16,1,128]{2,1,0:T(1,128)}), f32[16,1,128]{2,1,0:T(1,128)S(1)}, u32[]{:S(2)}, u32[]{:S(2)}) %all-to-all-start.2) | async-done | bytes 8224 | tf_op jit(solution)/shard_map/all_to_all | solution.py:373
  64.0 4.5 %all-to-all-start = ((bf16[16,384,128]{2,1,0:T(8,128)(2,1)}), bf16[16,384,128]{2,1,0:T(8,128)(2,1)}, u32[]{:S(2)}, u32[]{:S(2)}) async-start(bf16[16,384,128]{2,1,0:T(8,128)(2,1)} %pack_rows.1), calls=%async_computation | async-start | bytes 3145728 | tf_op jit(solution)/shard_map/all_to_all | solution.py:417
  76.6 23.3 %collective-permute-done.18.refs_3_ = bf16[128,2048]{1,0:T(8,128)(2,1)} collective-permute-done((bf16[128,2048]{1,0:T(8,128)(2,1)}, bf16[128,2048]{1,0:T(8,128)(2,1)}, u32[]{:S(2)}, u32[]{:S(2)}) %collective-permute-start.18) | collective-permute-done | bytes 524320 | tf_op jit(solution)/shard_map/ppermute | solution.py:219
  101.9 11.3 %attention_rows.1 = (bf16[16,192,128]{2,1,0:T(8,128)(2,1)}, bf16[16,128,128]{2,1,0:T(8,128)(2,1)}) custom-call(s32[64]{0:T(128)} %reshape.699.lists_ref, s32[16]{0:T(128)} %bitcast.123, s32[1]{0:T(128)} %bitcast.1.half_ref, bf16[16,384,128]{2,1,0:T(8,128)(2,1)} %all-to-all-done.rows_ref), custom_call_target="tpu_custom_call" | custom-call | bytes 3000000 | tf_op jit(solution)/shard_map/attention_rows/pallas_call | solution.py:146
  114.2 4.9 %pick_rows.4.refs_6_ = bf16[1024,2048]{1,0:T(8,128)(2,1)} custom-call(bf16[16,64,128]{2,1,0:T(8,128)(2,1)} %fusion.15.refs_0_, f32[16,64,1]{2,1,0:T(8,128)} %copy.41.refs_1_, bf16[128,2048]{1,0:T(8,128)(2,1)} %bitcast.110, bf16[128,2048]{1,0:T(8,128)(2,1)} %collective-permute-done.1.refs_3_, bf16[128,2048]{1,0:T(8,128)(2,1)} %copy-done.7, ...), custom_call_target="tpu_custom_call" | custom-call | flops 402653184 | bytes 9437184 | tf_op jit(solution)/shard_map/pick_rows/pallas_call | solution.py:259
  120.2 4.8 %pick_rows.6.refs_6_ = bf16[1024,2048]{1,0:T(8,128)(2,1)} custom-call(bf16[16,64,128]{2,1,0:T(8,128)(2,1)} %fusion.15.refs_0_, f32[16,64,1]{2,1,0:T(8,128)} %copy.41.refs_1_, bf16[128,2048]{1,0:T(8,128)(2,1)} %bitcast.116, bf16[128,2048]{1,0:T(8,128)(2,1)} %collective-permute-done.16.refs_3_, bf16[128,2048]{1,0:T(8,128)(2,1)} %copy-done.5, ...), custom_call_target="tpu_custom_call" | custom-call | flops 402653184 | bytes 9437184 | tf_op jit(solution)/shard_map/pick_rows/pallas_call | solution.py:259
  127.9 6.0 %fusion.2 = f32[1024,704]{0,1:T(8,128)S(1)} fusion(bf16[1024,2048]{1,0:T(8,128)(2,1)} %pick_rows.7.refs_2_.refs_3_.refs_4_.refs_5_, bf16[1,2048,704]{1,2,0:T(8,128)(2,1)} %param.24), kind=kOutput, calls=%fused_computation.3 | convolution fusion | flops 2952790016 | bytes 9961472 | tf_op jit(solution)/shard_map/dot_general | solution.py:25
  137.1 4.0 %add_multiply_fusion = (f32[1024,704]{0,1:T(8,128)}, bf16[1024,704]{0,1:T(8,128)(2,1)}, f32[1024,704]{0,1:T(8,128)}) fusion(f32[1024,704]{0,1:T(8,128)S(1)} %fusion.4, f32[1024,704]{0,1:T(8,128)S(1)} %fusion.2), kind=kLoop, calls=%fused_computation.9 | loop fusion | flops 7929856 | bytes 12976128 | tf_op jit(solution)/shard_map/mul | solution.py:405
  143.9 7.2 %weight_terms.3 = (bf16[2,704,256]{2,1,0:T(8,128)(2,1)}, bf16[2,704,256]{2,1,0:T(8,128)(2,1)}, bf16[2,704,256]{2,1,0:T(8,128)(2,1)}, bf16[2,704,256]{2,1,0:T(8,128)(2,1)}) custom-call(s32[8]{0:T(128)} %stack.97.refs_0_, bf16[704,1024]{1,0:T(8,128)(2,1)} %bitcast.104, bf16[1024,2048]{1,0:T(8,128)(2,1)} %pick_rows.5.refs_2_.refs_3_.refs_4_.refs_5_, ...), custom_call_target="tpu_custom_call" | custom-call | bytes 1000000 | tf_op jit(solution)/shard_map/weight_terms/pallas_call | solution.py:297
  153.2 7.6 %fusion.8 = (bf16[704,1024]{1,0:T(8,128)(2,1)}, bf16[704,1024]{1,0:T(8,128)(2,1)}) fusion(f32[1024,704]{0,1:T(8,128)} %get-tuple-element.38, f32[1024,704]{0,1:T(8,128)} %get-tuple-element.33, bf16[1024,2048]{1,0:T(8,128)(2,1)} %pick_rows.5.refs_2_.refs_3_.refs_4_.refs_5_, bf16[1,2048,704]{1,2,0:T(8,128)(2,1)S(1)} %copy-done), kind=kOutput, calls=%fused_computation.14 | convolution fusion | flops 2955673600 | bytes 15728640 | tf_op jit(solution)/shard_map/dot_general | solution.py:25
  160.8 7.2 %weight_terms.5 = (bf16[4,704,256]{2,1,0:T(8,128)(2,1)}, bf16[4,704,256]{2,1,0:T(8,128)(2,1)}) custom-call(s32[8]{0:T(128)} %stack.115.refs_0_, bf16[704,1024]{1,0:T(8,128)(2,1)} %get-tuple-element.51.refs_1_, bf16[1024,2048]{1,0:T(8,128)(2,1)} %pick_rows.7.refs_2_.refs_3_.refs_4_.refs_5_, bf16[1024,2048]{1,0:T(8,128)(2,1)} %pick_rows.7.refs_2_.refs_3_.refs_4_.refs_5_, ...), custom_call_target="tpu_custom_call" | custom-call | bytes 1000000 | tf_op jit(solution)/shard_map/weight_terms/pallas_call | solution.py:297
  168.0 3.6 %collective-permute-start.35 = (bf16[4,704,256]{2,1,0:T(8,128)(2,1)}, bf16[4,704,256]{2,1,0:T(8,128)(2,1)}, u32[]{:S(2)}, u32[]{:S(2)}) collective-permute-start(bf16[4,704,256]{2,1,0:T(8,128)(2,1)} %get-tuple-element.40), channel_id=1, source_target_pairs={{0,4},{1,5},{2,6},{3,7},{4,0},{5,1},{6,2},{7,3},{8,12},{9,13},{10,... | collective-permute-start | bytes 4325384 | tf_op jit(solution)/shard_map/ppermute | solution.py:343
  173.9 5.2 %all-to-all-start.1 = ((bf16[16,192,128]{2,1,0:T(8,128)(2,1)}), bf16[16,192,128]{2,1,0:T(8,128)(2,1)}, u32[]{:S(2)}, u32[]{:S(2)}) async-start(bf16[16,192,128]{2,1,0:T(8,128)(2,1)} %pad_maximum_fusion), calls=%async_computation.1 | async-start | bytes 1572864 | tf_op jit(solution)/shard_map/all_to_all | solution.py:433
  181.1 7.2 %weight_terms.4 = (bf16[2,704,256]{2,1,0:T(8,128)(2,1)}, bf16[2,704,256]{2,1,0:T(8,128)(2,1)}, bf16[2,704,256]{2,1,0:T(8,128)(2,1)}, bf16[2,704,256]{2,1,0:T(8,128)(2,1)}) custom-call(s32[8]{0:T(128)} %stack.97.refs_0_, bf16[704,1024]{1,0:T(8,128)(2,1)} %get-tuple-element.52.refs_1_, bf16[1024,2048]{1,0:T(8,128)(2,1)} %pick_rows.7.refs_2_.refs_3_.refs_4_.refs_5_, ...), custom_call_target="tpu_custom_call" | custom-call | bytes 1000000 | tf_op jit(solution)/shard_map/weight_terms/pallas_call | solution.py:297
  192.4 20.6 %all-to-all-done.1.rows_ref = bf16[16,192,128]{2,1,0:T(8,128)(2,1)} async-done(((bf16[16,192,128]{2,1,0:T(8,128)(2,1)}), bf16[16,192,128]{2,1,0:T(8,128)(2,1)}, u32[]{:S(2)}, u32[]{:S(2)}) %all-to-all-start.1) | async-done | bytes 786464 | tf_op jit(solution)/shard_map/all_to_all | solution.py:433
  218.1 5.0 %collective-permute-done.32 = bf16[2,704,256]{2,1,0:T(8,128)(2,1)} collective-permute-done((bf16[2,704,256]{2,1,0:T(8,128)(2,1)}, bf16[2,704,256]{2,1,0:T(8,128)(2,1)}, u32[]{:S(2)}, u32[]{:S(2)}) %collective-permute-start.32) | collective-permute-done | bytes 720928 | tf_op jit(solution)/shard_map/ppermute | solution.py:335
  223.1 5.8 %collective-permute-done.33 = bf16[2,704,256]{2,1,0:T(8,128)(2,1)} collective-permute-done((bf16[2,704,256]{2,1,0:T(8,128)(2,1)}, bf16[2,704,256]{2,1,0:T(8,128)(2,1)}, u32[]{:S(2)}, u32[]{:S(2)}) %collective-permute-start.33) | collective-permute-done | bytes 720928 | tf_op jit(solution)/shard_map/ppermute | solution.py:335
  232.5 4.6 %collective-permute-start.36 = (bf16[704,256]{1,0:T(8,128)(2,1)S(1)}, bf16[704,256]{1,0:T(8,128)(2,1)S(1)}, u32[]{:S(2)}, u32[]{:S(2)}) collective-permute-start(bf16[704,256]{1,0:T(8,128)(2,1)S(1)} %get-tuple-element.48), channel_id=1, source_target_pairs={{0,2},{1,3},{2,0},{3,1},{4,6},{5,7},{6,4},{7,5},{8,10},{9,11},{10,... | collective-permute-start | bytes 1081352 | tf_op jit(solution)/shard_map/ppermute | solution.py:345
  246.4 5.9 %collective-permute-done.37 = bf16[704,256]{1,0:T(8,128)(2,1)S(1)} collective-permute-done((bf16[704,256]{1,0:T(8,128)(2,1)S(1)}, bf16[704,256]{1,0:T(8,128)(2,1)S(1)}, u32[]{:S(2)}, u32[]{:S(2)}) %collective-permute-start.37) | collective-permute-done | bytes 360480 | tf_op jit(solution)/shard_map/ppermute | solution.py:345
  (146 shorter events, 75.8 us)
Async XLA Ops:
  40.4 30.5 %collective-permute-start.2 = (bf16[128,2048]{1,0:T(8,128)(2,1)}, bf16[128,2048]{1,0:T(8,128)(2,1)}, u32[]{:S(2)}, u32[]{:S(2)}) collective-permute-start(bf16[128,2048]{1,0:T(8,128)(2,1)} %collective-permute-done.1.refs_3_), channel_id=1, source_target_pairs={{0,96},{8,104},{16,112},{24,120},{32,0},{40,8},{48,16},{56,24},{64... | collective-permute-start | bytes 1572872 | tf_op jit(solution)/shard_map/ppermute | solution.py:219
  42.1 28.9 %collective-permute-start.23 = (bf16[128,2048]{1,0:T(8,128)(2,1)S(1)}, bf16[128,2048]{1,0:T(8,128)(2,1)}, u32[]{:S(2)}, u32[]{:S(2)}) collective-permute-start(bf16[128,2048]{1,0:T(8,128)(2,1)S(1)} %collective-permute-done.21.refs_4_), channel_id=1, source_target_pairs={{0,16},{8,24},{16,0},{24,8},{32,48},{40,56},{48,32},{56,40},{64,80... | collective-permute-start | bytes 1572872 | tf_op jit(solution)/shard_map/ppermute | solution.py:219
  43.9 27.6 %collective-permute-start.24 = (bf16[128,2048]{1,0:T(8,128)(2,1)S(1)}, bf16[128,2048]{1,0:T(8,128)(2,1)}, u32[]{:S(2)}, u32[]{:S(2)}) collective-permute-start(bf16[128,2048]{1,0:T(8,128)(2,1)S(1)} %collective-permute-done.21.refs_4_), channel_id=1, source_target_pairs={{0,32},{8,40},{16,48},{24,56},{32,64},{40,72},{48,80},{56,88},{64,... | collective-permute-start | bytes 1572872 | tf_op jit(solution)/shard_map/ppermute | solution.py:219
  44.2 27.4 %collective-permute-start.27 = (bf16[128,2048]{1,0:T(8,128)(2,1)S(1)}, bf16[128,2048]{1,0:T(8,128)(2,1)}, u32[]{:S(2)}, u32[]{:S(2)}) collective-permute-start(bf16[128,2048]{1,0:T(8,128)(2,1)S(1)} %collective-permute-done.21.refs_4_), channel_id=1, source_target_pairs={{0,8},{8,0},{16,24},{24,16},{32,40},{40,32},{48,56},{56,48},{64,72... | collective-permute-start | bytes 1572872 | tf_op jit(solution)/shard_map/ppermute | solution.py:219
  45.8 26.2 %collective-permute-start.17 = (bf16[128,2048]{1,0:T(8,128)(2,1)}, bf16[128,2048]{1,0:T(8,128)(2,1)}, u32[]{:S(2)}, u32[]{:S(2)}) collective-permute-start(bf16[128,2048]{1,0:T(8,128)(2,1)} %collective-permute-done.16.refs_3_), channel_id=1, source_target_pairs={{0,96},{8,104},{16,112},{24,120},{32,0},{40,8},{48,16},{56,24},{64... | collective-permute-start | bytes 1572872 | tf_op jit(solution)/shard_map/ppermute | solution.py:219
  64.0 37.9 %all-to-all-start = ((bf16[16,384,128]{2,1,0:T(8,128)(2,1)}), bf16[16,384,128]{2,1,0:T(8,128)(2,1)}, u32[]{:S(2)}, u32[]{:S(2)}) async-start(bf16[16,384,128]{2,1,0:T(8,128)(2,1)} %pack_rows.1), calls=%async_computation | async-start | bytes 3145728 | tf_op jit(solution)/shard_map/all_to_all | solution.py:417
  72.0 27.8 %collective-permute-start.18 = (bf16[128,2048]{1,0:T(8,128)(2,1)}, bf16[128,2048]{1,0:T(8,128)(2,1)}, u32[]{:S(2)}, u32[]{:S(2)}) collective-permute-start(bf16[128,2048]{1,0:T(8,128)(2,1)} %collective-permute-done.17.refs_2_), channel_id=1, source_target_pairs={{0,96},{8,104},{16,112},{24,120},{32,0},{40,8},{48,16},{56,24},{64... | collective-permute-start | bytes 1572872 | tf_op jit(solution)/shard_map/ppermute | solution.py:219
  75.8 43.3 %collective-permute-start.5 = (bf16[128,2048]{1,0:T(8,128)(2,1)}, bf16[128,2048]{1,0:T(8,128)(2,1)}, u32[]{:S(2)}, u32[]{:S(2)}) collective-permute-start(bf16[128,2048]{1,0:T(8,128)(2,1)} %copy-done.11), channel_id=1, source_target_pairs={{0,32},{8,40},{16,48},{24,56},{32,64},{40,72},{48,80},{56,88},{64,... | collective-permute-start | bytes 1572872 | tf_op jit(solution)/shard_map/ppermute | solution.py:219
  75.9 49.2 %collective-permute-start.19 = (bf16[128,2048]{1,0:T(8,128)(2,1)}, bf16[128,2048]{1,0:T(8,128)(2,1)}, u32[]{:S(2)}, u32[]{:S(2)}) collective-permute-start(bf16[128,2048]{1,0:T(8,128)(2,1)} %collective-permute-done.17.refs_2_), channel_id=1, source_target_pairs={{0,8},{8,0},{16,24},{24,16},{32,40},{40,32},{48,56},{56,48},{64,72... | collective-permute-start | bytes 1572872 | tf_op jit(solution)/shard_map/ppermute | solution.py:219
  76.0 43.7 %collective-permute-start.29 = (bf16[128,2048]{1,0:T(8,128)(2,1)}, bf16[128,2048]{1,0:T(8,128)(2,1)}, u32[]{:S(2)}, u32[]{:S(2)}) collective-permute-start(bf16[128,2048]{1,0:T(8,128)(2,1)} %collective-permute-done.23.refs_6_), channel_id=1, source_target_pairs={{0,8},{8,0},{16,24},{24,16},{32,40},{40,32},{48,56},{56,48},{64,72... | collective-permute-start | bytes 1572872 | tf_op jit(solution)/shard_map/ppermute | solution.py:219
  76.5 43.4 %collective-permute-start.30 = (bf16[128,2048]{1,0:T(8,128)(2,1)}, bf16[128,2048]{1,0:T(8,128)(2,1)}, u32[]{:S(2)}, u32[]{:S(2)}) collective-permute-start(bf16[128,2048]{1,0:T(8,128)(2,1)} %collective-permute-done.24.refs_7_), channel_id=1, source_target_pairs={{0,8},{8,0},{16,24},{24,16},{32,40},{40,32},{48,56},{56,48},{64,72... | collective-permute-start | bytes 1572872 | tf_op jit(solution)/shard_map/ppermute | solution.py:219
  99.8 25.2 %collective-permute-start.20 = (bf16[128,2048]{1,0:T(8,128)(2,1)}, bf16[128,2048]{1,0:T(8,128)(2,1)}, u32[]{:S(2)}, u32[]{:S(2)}) collective-permute-start(bf16[128,2048]{1,0:T(8,128)(2,1)} %collective-permute-done.18.refs_3_), channel_id=1, source_target_pairs={{0,8},{8,0},{16,24},{24,16},{32,40},{40,32},{48,56},{56,48},{64,72... | collective-permute-start | bytes 1572872 | tf_op jit(solution)/shard_map/ppermute | solution.py:219
  119.1 22.0 %collective-permute-start.6 = (bf16[128,2048]{1,0:T(8,128)(2,1)}, bf16[128,2048]{1,0:T(8,128)(2,1)}, u32[]{:S(2)}, u32[]{:S(2)}) collective-permute-start(bf16[128,2048]{1,0:T(8,128)(2,1)} %collective-permute-done.2.refs_2_), channel_id=1, source_target_pairs={{0,8},{8,0},{16,24},{24,16},{32,40},{40,32},{48,56},{56,48},{64,72... | collective-permute-start | bytes 1572872 | tf_op jit(solution)/shard_map/ppermute | solution.py:219
  119.7 51.9 %collective-permute-start = (bf16[16,128,128]{2,1,0:T(8,128)(2,1)}, bf16[16,128,128]{2,1,0:T(8,128)(2,1)}, u32[]{:S(2)}, u32[]{:S(2)}) collective-permute-start(bf16[16,128,128]{2,1,0:T(8,128)(2,1)} %get-tuple-element.26), channel_id=1, source_target_pairs={{0,8},{8,0},{16,24},{24,16},{32,40},{40,32},{48,56},{56,48},{64,72... | collective-permute-start | bytes 1572872 | tf_op jit(solution)/shard_map/ppermute | solution.py:219
  119.8 21.3 %collective-permute-start.7 = (bf16[128,2048]{1,0:T(8,128)(2,1)}, bf16[128,2048]{1,0:T(8,128)(2,1)}, u32[]{:S(2)}, u32[]{:S(2)}) collective-permute-start(bf16[128,2048]{1,0:T(8,128)(2,1)} %collective-permute-done.5.refs_3_), channel_id=1, source_target_pairs={{0,8},{8,0},{16,24},{24,16},{32,40},{40,32},{48,56},{56,48},{64,72... | collective-permute-start | bytes 1572872 | tf_op jit(solution)/shard_map/ppermute | solution.py:219
  151.1 38.7 %collective-permute-start.39 = (bf16[2,704,256]{2,1,0:T(8,128)(2,1)}, bf16[2,704,256]{2,1,0:T(8,128)(2,1)}, u32[]{:S(2)}, u32[]{:S(2)}) collective-permute-start(bf16[2,704,256]{2,1,0:T(8,128)(2,1)} %get-tuple-element.31), channel_id=1, source_target_pairs={{0,2},{1,3},{2,0},{3,1},{4,6},{5,7},{6,4},{7,5},{8,10},{9,11},{10,... | collective-permute-start | bytes 2162696 | tf_op jit(solution)/shard_map/ppermute | solution.py:335
  153.2 39.2 %collective-permute-start.40 = (bf16[2,704,256]{2,1,0:T(8,128)(2,1)}, bf16[2,704,256]{2,1,0:T(8,128)(2,1)}, u32[]{:S(2)}, u32[]{:S(2)}) collective-permute-start(bf16[2,704,256]{2,1,0:T(8,128)(2,1)} %get-tuple-element.42), channel_id=1, source_target_pairs={{0,1},{1,2},{2,3},{3,0},{4,5},{5,6},{6,7},{7,4},{8,9},{9,10},{10,1... | collective-permute-start | bytes 2162696 | tf_op jit(solution)/shard_map/ppermute | solution.py:335
  168.0 62.9 %collective-permute-start.35 = (bf16[4,704,256]{2,1,0:T(8,128)(2,1)}, bf16[4,704,256]{2,1,0:T(8,128)(2,1)}, u32[]{:S(2)}, u32[]{:S(2)}) collective-permute-start(bf16[4,704,256]{2,1,0:T(8,128)(2,1)} %get-tuple-element.40), channel_id=1, source_target_pairs={{0,4},{1,5},{2,6},{3,7},{4,0},{5,1},{6,2},{7,3},{8,12},{9,13},{10,... | collective-permute-start | bytes 4325384 | tf_op jit(solution)/shard_map/ppermute | solution.py:343
  173.9 39.1 %all-to-all-start.1 = ((bf16[16,192,128]{2,1,0:T(8,128)(2,1)}), bf16[16,192,128]{2,1,0:T(8,128)(2,1)}, u32[]{:S(2)}, u32[]{:S(2)}) async-start(bf16[16,192,128]{2,1,0:T(8,128)(2,1)} %pad_maximum_fusion), calls=%async_computation.1 | async-start | bytes 1572864 | tf_op jit(solution)/shard_map/all_to_all | solution.py:433
  179.0 36.2 %collective-permute-start.41 = (bf16[2,704,256]{2,1,0:T(8,128)(2,1)}, bf16[2,704,256]{2,1,0:T(8,128)(2,1)}, u32[]{:S(2)}, u32[]{:S(2)}) collective-permute-start(bf16[2,704,256]{2,1,0:T(8,128)(2,1)} %get-tuple-element.43), channel_id=1, source_target_pairs={{0,3},{1,0},{2,1},{3,2},{4,7},{5,4},{6,5},{7,6},{8,11},{9,8},{10,9... | collective-permute-start | bytes 2162696 | tf_op jit(solution)/shard_map/ppermute | solution.py:335
  188.3 29.8 %collective-permute-start.31 = (bf16[2,704,256]{2,1,0:T(8,128)(2,1)}, bf16[2,704,256]{2,1,0:T(8,128)(2,1)}, u32[]{:S(2)}, u32[]{:S(2)}) collective-permute-start(bf16[2,704,256]{2,1,0:T(8,128)(2,1)} %get-tuple-element.35), channel_id=1, source_target_pairs={{0,2},{1,3},{2,0},{3,1},{4,6},{5,7},{6,4},{7,5},{8,10},{9,11},{10,... | collective-permute-start | bytes 2162696 | tf_op jit(solution)/shard_map/ppermute | solution.py:335
  189.8 33.3 %collective-permute-start.32 = (bf16[2,704,256]{2,1,0:T(8,128)(2,1)}, bf16[2,704,256]{2,1,0:T(8,128)(2,1)}, u32[]{:S(2)}, u32[]{:S(2)}) collective-permute-start(bf16[2,704,256]{2,1,0:T(8,128)(2,1)} %get-tuple-element.36), channel_id=1, source_target_pairs={{0,1},{1,2},{2,3},{3,0},{4,5},{5,6},{6,7},{7,4},{8,9},{9,10},{10,1... | collective-permute-start | bytes 2162696 | tf_op jit(solution)/shard_map/ppermute | solution.py:335
  192.4 36.5 %collective-permute-start.33 = (bf16[2,704,256]{2,1,0:T(8,128)(2,1)}, bf16[2,704,256]{2,1,0:T(8,128)(2,1)}, u32[]{:S(2)}, u32[]{:S(2)}) collective-permute-start(bf16[2,704,256]{2,1,0:T(8,128)(2,1)} %get-tuple-element.37), channel_id=1, source_target_pairs={{0,3},{1,0},{2,1},{3,2},{4,7},{5,4},{6,5},{7,6},{8,11},{9,8},{10,9... | collective-permute-start | bytes 2162696 | tf_op jit(solution)/shard_map/ppermute | solution.py:335
  216.8 22.2 %collective-permute-start.42 = (bf16[704,256]{1,0:T(8,128)(2,1)S(1)}, bf16[704,256]{1,0:T(8,128)(2,1)S(1)}, u32[]{:S(2)}, u32[]{:S(2)}) collective-permute-start(bf16[704,256]{1,0:T(8,128)(2,1)S(1)} %fusion.20), channel_id=1, source_target_pairs={{0,4},{1,5},{2,6},{3,7},{4,0},{5,1},{6,2},{7,3},{8,12},{9,13},{10,... | collective-permute-start | bytes 1081352 | tf_op jit(solution)/shard_map/ppermute | solution.py:338
  (41 other events, 684.4 us)
